TPU v7x, 256 devices: a whole 4x4x8 slice. The times are simulated.
256 devices in a mesh: kv: 4 (over y), blk: 64 (over x, z, core).
Axes of the slice: x: 4, y: 4, z: 8, core: 2. Of those that a mesh axis runs over, the one named last changes fastest.
Arguments:
- hidden: bfloat16 [64, 2560], replicated
- positions: int32 [64], replicated, may hold values from 0 to 16383, as said below
- cache_len: int32 [64], replicated, may hold values from 0 to 16383, as said below
- page_table: int32 [64, 512], replicated, may hold values from -1 to 4095, as said below
- move_dest: int32 [4096, 1], replicated, may hold values from 0 to 63; in each aligned block of 64 rows (0 to 63, 64 to 127, ...) at most 2 rows name the same one
- paged_keys: bfloat16 [4096, 32, 1024], P('blk', None, 'kv')
- paged_values: bfloat16 [4096, 32, 1024], P('blk', None, 'kv'), may hold values from -6 to 6
- qkv_projection: bfloat16 [2560, 4096], P('blk', 'kv'), may hold values from -0.125 to 0.125
- query_norm_gain: float32 [256], replicated, may hold values from 0.5 to 2.5
- key_gain: float32 [256], replicated, may hold values from 0.5 to 2.5
- output_proj: bfloat16 [2048, 2560], P('kv'), may hold values from -0.125 to 0.125
- input_gain: float32 [2560], replicated, may hold values from 0.1 to 1.9
- attn_gain: float32 [2560], replicated, may hold values from 0.1 to 1.9
- ffw_gain: float32 [2560], replicated, may hold values from 0.1 to 1.9
- final_gain: float32 [2560], replicated, may hold values from 0.1 to 1.9
- gate_weight: bfloat16 [2560, 10240], P(None, 'blk'), may hold values from -0.125 to 0.125
- up_weight: bfloat16 [2560, 10240], P(None, 'blk'), may hold values from -0.125 to 0.125
- down_weight: bfloat16 [10240, 2560], P('blk')
Outputs:
- out_hidden: float32 [64, 2560], replicated
- relocated_keys: bfloat16 [8192, 32, 1024], P('blk', None, 'kv')
- relocated_values: bfloat16 [8192, 32, 1024], P('blk', None, 'kv')
Inputs may be any that keep to these rules, and one draw needn't show every extreme that they name: `cache_len`: one request holds exactly 16383 tokens. `positions`: at most the request's cache length. `page_table`: entry j of request r is a global slot for j <= cache_len[r] // 32 and -1 after; all slots named are distinct.
All inputs are finite; a program needn't handle non-finite values.
Results may differ from a plain program's by a relative error of at most 0.015.
The roundings to bfloat16 on the way count: a program that leaves them out, or rounds other values in their place, can miss the bound.
Values may be sent and summed in bfloat16 or wider, within the bound.
No kernel may reach another device: no remote copies, remote signals or barrier semaphores. Data moves between devices by JAX's collectives and lax.ppermute only.
A program may use at most 128 MiB of HBM per device.

v0:
```python
import math

import jax
import jax.numpy as jnp
from jax import lax
from jax.sharding import PartitionSpec as P

EPSILON = 1e-06
QK_SCALE = 0.0625
ROPE_LOG = math.log(1000000.0)
NEG_LARGE = -1e30


def merged(x, axis, combine):
    everything = jax.tree.map(lambda part: lax.all_gather(part, axis), x)
    first = jax.tree.map(lambda part: part[0], everything)

    def hop(k, so_far):
        return combine(so_far, jax.tree.map(lambda part: part[k], everything))

    return lax.fori_loop(1, lax.axis_size(axis), hop, first)


def root_mean_norm(values, scale_vec):
    return (
        values * lax.rsqrt(jnp.mean(values * values, axis=-1, keepdims=True) + EPSILON) * scale_vec
    )


def rotary_embed(values, positions):
    head_width = values.shape[-1]
    half_width = head_width // 2
    frequency = jnp.exp(-(2.0 * jnp.arange(half_width, dtype=jnp.float32) / head_width) * ROPE_LOG)
    angles = positions.astype(jnp.float32)[:, None] * frequency[None, :]
    cosine = jnp.cos(angles)[:, None, :]
    sine_part = jnp.sin(angles)[:, None, :]
    front = values[..., :half_width]
    back = values[..., half_width:]
    return jnp.concatenate(
        [front * cosine - back * sine_part, back * cosine + front * sine_part], axis=-1
    )


def combine_parts(earlier, later):
    top_score = jnp.maximum(earlier[0], later[0])
    weight_early = jnp.exp(earlier[0] - top_score)
    weight_late = jnp.exp(later[0] - top_score)
    return (
        top_score,
        earlier[1] * weight_early + later[1] * weight_late,
        earlier[2] * weight_early[..., None] + later[2] * weight_late[..., None],
    )


def local(
    hidden,
    positions,
    cache_len,
    page_table,
    move_dest,
    paged_keys,
    paged_values,
    qkv_projection,
    query_norm_gain,
    key_gain,
    output_proj,
    input_gain,
    attn_gain,
    ffw_gain,
    final_gain,
    gate_weight,
    up_weight,
    down_weight,
):
    blocks = lax.axis_size("blk")
    device = lax.axis_index("blk")
    request_count = hidden.shape[0]
    head_size = query_norm_gain.shape[0]
    slot_count = paged_keys.shape[0]
    page_size = paged_keys.shape[1]
    max_pages = page_table.shape[1]
    total_slots = slot_count * blocks
    capacity = max(2, (slot_count + blocks - 1) // blocks)
    recv_slots = blocks * capacity
    feature_rows = qkv_projection.shape[0]
    normed = root_mean_norm(hidden.astype(jnp.float32), input_gain).astype(jnp.bfloat16)
    normed_part = lax.dynamic_slice_in_dim(normed, device * feature_rows, feature_rows, 1)
    column_terms = jnp.dot(normed_part, qkv_projection, preferred_element_type=jnp.float32)
    projected_input = lax.psum(column_terms, "blk").astype(jnp.bfloat16)
    groups = projected_input.shape[1] // head_size - 2
    projected_input = projected_input.reshape(request_count, groups + 2, head_size).astype(
        jnp.float32
    )
    query_vectors = rotary_embed(
        root_mean_norm(projected_input[:, :groups], query_norm_gain), positions
    ).astype(jnp.bfloat16)
    fresh_keys = rotary_embed(
        root_mean_norm(projected_input[:, groups : groups + 1], key_gain), positions
    )[:, 0].astype(jnp.bfloat16)
    fresh_values = projected_input[:, groups + 1].astype(jnp.bfloat16)
    flat_table = page_table.reshape(-1)
    slot_owner = (
        jnp.full((total_slots,), -1, jnp.int32)
        .at[jnp.where(flat_table >= 0, flat_table, total_slots)]
        .set(jnp.arange(flat_table.shape[0], dtype=jnp.int32), mode="drop")
    )
    destination = move_dest[:, 0]
    dest_onehot = (destination[:, None] == jnp.arange(blocks, dtype=jnp.int32)[None, :]).astype(
        jnp.int32
    )
    dest_onehot = dest_onehot.reshape(blocks, slot_count, blocks)
    slot_rank = jnp.sum(
        (jnp.cumsum(dest_onehot, axis=1) - dest_onehot) * dest_onehot, axis=-1
    ).reshape(total_slots)
    fresh_index = (
        destination * recv_slots
        + jnp.arange(total_slots, dtype=jnp.int32) // slot_count * capacity
        + slot_rank
    )
    target_slot = page_table[jnp.arange(request_count, dtype=jnp.int32), cache_len // page_size]
    position_offsets = cache_len % page_size
    own_old = jnp.where(target_slot // slot_count == device, target_slot - device * slot_count, -1)
    count = paged_keys.shape[0]
    flat_pos = jnp.where(own_old >= 0, own_old * page_size + position_offsets, count * page_size)
    key_flat = (
        paged_keys.reshape(count * page_size, head_size).at[flat_pos].set(fresh_keys, mode="drop")
    )
    value_flat = (
        paged_values.reshape(count * page_size, head_size)
        .at[flat_pos]
        .set(fresh_values, mode="drop")
    )
    written_keys = key_flat.reshape(count, page_size, head_size)
    written_values = value_flat.reshape(count, page_size, head_size)
    local_dest = lax.dynamic_slice_in_dim(destination, device * slot_count, slot_count)
    local_rank = lax.dynamic_slice_in_dim(slot_rank, device * slot_count, slot_count)
    source_of = (
        jnp.full((recv_slots,), slot_count, jnp.int32)
        .at[local_dest * capacity + local_rank]
        .set(jnp.arange(slot_count, dtype=jnp.int32))
    )
    send_keys = jnp.take(written_keys, source_of, axis=0, mode="fill", fill_value=0)
    send_values = jnp.take(written_values, source_of, axis=0, mode="fill", fill_value=0)
    send_keys = send_keys.reshape(blocks, capacity, page_size, head_size)
    send_values = send_values.reshape(blocks, capacity, page_size, head_size)
    got_keys = lax.all_to_all(send_keys, "blk", split_axis=0, concat_axis=0, tiled=True)
    got_values = lax.all_to_all(send_values, "blk", split_axis=0, concat_axis=0, tiled=True)
    relocated_keys = got_keys.reshape(recv_slots, page_size, head_size)
    relocated_values = got_values.reshape(recv_slots, page_size, head_size)
    owner_new = jnp.full((blocks * recv_slots,), -1, jnp.int32).at[fresh_index].set(slot_owner)
    page_ids = lax.dynamic_slice_in_dim(owner_new, device * recv_slots, recv_slots)
    count = relocated_keys.shape[0]
    present = page_ids >= 0
    owners = jnp.where(present, page_ids // max_pages, 0)
    slot_queries = query_vectors[owners]
    scores = (
        jnp.einsum("ngd,npd->ngp", slot_queries, relocated_keys, preferred_element_type=jnp.float32)
        * QK_SCALE
    )
    key_pos = (page_ids % max_pages)[:, None] * page_size + jnp.arange(page_size, dtype=jnp.int32)[
        None, :
    ]
    key_valid = present[:, None] & (key_pos <= cache_len[owners][:, None])
    scores = jnp.where(key_valid[:, None, :], scores, NEG_LARGE)
    member = (owners[None, :] == jnp.arange(request_count, dtype=jnp.int32)[:, None]) & present[
        None, :
    ]
    slot_peak = jnp.max(scores, axis=-1)
    maxima = jnp.max(jnp.where(member[:, :, None], slot_peak[None], NEG_LARGE), axis=1)
    weights = jnp.where(key_valid[:, None, :], jnp.exp(scores - maxima[owners][:, :, None]), 0.0)
    slot_totals = jnp.sum(weights, axis=-1)
    slot_weighted = jnp.einsum(
        "ngp,npd->ngd",
        weights.astype(jnp.bfloat16),
        relocated_values,
        preferred_element_type=jnp.float32,
    )
    select = member.astype(jnp.float32)
    totals = jnp.dot(select, slot_totals, precision=lax.Precision.HIGHEST)
    weighted = jnp.dot(
        select, slot_weighted.reshape(count, groups * head_size), precision=lax.Precision.HIGHEST
    )
    maxima, totals, weighted = (maxima, totals, weighted.reshape(request_count, groups, head_size))
    maxima, totals, weighted = merged((maxima, totals, weighted), "blk", combine_parts)
    attended = (
        (weighted / totals[..., None])
        .astype(jnp.bfloat16)
        .reshape(request_count, groups * head_size)
    )
    head_terms = jnp.dot(attended, output_proj, preferred_element_type=jnp.float32)
    attn_out = lax.psum(head_terms, "kv")
    residual = hidden.astype(jnp.float32) + root_mean_norm(attn_out, attn_gain)
    ffw_in = root_mean_norm(residual, ffw_gain).astype(jnp.bfloat16)
    gate_proj = jnp.dot(ffw_in, gate_weight, preferred_element_type=jnp.float32)
    up_proj = jnp.dot(ffw_in, up_weight, preferred_element_type=jnp.float32)
    hidden_units = (jax.nn.gelu(gate_proj, approximate=True) * up_proj).astype(jnp.bfloat16)
    unit_terms = jnp.dot(hidden_units, down_weight, preferred_element_type=jnp.float32)
    ffw_out = lax.psum(unit_terms, "blk")
    out_hidden = residual + root_mean_norm(ffw_out, final_gain)
    return (out_hidden, relocated_keys, relocated_values)


def solution(mesh):
    return jax.shard_map(
        local,
        mesh=mesh,
        in_specs=(
            P(),
            P(),
            P(),
            P(),
            P(),
            P("blk", None, "kv"),
            P("blk", None, "kv"),
            P("blk", "kv"),
            P(),
            P(),
            P("kv", None),
            P(),
            P(),
            P(),
            P(),
            P(None, "blk"),
            P(None, "blk"),
            P("blk", None),
        ),
        out_specs=(P(), P("blk", None, "kv"), P("blk", None, "kv")),
        check_vma=False,
    )
```

profile of v0, /device:TPU:1, one launch (start us, length us, event | category | flops | bytes accessed | tf_op | source)
XLA Modules:
  0.0 980.5 jit_solution(3901637157528463093)
XLA Ops:
  7.2 2.4 copy.156
  9.7 1.0 copy.157
  12.0 2.3 fusion.7
  17.9 120.0 %scatter_custom_fusion = s32[4096]{0:T(1024)S(1)} fusion(s32[32768]{0:T(1024)S(1)} %bitcast.109, s32[32768]{0:T(1024)S(1)} %iota.51, s32[]{:T(128)} %constant.171.clone.1), kind=kCustom, calls=%fused_computation.116 | custom fusion | bytes 16388 | tf_op jit(solution)/shard_map/scatter | solution.py:105
  137.9 15.5 %scatter_custom_fusion.1 = s32[8192]{0:T(1024)S(1)} fusion(s32[4096]{0:T(1024)S(1)} %bitcast.111, s32[4096]{0:T(1024)S(1)} %scatter_custom_fusion, s32[]{:T(128)} %constant.171.clone.1), kind=kCustom, calls=%fused_computation.113 | custom fusion | bytes 32772 | tf_op jit(solution)/shard_map/scatter | solution.py:150
  154.4 1.1 fusion.51
  155.5 249.4 %all-reduce.7 = bf16[64,1024]{1,0:T(8,128)(2,1)S(1)} all-reduce(f32[64,1024]{1,0:T(8,128)S(1)} %fusion.51), channel_id=1, replica_groups=mesh['kv'=4,'blk'=64] {'blk'}, use_global_device_ids=true, to_apply=%region_5.6 | all-reduce | flops 65536 | bytes 393216 | tf_op jit(solution)/shard_map/psum | solution.py:89
  405.5 3.2 scatter_custom_fusion.2
  408.7 3.2 gather_fusion.4
  412.0 3.2 scatter_custom_fusion.4
  415.2 3.2 gather_fusion.5
  418.4 3.9 broadcast_select_fusion
  422.3 60.9 %all_to_all.10 = bf16[64,2,32,256]{3,2,1,0:T(8,128)(2,1)} all-to-all(bf16[64,2,32,256]{3,2,1,0:T(8,128)(2,1)S(1)} %bitcast.100), channel_id=1, replica_groups=mesh['kv'=4,'blk'=64] {'blk'}, dimensions={0} | all-to-all | bytes 4194304 | tf_op jit(solution)/shard_map/all_to_all | solution.py:146
  483.2 6.1 all-to-all-start.1
  489.6 1.2 gather_fusion
  492.5 2.3 fusion.81
  495.7 44.8 %all-to-all-done.1 = bf16[64,2,32,256]{3,2,1,0:T(8,128)(2,1)} async-done(((bf16[64,2,32,256]{3,2,1,0:T(8,128)(2,1)}), bf16[64,2,32,256]{3,2,1,0:T(8,128)(2,1)}, u32[]{:S(2)}, u32[]{:S(2)}) %all-to-all-start.1) | async-done | bytes 2097184 | tf_op jit(solution)/shard_map/all_to_all | solution.py:147
  540.5 2.0 fusion.20
  542.7 1.0 fusion.46
  543.8 41.5 %all-gather.3 = f32[64,64,2]{1,2,0:T(2,128)S(1)} all-gather(f32[1,64,2]{1,2,0:T(2,128)S(1)} %bitcast.112), channel_id=2, replica_groups=mesh['kv'=4,'blk'=64] {'blk'}, dimensions={0}, use_global_device_ids=true | all-gather | bytes 33280 | tf_op jit(solution)/shard_map/all_gather | solution.py:15
  585.8 43.0 %all-gather.4 = f32[64,64,2]{1,2,0:T(2,128)S(1)} all-gather(f32[1,64,2]{1,2,0:T(2,128)S(1)} %convolution_bitcast_fusion), channel_id=3, replica_groups=mesh['kv'=4,'blk'=64] {'blk'}, dimensions={0}, use_global_device_ids=true | all-gather | bytes 33280 | tf_op jit(solution)/shard_map/all_gather | solution.py:15
  628.8 0.9 slice.67
  629.8 99.3 %while.19 = (s32[]{:T(128)}, f32[64,2]{0,1:T(2,128)S(1)}, f32[64,2]{0,1:T(2,128)S(1)}, f32[64,2,256]{2,1,0:T(2,128)S(1)}, f32[64,64,2]{1,2,0:T(2,128)S(1)}, /*in...) while((s32[]{:T(128)}, f32[64,2]{0,1:T(2,128)S(1)}, ...), condition=%wide.region_15.17_spmd, body=%wide.region_14.16_spmd.sunk | while | flops 99077 | bytes 662671 | solution.py:21
  631.6 0.9 constant_dynamic-slice_fusion.3
  634.8 0.9 constant_dynamic-slice_fusion.3
  637.9 0.9 constant_dynamic-slice_fusion.3
  639.5 0.9 constant_dynamic-slice_fusion.3
  641.1 0.9 constant_dynamic-slice_fusion.3
  642.7 0.9 constant_dynamic-slice_fusion.3
  644.2 0.9 constant_dynamic-slice_fusion.3
  645.8 0.9 constant_dynamic-slice_fusion.3
  647.4 0.9 constant_dynamic-slice_fusion.3
  649.0 0.9 constant_dynamic-slice_fusion.3
  650.5 0.9 constant_dynamic-slice_fusion.3
  652.1 0.9 constant_dynamic-slice_fusion.3
  653.7 0.9 constant_dynamic-slice_fusion.3
  655.3 0.9 constant_dynamic-slice_fusion.3
  729.4 1.4 fusion.82
  730.9 43.6 %all-reduce.4.cloned.1.call-done = f32[64,2560]{1,0:T(8,128)} async-done(((f32[64,2560]{1,0:T(8,128)}), f32[64,2560]{1,0:T(8,128)}) %all-reduce.4.cloned.1.call-update) | async-done | bytes 655376 | tf_op jit(solution)/shard_map/psum | solution.py:191
  774.5 1.3 multiply_reduce_fusion.2
  775.8 1.5 multiply_reduce_fusion.1
  777.3 1.9 fusion.78
  779.2 3.2 fusion.10
  782.4 183.5 %all-reduce.6.cloned.1.call-done = f32[64,2560]{1,0:T(8,128)} async-done(((f32[64,2560]{1,0:T(8,128)}), f32[64,2560]{1,0:T(8,128)}) %all-reduce.6.cloned.1.call-update) | async-done | bytes 655376 | tf_op jit(solution)/shard_map/psum | solution.py:198
  965.9 1.4 multiply_reduce_fusion
  967.3 2.3 multiply_add_fusion
  969.6 1.3 copy.158
  970.9 3.1 copy.159
  (401 shorter events, 95.6 us)
Async XLA Ops:
  7.2 722.2 %copy-start = (bf16[512,2560]{1,0:T(8,128)(2,1)S(1)}, bf16[512,2560]{1,0:T(8,128)(2,1)}, u32[]{:S(2)}) copy-start(bf16[512,2560]{1,0:T(8,128)(2,1)} %param.32) | copy-start | bytes 7864324
  7.2 7.4 copy-start.3
  7.2 4.0 copy-start.9
  7.2 2.4 copy-start.6
  9.6 6.0 copy-start.14
  9.6 6.0 copy-start.1
  9.6 6.0 copy-start.5
  9.6 144.8 %copy-start.8 = (bf16[40,1024]{1,0:T(8,128)(2,1)S(1)}, bf16[40,1024]{1,0:T(8,128)(2,1)}, u32[]{:S(2)}) copy-start(bf16[40,1024]{1,0:T(8,128)(2,1)} %param.29) | copy-start | bytes 245764
  14.5 390.7 %copy-start.12 = (f32[256]{0:T(256)S(1)}, f32[256]{0:T(256)}, u32[]{:S(2)}) copy-start(f32[256]{0:T(256)} %param.31) | copy-start | bytes 3076
  483.2 7.9 copy-start.13
  483.2 57.3 %all-to-all-start.1 = ((bf16[64,2,32,256]{3,2,1,0:T(8,128)(2,1)}), bf16[64,2,32,256]{3,2,1,0:T(8,128)(2,1)}, u32[]{:S(2)}, u32[]{:S(2)}) async-start(bf16[64,2,32,256]{3,2,1,0:T(8,128)(2,1)} %bitcast.99), calls=%async_computation.1 | async-start | bytes 4194304 | tf_op jit(solution)/shard_map/all_to_all | solution.py:147
  489.4 139.4 %all-gather.7.cloned.1.call-start = ((), (), s32[]{:S(2)}) async-start(), calls=%async_computation.4 | async-start | bytes 8519680 | tf_op jit(solution)/shard_map/all_gather | solution.py:15
  543.7 230.8 %all-reduce.4.cloned.1.call-start = ((), (), s32[]{:S(2)}) async-start(), calls=%async_computation.2 | async-start | bytes 1310720 | tf_op jit(solution)/shard_map/psum | solution.py:191
  729.4 46.4 %copy-start.7 = (f32[2560]{0:T(1024)S(1)}, f32[2560]{0:T(1024)}, u32[]{:S(2)}) copy-start(f32[2560]{0:T(1024)} %param.34) | copy-start | bytes 30724
  729.4 47.9 %copy-start.10 = (f32[2560]{0:T(1024)S(1)}, f32[2560]{0:T(1024)}, u32[]{:S(2)}) copy-start(f32[2560]{0:T(1024)} %param.35) | copy-start | bytes 30724
  730.8 235.1 %all-reduce.6.cloned.1.call-start = ((), (), s32[]{:S(2)}) async-start(), calls=%async_computation.3 | async-start | bytes 1310720 | tf_op jit(solution)/shard_map/psum | solution.py:198
  774.5 4.7 copy-start.2
  779.2 188.1 %copy-start.11 = (f32[2560]{0:T(1024)S(1)}, f32[2560]{0:T(1024)}, u32[]{:S(2)}) copy-start(f32[2560]{0:T(1024)} %param.36) | copy-start | bytes 30724
  965.9 3.7 copy-start.4
Sparse Core Ops, SparseCore 0:
  543.8 79.9 all-gather.6
  731.0 43.4 all-reduce.3
  782.5 183.3 all-reduce.5
where the time goes:
time: 982 us; the launch traced here: 981 us
  blocking collectives  395 us (40%)
  waiting for transfers between devices  272 us (28%)
  local copies, waits for them, and re-layouts  231 us (24%)
  other arithmetic  48.2 us (5%)
  between operations  14.2 us (1%)
  matrix products  13 us (1%)
    psum x1, blocking collectives, local(): projected_input = lax.psum(column_terms, 'blk').astype(jnp.bfloat16)  249 us
    psum x1, waiting for transfers between devices, local(): ffw_out = lax.psum(unit_terms, 'blk')  184 us
    scatter x1, local copies, waits for them, and re-layouts, local(): slot_owner = jnp.full((total_slots,), -1, jnp.int32).at[jnp.where(flat_ta...  120 us
    all_gather x2, blocking collectives, merged(): everything = jax.tree.map(lambda part: lax.all_gather(part, axis), x)  84.4 us
    all_to_all x1, blocking collectives, local(): lax.all_to_all(send_keys, 'blk', split_axis=0, concat_axis=0, tiled=True)  60.9 us
    dynamic_slice x63, local copies, waits for them, and re-layouts, hop(): return combine(so_far, jax.tree.map(lambda part: part[k], everything))  57.6 us
    all_to_all x1, waiting for transfers between devices, local(): lax.all_to_all(send_values, 'blk', split_axis=0, concat_axis=0, tiled=True)  44.8 us
    psum x1, waiting for transfers between devices, local(): attn_out = lax.psum(head_terms, 'kv')  43.6 us
  transfers between devices with their start and end apart: 4, of which 3 were waited for; matrix products, arithmetic and copies ran while one was open for 1% of the time, Pallas kernels for 0%

commit v1 on v0

v1 whole, which is shorter than its diff:
```python
import functools
import math

import jax
import jax.numpy as jnp
from jax import lax
from jax.experimental import pallas as pl
from jax.experimental.pallas import tpu as pltpu
from jax.sharding import PartitionSpec as P

EPSILON = 1e-06
QK_SCALE = 0.0625
ROPE_LOG = math.log(1000000.0)
NEG_LARGE = -1e30
LANES = 128
BF16 = jnp.bfloat16
F32 = jnp.float32


def call(body, out_shape, n_in, flops, bytes_accessed):
    vmem = pl.BlockSpec(memory_space=pltpu.VMEM)
    return pl.pallas_call(
        body,
        out_shape=out_shape,
        in_specs=[vmem] * n_in,
        out_specs=jax.tree.map(lambda _: vmem, out_shape),
        cost_estimate=pl.CostEstimate(
            flops=flops, bytes_accessed=bytes_accessed, transcendentals=0
        ),
    )


def exchange(x):
    return lax.all_to_all(x, "blk", split_axis=0, concat_axis=0, tiled=True)


def inv_rms(square_sum, width):
    return lax.rsqrt(square_sum / width + EPSILON)


def tile_sum(x):
    return jnp.sum(jnp.sum(x, axis=1, keepdims=True), axis=0, keepdims=True)


def head_body(terms_ref, cos_ref, sin_ref, qgain_ref, kgain_ref, all_ref, own_ref):
    total = jnp.sum(terms_ref[...].astype(F32), axis=0)
    total = total.astype(BF16).astype(F32)
    cosine, sine = cos_ref[...], sin_ref[...]
    rows = []
    heads = total.shape[0] // 2 - 1
    for h in range(heads):
        gain = qgain_ref[...] if h < heads - 1 else kgain_ref[...]
        pair = total[2 * h : 2 * h + 2]
        pair = pair * inv_rms(tile_sum(pair * pair), 2 * LANES) * gain
        front, back = pair[0:1], pair[1:2]
        rows.append(front * cosine - back * sine)
        rows.append(back * cosine + front * sine)
    rows.append(total[2 * heads :])
    done = jnp.concatenate(rows, axis=0).astype(BF16)
    own_ref[...] = done
    all_ref[...] = jnp.broadcast_to(done[None], all_ref.shape)


def split3(x):
    first = x.astype(BF16).astype(F32)
    second = (x - first).astype(BF16).astype(F32)
    return first, second, x - first - second


def attend_body(groups, query_ref, keys_ref, values_ref, limit_ref, out_ref):
    slots, page, width = keys_ref.shape
    requests = query_ref.shape[0]
    tokens = slots * page
    keys = keys_ref[...].reshape(tokens, width)
    values = values_ref[...].reshape(tokens, width)
    spread = (
        lax.broadcasted_iota(jnp.int32, (slots, tokens), 1) // page
        == lax.broadcasted_iota(jnp.int32, (slots, tokens), 0)
    ).astype(F32).astype(BF16)
    limit = jnp.dot(limit_ref[...], spread, preferred_element_type=F32)
    offset = (lax.broadcasted_iota(jnp.int32, (requests, tokens), 1) % page).astype(F32)
    valid = offset < limit
    lane = lax.broadcasted_iota(jnp.int32, (requests, LANES), 1)
    extra = jnp.zeros((requests, LANES), F32)
    for g in range(groups):
        scores = lax.dot_general(
            query_ref[:, g * width : (g + 1) * width],
            keys,
            (((1,), (1,)), ((), ())),
            preferred_element_type=F32,
        )
        scores = jnp.where(valid, scores * QK_SCALE, NEG_LARGE)
        peak = jnp.max(scores, axis=1, keepdims=True)
        weights = jnp.where(valid, jnp.exp(scores - peak), 0.0)
        total = jnp.sum(weights, axis=1, keepdims=True)
        mixed = jnp.dot(weights.astype(BF16), values, preferred_element_type=F32)
        out_ref[:, g * width : (g + 1) * width] = mixed.astype(BF16)
        for i, part in enumerate(split3(peak) + split3(total)):
            extra = jnp.where(lane == 8 * g + i, part, extra)
    start = groups * width
    out_ref[:, start : start + LANES] = extra.astype(BF16)
    rest = out_ref.shape[1] - start - LANES
    out_ref[:, start + LANES :] = jnp.zeros((requests, rest), BF16)


def merge_body(groups, parts_ref, own_ref, proj_ref, out_ref):
    own = own_ref[...].astype(F32)
    rows = []
    stats = parts_ref[:, 2 * groups : 2 * groups + 1, :].astype(F32)
    key = own[2 * groups : 2 * groups + 2]
    value = own[2 * groups + 2 : 2 * groups + 4]
    for g in range(groups):
        def stat(i):
            at = 8 * g + i
            return stats[:, :, at : at + 1]

        peaks = stat(0) + stat(1) + stat(2)
        sums = stat(3) + stat(4) + stat(5)
        fresh = tile_sum(own[2 * g : 2 * g + 2] * key)[None] * QK_SCALE
        peak = jnp.maximum(jnp.max(peaks, axis=0, keepdims=True), fresh)
        scale = jnp.exp(peaks - peak)
        fresh = jnp.exp(fresh - peak)
        total = jnp.sum(scale * sums, axis=0) + fresh[0]
        mixed = jnp.sum(scale * parts_ref[:, 2 * g : 2 * g + 2, :].astype(F32), axis=0)
        mixed = mixed + fresh[0].astype(BF16).astype(F32) * value
        rows.append(mixed / total)
    heads = jnp.concatenate(rows, axis=0)
    flat = jnp.concatenate([heads[i : i + 1] for i in range(heads.shape[0])], axis=1)
    flat = jnp.broadcast_to(flat, (8, flat.shape[1])).astype(BF16)
    terms = jnp.dot(flat, proj_ref[...], preferred_element_type=F32)
    out_ref[...] = jnp.concatenate(
        [terms[0:1, i * LANES : (i + 1) * LANES] for i in range(out_ref.shape[0])], axis=0
    )


def residual_body(*refs):
    part_refs = refs[:-5]
    hidden_ref, attn_gain_ref, ffw_gain_ref, residual_ref, all_ref = refs[-5:]
    parts = [ref[...] for ref in part_refs]
    while len(parts) > 1:
        half = len(parts) // 2
        parts = [parts[i] + parts[i + half] for i in range(half)]
    attn = parts[0]
    width = attn.shape[0] * attn.shape[1]
    residual = (
        hidden_ref[...].astype(F32)
        + attn * inv_rms(tile_sum(attn * attn), width) * attn_gain_ref[...]
    )
    residual_ref[...] = residual
    ffw_in = residual * inv_rms(tile_sum(residual * residual), width) * ffw_gain_ref[...]
    all_ref[...] = jnp.broadcast_to(ffw_in.astype(BF16)[None], all_ref.shape)


def ffw_body(x_ref, gate_ref, up_ref, down_ref, out_ref):
    x = x_ref[...]
    gate = jnp.dot(x, gate_ref[...], preferred_element_type=F32)
    up = jnp.dot(x, up_ref[...], preferred_element_type=F32)
    units = (jax.nn.gelu(gate, approximate=True) * up).astype(BF16)
    out_ref[...] = jnp.dot(units, down_ref[...], preferred_element_type=F32).astype(BF16)


def output_body(terms_ref, residual_ref, gain_ref, all_ref):
    total = jnp.sum(terms_ref[...].astype(F32), axis=0)
    width = total.shape[0] * total.shape[1]
    row = residual_ref[...] + total * inv_rms(tile_sum(total * total), width) * gain_ref[...]
    all_ref[...] = jnp.broadcast_to(row.astype(BF16)[None], all_ref.shape)


def migrate(pages, source_of, blocks, capacity):
    send = jnp.take(pages, source_of, axis=0, mode="fill", fill_value=0)
    send = send.reshape((blocks, capacity) + pages.shape[1:])
    got = lax.all_to_all(send, "blk", split_axis=0, concat_axis=0, tiled=True)
    return got.reshape((blocks * capacity,) + pages.shape[1:])


def patch(pages, flat_pos, rows):
    count, page, width = pages.shape
    flat = pages.reshape(count * page, width).at[flat_pos].set(rows, mode="drop")
    return flat.reshape(count, page, width)


def local(
    hidden,
    positions,
    cache_len,
    page_table,
    move_dest,
    paged_keys,
    paged_values,
    qkv_projection,
    query_norm_gain,
    key_gain,
    output_proj,
    input_gain,
    attn_gain,
    ffw_gain,
    final_gain,
    gate_weight,
    up_weight,
    down_weight,
):
    blocks = lax.axis_size("blk")
    kv_size = lax.axis_size("kv")
    device = lax.axis_index("blk")
    requests, model = hidden.shape
    head = query_norm_gain.shape[0]
    slots, page, _ = paged_keys.shape
    pages_per_seq = page_table.shape[1]
    capacity = max(2, (slots + blocks - 1) // blocks)
    recv_slots = blocks * capacity
    feature_rows, columns = qkv_projection.shape
    groups = columns // head - 2
    col_tiles = columns // LANES
    model_tiles = model // LANES
    assert requests == blocks

    hidden32 = hidden.astype(F32)
    scale = lax.rsqrt(jnp.mean(hidden32 * hidden32, axis=-1, keepdims=True) + EPSILON)
    start = device * feature_rows
    normed = (
        lax.dynamic_slice_in_dim(hidden, start, feature_rows, 1).astype(F32)
        * scale
        * lax.dynamic_slice_in_dim(input_gain, start, feature_rows, 0)
    ).astype(BF16)
    terms = jnp.dot(normed, qkv_projection, preferred_element_type=F32).astype(BF16)
    terms = exchange(terms.reshape(requests, col_tiles, LANES))

    frequency = jnp.exp(-(2.0 * jnp.arange(head // 2, dtype=F32) / head) * ROPE_LOG)
    position = lax.dynamic_slice_in_dim(positions, device, 1).astype(F32)
    angles = position[:, None] * frequency[None, :]
    tile = (head // LANES, LANES)
    every, own = call(
        head_body,
        (
            jax.ShapeDtypeStruct((requests, col_tiles, LANES), BF16),
            jax.ShapeDtypeStruct((col_tiles, LANES), BF16),
        ),
        5,
        requests * columns,
        4 * requests * columns,
    )(
        terms,
        jnp.cos(angles),
        jnp.sin(angles),
        query_norm_gain.reshape(tile),
        key_gain.reshape(tile),
    )
    every = exchange(every).reshape(requests, columns)

    slot_ids = device * slots + jnp.arange(slots, dtype=jnp.int32)
    page_starts = jnp.arange(pages_per_seq, dtype=jnp.int32) * page
    held = jnp.clip(cache_len[:, None] - page_starts[None, :], 0, page)
    limit = jnp.sum(
        jnp.where(page_table[:, None, :] == slot_ids[None, :, None], held[:, None, :], 0), axis=-1
    ).astype(BF16)
    parts = call(
        functools.partial(attend_body, groups),
        jax.ShapeDtypeStruct((requests, columns), BF16),
        4,
        4 * groups * requests * slots * page * head,
        4 * slots * page * head,
    )(every, paged_keys, paged_values, limit)
    parts = exchange(parts.reshape(requests, col_tiles, LANES))
    attn_terms = call(
        functools.partial(merge_body, groups),
        jax.ShapeDtypeStruct((model_tiles, LANES), F32),
        3,
        16 * groups * head * model,
        2 * groups * head * model,
    )(parts, own, output_proj)

    everyone = [attn_terms] + [
        lax.ppermute(attn_terms, "kv", [(i, (i + d) % kv_size) for i in range(kv_size)])
        for d in range(1, kv_size)
    ]
    wide = (model_tiles, LANES)
    residual, ffw_in = call(
        residual_body,
        (
            jax.ShapeDtypeStruct(wide, F32),
            jax.ShapeDtypeStruct((requests,) + wide, BF16),
        ),
        kv_size + 3,
        model * 16,
        2 * requests * model,
    )(
        *everyone,
        lax.dynamic_slice_in_dim(hidden, device, 1, 0).reshape(wide),
        attn_gain.reshape(wide),
        ffw_gain.reshape(wide),
    )
    ffw_in = exchange(ffw_in).reshape(requests, model)
    units = gate_weight.shape[1]
    ffw_terms = call(
        ffw_body,
        jax.ShapeDtypeStruct((requests, model), BF16),
        4,
        6 * requests * units * model,
        6 * units * model,
    )(ffw_in, gate_weight, up_weight, down_weight)
    ffw_terms = exchange(ffw_terms.reshape((requests,) + wide))
    out_rows = call(
        output_body,
        jax.ShapeDtypeStruct((requests,) + wide, BF16),
        3,
        requests * model,
        4 * requests * model,
    )(ffw_terms, residual, final_gain.reshape(wide))
    out_hidden = exchange(out_rows).reshape(requests, model).astype(F32)

    dest = lax.dynamic_slice_in_dim(move_dest[:, 0], device * slots, slots)
    slot_iota = jnp.arange(slots, dtype=jnp.int32)
    earlier = (dest[None, :] == dest[:, None]) & (slot_iota[None, :] < slot_iota[:, None])
    outgoing = dest * capacity + jnp.sum(earlier.astype(jnp.int32), axis=1)
    match = outgoing[None, :] == jnp.arange(recv_slots, dtype=jnp.int32)[:, None]
    source_of = slots + jnp.sum(jnp.where(match, slot_iota[None, :] - slots, 0), axis=1)
    relocated_keys = migrate(paged_keys, source_of, blocks, capacity)
    relocated_values = migrate(paged_values, source_of, blocks, capacity)

    target = jnp.sum(
        jnp.where(
            jnp.arange(pages_per_seq, dtype=jnp.int32)[None, :] == cache_len[:, None] // page,
            page_table,
            0,
        ),
        axis=1,
    )
    all_dest = move_dest[:, 0]
    all_slots = jnp.arange(all_dest.shape[0], dtype=jnp.int32)
    target_dest = jnp.sum(
        jnp.where(all_slots[None, :] == target[:, None], all_dest[None, :], 0), axis=1
    )
    target_rank = jnp.sum(
        (
            (all_slots[None, :] // slots == target[:, None] // slots)
            & (all_slots[None, :] < target[:, None])
            & (all_dest[None, :] == target_dest[:, None])
        ).astype(jnp.int32),
        axis=1,
    )
    arrival = target // slots * capacity + target_rank
    flat_pos = jnp.where(
        target_dest == device, arrival * page + cache_len % page, recv_slots * page
    )
    fresh_keys = every[:, groups * head : (groups + 1) * head]
    fresh_values = every[:, (groups + 1) * head :]
    relocated_keys = patch(relocated_keys, flat_pos, fresh_keys)
    relocated_values = patch(relocated_values, flat_pos, fresh_values)
    return (out_hidden, relocated_keys, relocated_values)


def solution(mesh):
    return jax.shard_map(
        local,
        mesh=mesh,
        in_specs=(
            P(),
            P(),
            P(),
            P(),
            P(),
            P("blk", None, "kv"),
            P("blk", None, "kv"),
            P("blk", "kv"),
            P(),
            P(),
            P("kv", None),
            P(),
            P(),
            P(),
            P(),
            P(None, "blk"),
            P(None, "blk"),
            P("blk", None),
        ),
        out_specs=(P(), P("blk", None, "kv"), P("blk", None, "kv")),
        check_vma=False,
    )
```

time: 982 us -> 273 us (0.28)
  blocking collectives: 395 us -> 72.5 us
  local copies, waits for them, and re-layouts: 231 us -> 29 us
  waiting for transfers between devices: 272 us -> 94.4 us
  starting transfers between devices: 6.44 us -> 46.5 us
  other arithmetic: 48.2 us -> 10.6 us
  Pallas kernels: 0 us -> 16.6 us
  between operations: 14.2 us -> 1.51 us
  matrix products: 13 us -> 0.98 us
    psum x1 -> x0, blocking collectives: 249 us -> none  [local(): projected_input = lax.psum(column_terms, 'blk').astype(jnp.bfloat16)]
    psum x2 -> x0, waiting for transfers between devices: 227 us -> none  [the longest x1 184 us: local(): ffw_out = lax.psum(unit_terms, 'blk')]
    scatter x4 -> x2, local copies, waits for them, and re-layouts: 140 us -> 6.21 us  [patch(): pages.reshape(count * page, width).at[flat_pos].set(rows, mode='drop')]
    all_gather x2 -> x0, blocking collectives: 84.4 us -> none  [merged(): everything = jax.tree.map(lambda part: lax.all_gather(part, axis), x)]
    dynamic_slice x64 -> x4, local copies, waits for them, and re-layouts: 58.4 us -> 3.51 us  [the longest x1 1.41 us: local(): lax.dynamic_slice_in_dim(hidden, device, 1, 0).reshape(wide)]
    all_to_all x1 -> x6, waiting for transfers between devices: 44.8 us -> 92.4 us  [the longest x5 47.3 us: exchange(): return lax.all_to_all(x, 'blk', split_axis=0, concat_axis=0, tiled=True)]
    all_to_all x1 -> x6, starting transfers between devices: 6.14 us -> 42.7 us  [the longest x5 36.8 us: exchange(): return lax.all_to_all(x, 'blk', split_axis=0, concat_axis=0, tiled=True)]
    add x127 -> x1, other arithmetic: 30.6 us -> 0.01 us  [local(): slot_ids = device * slots + jnp.arange(slots, dtype=jnp.int32)]
  transfers between devices with their start and end apart: 4 -> 9, of which waited for: 3 -> 8; matrix products, arithmetic and copies ran while one was open for 1% -> 9% of each run, Pallas kernels for 0% -> 0%
where the time goes in v1:
time: 273 us; the launch traced here: 272 us
  waiting for transfers between devices  94.4 us (35%)
  blocking collectives  72.5 us (27%)
  starting transfers between devices  46.5 us (17%)
  local copies, waits for them, and re-layouts  29 us (11%)
  Pallas kernels  16.6 us (6%)
  other arithmetic  10.6 us (4%)
    all_to_all x1, blocking collectives, migrate(): got = lax.all_to_all(send, 'blk', split_axis=0, concat_axis=0, tiled=True)  57.3 us
    all_to_all x5, waiting for transfers between devices, exchange(): return lax.all_to_all(x, 'blk', split_axis=0, concat_axis=0, tiled=True)  47.3 us
    all_to_all x1, waiting for transfers between devices, migrate(): got = lax.all_to_all(send, 'blk', split_axis=0, concat_axis=0, tiled=True)  45.2 us
    all_to_all x5, starting transfers between devices, exchange(): return lax.all_to_all(x, 'blk', split_axis=0, concat_axis=0, tiled=True)  36.8 us
    all_to_all x1, blocking collectives, exchange(): return lax.all_to_all(x, 'blk', split_axis=0, concat_axis=0, tiled=True)  15.1 us
    unnamed x37, local copies, waits for them, and re-layouts  13.2 us
    scatter x2, local copies, waits for them, and re-layouts, patch(): pages.reshape(count * page, width).at[flat_pos].set(rows, mode='drop')  6.21 us
    all_to_all x1, starting transfers between devices, migrate(): got = lax.all_to_all(send, 'blk', split_axis=0, concat_axis=0, tiled=True)  5.95 us
  transfers between devices with their start and end apart: 9, of which 8 were waited for; matrix products, arithmetic and copies ran while one was open for 9% of the time, Pallas kernels for 0%

profile of v1, /device:TPU:1, one launch (start us, length us, event | category | flops | bytes accessed | tf_op | source)
XLA Modules:
  0.0 272.0 jit_solution(4289711879335747937)
XLA Ops:
  0.6 1.2 multiply_reduce_fusion
  1.8 0.8 dynamic_slice.18
  2.6 1.0 fusion
  3.6 0.7 copy.27
  4.3 13.0 %all-to-all-start = ((bf16[64,8,128]{2,1,0:T(8,128)(2,1)}), bf16[64,8,128]{2,1,0:T(8,128)(2,1)S(1)}, u32[]{:S(2)}, u32[]{:S(2)}) async-start(bf16[64,8,128]{2,1,0:T(8,128)(2,1)} %bitcast.16), calls=%async_computation | async-start | bytes 262144 | tf_op jit(solution)/shard_map/all_to_all | solution.py:34
  17.3 1.2 dynamic_slice.19
  19.2 0.6 fusion.17
  19.8 0.7 subtract_clamp_fusion
  20.6 7.1 %all-to-all-done.terms_ref = bf16[64,8,128]{2,1,0:T(8,128)(2,1)S(1)} async-done(((bf16[64,8,128]{2,1,0:T(8,128)(2,1)}), bf16[64,8,128]{2,1,0:T(8,128)(2,1)S(1)}, u32[]{:S(2)}, u32[]{:S(2)}) %all-to-all-start) | async-done | bytes 131104 | tf_op jit(solution)/shard_map/all_to_all | solution.py:34
  27.6 0.7 copy-done.8
  28.3 1.8 shard_map.193
  30.1 4.9 %all-to-all-start.1 = ((bf16[64,8,128]{2,1,0:T(8,128)(2,1)}), bf16[64,8,128]{2,1,0:T(8,128)(2,1)S(1)}, u32[]{:S(2)}, u32[]{:S(2)}) async-start(bf16[64,8,128]{2,1,0:T(8,128)(2,1)} %get-tuple-element.8), calls=%async_computation.1 | async-start | bytes 262144 | tf_op jit(solution)/shard_map/all_to_all | solution.py:34
  35.0 2.1 select_reduce_fusion
  37.7 7.6 %all-to-all-done.1 = bf16[64,8,128]{2,1,0:T(8,128)(2,1)S(1)} async-done(((bf16[64,8,128]{2,1,0:T(8,128)(2,1)}), bf16[64,8,128]{2,1,0:T(8,128)(2,1)S(1)}, u32[]{:S(2)}, u32[]{:S(2)}) %all-to-all-start.1) | async-done | bytes 131104 | tf_op jit(solution)/shard_map/all_to_all | solution.py:34
  45.3 0.7 copy.37
  46.0 4.1 %shard_map.194 = bf16[64,1024]{1,0:T(8,128)(2,1)} custom-call(bf16[64,1024]{1,0:T(8,128)(2,1)} %bitcast.48, bf16[64,32,256]{2,1,0:T(8,128)(2,1)} %keys_ref.1, bf16[64,32,256]{2,1,0:T(8,128)(2,1)} %values_ref.1, bf16[64,64]{1,0:T(8,128)(2,1)} %convert_element_type.35.limit_ref), custom_call_target="tpu_custom_call" | custom-call | flops 268435456 | bytes 2097152 | tf_op jit(solution)/shard_map/pallas_call | solution.py:256
  50.1 1.0 copy.29
  51.1 15.1 %all_to_all.40.parts_ref = bf16[64,8,128]{2,1,0:T(8,128)(2,1)} all-to-all(bf16[64,8,128]{2,1,0:T(8,128)(2,1)S(1)} %bitcast.54), channel_id=1, replica_groups=mesh['kv'=4,'blk'=64] {'blk'}, dimensions={0} | all-to-all | bytes 262144 | tf_op jit(solution)/shard_map/all_to_all | solution.py:34
  66.2 3.3 %shard_map.195.refs_0_ = f32[20,128]{1,0:T(8,128)} custom-call(bf16[64,8,128]{2,1,0:T(8,128)(2,1)} %all_to_all.40.parts_ref, bf16[8,128]{1,0:T(8,128)(2,1)} %get-tuple-element.9.own_ref, bf16[512,2560]{1,0:T(8,128)(2,1)} %proj_ref.1), custom_call_target="tpu_custom_call" | custom-call | flops 20971520 | bytes 2621440 | tf_op jit(solution)/shard_map/pallas_call | solution.py:264
  69.6 2.7 %collective-permute-start.2 = (f32[20,128]{1,0:T(8,128)}, f32[20,128]{1,0:T(8,128)S(1)}, u32[]{:S(2)}, u32[]{:S(2)}) collective-permute-start(f32[20,128]{1,0:T(8,128)} %shard_map.195.refs_0_), channel_id=1, source_target_pairs={{0,192},{64,0},{128,64},{192,128},{1,193},{65,1},{129,65},{193,129... | collective-permute-start | bytes 30728 | tf_op jit(solution)/shard_map/ppermute | solution.py:273
  72.6 0.7 collective-permute-start
  73.3 1.4 dynamic-slice_reduce_fusion
  74.7 1.8 collective-permute-done.1.refs_2_
  77.3 1.8 shard_map.196
  79.1 6.5 %all-to-all-start.3 = ((bf16[64,20,128]{2,1,0:T(8,128)(2,1)}), bf16[64,20,128]{2,1,0:T(8,128)(2,1)S(1)}, u32[]{:S(2)}, u32[]{:S(2)}) async-start(bf16[64,20,128]{2,1,0:T(8,128)(2,1)} %get-tuple-element.10), calls=%async_computation.3 | async-start | bytes 786432 | tf_op jit(solution)/shard_map/all_to_all | solution.py:34
  85.6 1.4 copy.25.gate_ref
  87.0 1.4 copy.26.up_ref
  88.4 11.8 %all-to-all-done.3 = bf16[64,20,128]{2,1,0:T(8,128)(2,1)S(1)} async-done(((bf16[64,20,128]{2,1,0:T(8,128)(2,1)}), bf16[64,20,128]{2,1,0:T(8,128)(2,1)S(1)}, u32[]{:S(2)}, u32[]{:S(2)}) %all-to-all-start.3) | async-done | bytes 327712 | tf_op jit(solution)/shard_map/all_to_all | solution.py:34
  100.2 0.8 copy.36
  101.0 3.6 %shard_map.197 = bf16[64,2560]{1,0:T(8,128)(2,1)} custom-call(bf16[64,2560]{1,0:T(8,128)(2,1)} %bitcast.47, bf16[2560,160]{1,0:T(8,128)(2,1)} %copy.25.gate_ref, bf16[2560,160]{1,0:T(8,128)(2,1)} %copy.26.up_ref, bf16[160,2560]{1,0:T(8,128)(2,1)} %down_ref.1), custom_call_target="tpu_custom_call" | custom-call | flops 157286400 | bytes 2457600 | tf_op jit(solution)/shard_map/pallas_call | solution.py:294
  104.6 2.0 reshape.253
  106.6 6.2 %all-to-all-start.4 = ((bf16[64,20,128]{2,1,0:T(8,128)(2,1)}), bf16[64,20,128]{2,1,0:T(8,128)(2,1)S(1)}, u32[]{:S(2)}, u32[]{:S(2)}) async-start(bf16[64,20,128]{2,1,0:T(8,128)(2,1)} %reshape.253), calls=%async_computation.4 | async-start | bytes 786432 | tf_op jit(solution)/shard_map/all_to_all | solution.py:34
  113.3 14.2 %all-to-all-done.4.terms_ref = bf16[64,20,128]{2,1,0:T(8,128)(2,1)S(1)} async-done(((bf16[64,20,128]{2,1,0:T(8,128)(2,1)}), bf16[64,20,128]{2,1,0:T(8,128)(2,1)S(1)}, u32[]{:S(2)}, u32[]{:S(2)}) %all-to-all-start.4) | async-done | bytes 327712 | tf_op jit(solution)/shard_map/all_to_all | solution.py:34
  127.4 0.7 copy-done.3
  128.2 2.0 shard_map.198
  130.2 6.2 %all-to-all-start.5 = ((bf16[64,20,128]{2,1,0:T(8,128)(2,1)}), bf16[64,20,128]{2,1,0:T(8,128)(2,1)S(1)}, u32[]{:S(2)}, u32[]{:S(2)}) async-start(bf16[64,20,128]{2,1,0:T(8,128)(2,1)} %shard_map.198), calls=%async_computation.5 | async-start | bytes 786432 | tf_op jit(solution)/shard_map/all_to_all | solution.py:34
  136.4 2.0 gather_fusion.1
  138.4 2.0 gather_fusion
  140.4 3.9 %broadcast_select_fusion = (bf16[128,32,256]{2,1,0:T(8,128)(2,1)}, bf16[128,32,256]{2,1,0:T(8,128)(2,1)S(1)}) fusion(bf16[128,32,256]{2,1,0:T(8,128)(2,1)} %gather_fusion.1, pred[128]{0:T(512)(128)(4,1)S(1)} %get-tuple-element.12, bf16[128,32,256]{2,1,0:T(8,128)(2,1)} %gather_fusion), kind=kLoop, calls=%fused_computation.5 | loop fusion | flops 2097152 | bytes 8388736 | tf_op jit(solution)/shard_map/jit(_take)/select_n | solution.py:170
  144.3 6.7 %all-to-all-done.5 = bf16[64,20,128]{2,1,0:T(8,128)(2,1)S(1)} async-done(((bf16[64,20,128]{2,1,0:T(8,128)(2,1)}), bf16[64,20,128]{2,1,0:T(8,128)(2,1)S(1)}, u32[]{:S(2)}, u32[]{:S(2)}) %all-to-all-start.5) | async-done | bytes 327712 | tf_op jit(solution)/shard_map/all_to_all | solution.py:34
  151.0 57.3 %all_to_all.41 = bf16[64,2,32,256]{3,2,1,0:T(8,128)(2,1)} all-to-all(bf16[64,2,32,256]{3,2,1,0:T(8,128)(2,1)S(1)} %bitcast.44), channel_id=1, replica_groups=mesh['kv'=4,'blk'=64] {'blk'}, dimensions={0} | all-to-all | bytes 4194304 | tf_op jit(solution)/shard_map/all_to_all | solution.py:172
  208.3 5.9 %all-to-all-start.7 = ((bf16[64,2,32,256]{3,2,1,0:T(8,128)(2,1)}), bf16[64,2,32,256]{3,2,1,0:T(8,128)(2,1)S(1)}, u32[]{:S(2)}, u32[]{:S(2)}) async-start(bf16[64,2,32,256]{3,2,1,0:T(8,128)(2,1)} %bitcast.43), calls=%async_computation.7 | async-start | bytes 4194304 | tf_op jit(solution)/shard_map/all_to_all | solution.py:172
  215.3 0.9 copy.35
  216.2 4.2 %scatter_custom_fusion = bf16[4096,256]{1,0:T(8,128)(2,1)} fusion(bf16[4096,256]{1,0:T(8,128)(2,1)} %bitcast.41, s32[64]{0:T(128)S(1)} %compare_select_fusion.1, bf16[64,1024]{1,0:T(8,128)(2,1)S(1)} %bitcast.49), kind=kCustom, calls=%fused_computation.24 | custom fusion | bytes 2129920 | tf_op jit(solution)/shard_map/scatter | solution.py:178
  220.4 45.2 %all-to-all-done.7 = bf16[64,2,32,256]{3,2,1,0:T(8,128)(2,1)S(1)} async-done(((bf16[64,2,32,256]{3,2,1,0:T(8,128)(2,1)}), bf16[64,2,32,256]{3,2,1,0:T(8,128)(2,1)S(1)}, u32[]{:S(2)}, u32[]{:S(2)}) %all-to-all-start.7) | async-done | bytes 2097184 | tf_op jit(solution)/shard_map/all_to_all | solution.py:172
  265.5 2.0 scatter_custom_fusion.1
  267.6 3.1 %copy.42 = bf16[128,32,256]{2,1,0:T(8,128)(2,1)} copy(bf16[128,32,256]{2,1,0:T(8,128)(2,1)} %bitcast.42) | data formatting | bytes 4194304
  270.7 1.3 copy.43
  (46 shorter events, 3.2 us)
Async XLA Ops:
  0.6 2.0 copy-start
  4.3 23.4 %all-to-all-start = ((bf16[64,8,128]{2,1,0:T(8,128)(2,1)}), bf16[64,8,128]{2,1,0:T(8,128)(2,1)S(1)}, u32[]{:S(2)}, u32[]{:S(2)}) async-start(bf16[64,8,128]{2,1,0:T(8,128)(2,1)} %bitcast.16), calls=%async_computation | async-start | bytes 262144 | tf_op jit(solution)/shard_map/all_to_all | solution.py:34
  27.6 0.7 copy-start.8
  30.1 15.2 %all-to-all-start.1 = ((bf16[64,8,128]{2,1,0:T(8,128)(2,1)}), bf16[64,8,128]{2,1,0:T(8,128)(2,1)S(1)}, u32[]{:S(2)}, u32[]{:S(2)}) async-start(bf16[64,8,128]{2,1,0:T(8,128)(2,1)} %get-tuple-element.8), calls=%async_computation.1 | async-start | bytes 262144 | tf_op jit(solution)/shard_map/all_to_all | solution.py:34
  50.1 35.5 %copy-start.5 = (bf16[2560,160]{0,1:T(8,128)(2,1)S(1)}, bf16[2560,160]{0,1:T(8,128)(2,1)}, u32[]{:S(2)}) copy-start(bf16[2560,160]{0,1:T(8,128)(2,1)} %param.35) | copy-start | bytes 2457604
  69.5 17.5 %copy-start.6 = (bf16[2560,160]{0,1:T(8,128)(2,1)S(1)}, bf16[2560,160]{0,1:T(8,128)(2,1)}, u32[]{:S(2)}) copy-start(bf16[2560,160]{0,1:T(8,128)(2,1)} %param.36) | copy-start | bytes 2457604
  69.6 5.2 %collective-permute-start.2 = (f32[20,128]{1,0:T(8,128)}, f32[20,128]{1,0:T(8,128)S(1)}, u32[]{:S(2)}, u32[]{:S(2)}) collective-permute-start(f32[20,128]{1,0:T(8,128)} %shard_map.195.refs_0_), channel_id=1, source_target_pairs={{0,192},{64,0},{128,64},{192,128},{1,193},{65,1},{129,65},{193,129... | collective-permute-start | bytes 30728 | tf_op jit(solution)/shard_map/ppermute | solution.py:273
  72.3 4.3 %collective-permute-start.1 = (f32[20,128]{1,0:T(8,128)}, f32[20,128]{1,0:T(8,128)S(1)}, u32[]{:S(2)}, u32[]{:S(2)}) collective-permute-start(f32[20,128]{1,0:T(8,128)} %shard_map.195.refs_0_), channel_id=1, source_target_pairs={{0,128},{64,192},{128,0},{192,64},{1,129},{65,193},{129,1},{193,65... | collective-permute-start | bytes 30728 | tf_op jit(solution)/shard_map/ppermute | solution.py:273
  72.6 4.1 %collective-permute-start = (f32[20,128]{1,0:T(8,128)}, f32[20,128]{1,0:T(8,128)S(1)}, u32[]{:S(2)}, u32[]{:S(2)}) collective-permute-start(f32[20,128]{1,0:T(8,128)} %shard_map.195.refs_0_), channel_id=1, source_target_pairs={{0,64},{64,128},{128,192},{192,0},{1,65},{65,129},{129,193},{193,1... | collective-permute-start | bytes 30728 | tf_op jit(solution)/shard_map/ppermute | solution.py:273
  74.7 1.9 copy-start.10
  76.6 0.6 copy-start.11
  76.7 0.6 copy-start.12
  79.1 21.1 %all-to-all-start.3 = ((bf16[64,20,128]{2,1,0:T(8,128)(2,1)}), bf16[64,20,128]{2,1,0:T(8,128)(2,1)S(1)}, u32[]{:S(2)}, u32[]{:S(2)}) async-start(bf16[64,20,128]{2,1,0:T(8,128)(2,1)} %get-tuple-element.10), calls=%async_computation.3 | async-start | bytes 786432 | tf_op jit(solution)/shard_map/all_to_all | solution.py:34
  101.0 11.8 %copy-start.9 = (s32[4096,1]{0,1:T(1,128)S(1)}, s32[4096,1]{0,1:T(1,128)}, u32[]{:S(2)}) copy-start(s32[4096,1]{0,1:T(1,128)} %param.24) | copy-start | bytes 49156
  104.6 31.8 %copy-start.1 = (bf16[64,32,256]{2,1,0:T(8,128)(2,1)S(1)}, bf16[64,32,256]{2,1,0:T(8,128)(2,1)}, u32[]{:S(2)}) copy-start(bf16[64,32,256]{2,1,0:T(8,128)(2,1)} %values_ref.1) | copy-start | bytes 3145732
  106.6 20.8 %all-to-all-start.4 = ((bf16[64,20,128]{2,1,0:T(8,128)(2,1)}), bf16[64,20,128]{2,1,0:T(8,128)(2,1)S(1)}, u32[]{:S(2)}, u32[]{:S(2)}) async-start(bf16[64,20,128]{2,1,0:T(8,128)(2,1)} %reshape.253), calls=%async_computation.4 | async-start | bytes 786432 | tf_op jit(solution)/shard_map/all_to_all | solution.py:34
  127.4 0.7 copy-start.3
  130.2 20.8 %all-to-all-start.5 = ((bf16[64,20,128]{2,1,0:T(8,128)(2,1)}), bf16[64,20,128]{2,1,0:T(8,128)(2,1)S(1)}, u32[]{:S(2)}, u32[]{:S(2)}) async-start(bf16[64,20,128]{2,1,0:T(8,128)(2,1)} %shard_map.198), calls=%async_computation.5 | async-start | bytes 786432 | tf_op jit(solution)/shard_map/all_to_all | solution.py:34
  136.4 2.0 copy-start.2
  208.3 6.0 %copy-start.13 = (s32[64]{0:T(128)S(1)}, s32[64]{0:T(128)}, u32[]{:S(2)}) copy-start(s32[64]{0:T(128)} %param.22) | copy-start | bytes 772
  208.3 6.0 %copy-start.7 = (s32[64,512]{1,0:T(8,128)S(1)}, s32[64,512]{1,0:T(8,128)}, u32[]{:S(2)}) copy-start(s32[64,512]{1,0:T(8,128)} %param.23) | copy-start | bytes 393220
  208.3 7.9 %copy-start.4 = (bf16[8,8,8,128]{3,1,2,0:T(8,128)(2,1)S(1)}, bf16[8,8,8,128]{3,1,2,0:T(8,128)(2,1)}, u32[]{:S(2)}) copy-start(bf16[8,8,8,128]{3,1,2,0:T(8,128)(2,1)} %copy.37) | copy-start | bytes 393220
  208.3 57.2 %all-to-all-start.7 = ((bf16[64,2,32,256]{3,2,1,0:T(8,128)(2,1)}), bf16[64,2,32,256]{3,2,1,0:T(8,128)(2,1)S(1)}, u32[]{:S(2)}, u32[]{:S(2)}) async-start(bf16[64,2,32,256]{3,2,1,0:T(8,128)(2,1)} %bitcast.43), calls=%async_computation.7 | async-start | bytes 4194304 | tf_op jit(solution)/shard_map/all_to_all | solution.py:172

commit v2 on v1

--- a/solution.py
+++ b/solution.py
@@ -28,6 +28,10 @@
             flops=flops, bytes_accessed=bytes_accessed, transcendentals=0
         ),
     )
+
+
+def tie(*values):
+    return lax.optimization_barrier(values)
 
 
 def exchange(x):
@@ -128,19 +132,16 @@
     flat = jnp.concatenate([heads[i : i + 1] for i in range(heads.shape[0])], axis=1)
     flat = jnp.broadcast_to(flat, (8, flat.shape[1])).astype(BF16)
     terms = jnp.dot(flat, proj_ref[...], preferred_element_type=F32)
-    out_ref[...] = jnp.concatenate(
-        [terms[0:1, i * LANES : (i + 1) * LANES] for i in range(out_ref.shape[0])], axis=0
-    )
-
-
-def residual_body(*refs):
-    part_refs = refs[:-5]
-    hidden_ref, attn_gain_ref, ffw_gain_ref, residual_ref, all_ref = refs[-5:]
-    parts = [ref[...] for ref in part_refs]
-    while len(parts) > 1:
-        half = len(parts) // 2
-        parts = [parts[i] + parts[i + half] for i in range(half)]
-    attn = parts[0]
+    tile = jnp.concatenate(
+        [terms[0:1, i * LANES : (i + 1) * LANES] for i in range(out_ref.shape[1])], axis=0
+    )
+    out_ref[...] = jnp.broadcast_to(tile[None], out_ref.shape)
+
+
+def residual_body(
+    parts_ref, hidden_ref, attn_gain_ref, ffw_gain_ref, residual_ref, all_ref
+):
+    attn = jnp.sum(parts_ref[...], axis=0)
     width = attn.shape[0] * attn.shape[1]
     residual = (
         hidden_ref[...].astype(F32)
@@ -166,17 +167,80 @@
     all_ref[...] = jnp.broadcast_to(row.astype(BF16)[None], all_ref.shape)
 
 
-def migrate(pages, source_of, blocks, capacity):
-    send = jnp.take(pages, source_of, axis=0, mode="fill", fill_value=0)
-    send = send.reshape((blocks, capacity) + pages.shape[1:])
-    got = lax.all_to_all(send, "blk", split_axis=0, concat_axis=0, tiled=True)
-    return got.reshape((blocks * capacity,) + pages.shape[1:])
-
-
-def patch(pages, flat_pos, rows):
-    count, page, width = pages.shape
-    flat = pages.reshape(count * page, width).at[flat_pos].set(rows, mode="drop")
-    return flat.reshape(count, page, width)
+def gather_body(source_ref, pages_ref, *outs):
+    per = outs[0].shape[0]
+    slots = pages_ref.shape[0]
+    for j, out in enumerate(outs):
+
+        @pl.loop(0, per, unroll=4)
+        def _(q, j=j, out=out):
+            source = source_ref[j * per + q]
+            page = pages_ref[jnp.minimum(source, slots - 1)]
+            out[q] = jnp.where(source < slots, page, jnp.zeros_like(page))
+
+
+def regroup_body(count, *refs):
+    ins, outs, sem = refs[:count], refs[count:-1], refs[-1]
+    cap = outs[0].shape[0] // count
+    for j, out in enumerate(outs):
+        for i, chunk in enumerate(ins):
+            pltpu.make_async_copy(
+                chunk.at[j * cap : (j + 1) * cap], out.at[i * cap : (i + 1) * cap], sem.at[j]
+            ).start()
+    for j, out in enumerate(outs):
+        pltpu.make_async_copy(out, out, sem.at[j]).wait()
+
+
+def assemble_body(counts, cap, place_ref, arrive_ref, fresh_ref, *refs):
+    arrays = len(counts)
+    chunks, outs = refs[: sum(counts)], refs[sum(counts) : -3]
+    pages, copy_sem, patch_sem = refs[-3:]
+    page = outs[0].shape[1]
+    requests, tiles = fresh_ref.shape[:2]
+    first = 0
+    for p, out in enumerate(outs):
+        inner = chunks[first].shape[0] // cap
+        for j in range(counts[p]):
+            for i in range(inner):
+                at = place_ref[p, j * inner + i] * cap
+                pltpu.make_async_copy(
+                    chunks[first + j].at[i * cap : (i + 1) * cap],
+                    out.at[pl.ds(at, cap)],
+                    copy_sem.at[p],
+                ).start()
+        first += counts[p]
+    for p, out in enumerate(outs):
+        pltpu.make_async_copy(out, out, copy_sem.at[p]).wait()
+
+    def each(act):
+        @pl.loop(0, requests)
+        def _(r):
+            where = arrive_ref[r]
+
+            @pl.when(where >= 0)
+            def _():
+                for p, out in enumerate(outs):
+                    act(p, r, out.at[where // page], where % page)
+
+    def fetch(p, r, slot):
+        return pltpu.make_async_copy(slot, pages.at[p, r], patch_sem.at[p, r])
+
+    def put(p, r, slot):
+        return pltpu.make_async_copy(pages.at[p, r], slot, patch_sem.at[p, r])
+
+    def change(p, r, slot, offset):
+        fetch(p, r, slot).wait()
+        at = tiles - 2 * arrays + 2 * p
+        new = fresh_ref[r].astype(F32)
+        row = jnp.concatenate([new[at : at + 1], new[at + 1 : at + 2]], axis=1)
+        old = pages[p, r].astype(F32)
+        here = lax.broadcasted_iota(jnp.int32, old.shape, 0) == offset
+        pages[p, r] = jnp.where(here, row, old).astype(BF16)
+        put(p, r, slot).start()
+
+    each(lambda p, r, slot, _: fetch(p, r, slot).start())
+    each(change)
+    each(lambda p, r, slot, _: put(p, r, slot).wait())
 
 
 def local(
@@ -225,6 +289,75 @@
     terms = jnp.dot(normed, qkv_projection, preferred_element_type=F32).astype(BF16)
     terms = exchange(terms.reshape(requests, col_tiles, LANES))
 
+    cores, depth = 2, 8
+    near = blocks // depth
+    across = device // (depth * cores)
+    along = device // cores % depth
+    core = device % cores
+
+    def index(x, z, c):
+        return (x % (near // cores) * depth + z % depth) * cores + c
+
+    def pairs(step_near, step_along):
+        out = []
+        for b in range(blocks):
+            x, z, c = b // (depth * cores), b // cores % depth, b % cores
+            out.append(
+                (b, index(x + step_near // cores, z + step_along, c ^ (step_near % cores)))
+            )
+        return out
+
+    to_near = [pairs(k, 0) for k in range(near)]
+    to_along = [pairs(0, k) for k in range(depth)]
+
+    vmem = pl.BlockSpec(memory_space=pltpu.VMEM)
+    smem = pl.BlockSpec(memory_space=pltpu.SMEM)
+    anywhere = pl.BlockSpec(memory_space=pl.ANY)
+
+    def buffers(count):
+        return [jax.ShapeDtypeStruct((recv_slots // count, page, head), BF16)] * count
+
+    def gather(pages, order, count):
+        match = order[None, :] == jnp.arange(recv_slots, dtype=jnp.int32)[:, None]
+        source_of = slots + jnp.sum(jnp.where(match, slot_iota[None, :] - slots, 0), axis=1)
+        return pl.pallas_call(
+            gather_body,
+            out_shape=buffers(count),
+            in_specs=[smem, vmem],
+            out_specs=[vmem] * count,
+            cost_estimate=pl.CostEstimate(
+                flops=0, bytes_accessed=6 * slots * page * head, transcendentals=0
+            ),
+        )(source_of, pages)
+
+    def regroup(chunks, count):
+        return pl.pallas_call(
+            functools.partial(regroup_body, len(chunks)),
+            out_shape=buffers(count),
+            in_specs=[anywhere] * len(chunks),
+            out_specs=[anywhere] * count,
+            scratch_shapes=[pltpu.SemaphoreType.DMA((count,))],
+            cost_estimate=pl.CostEstimate(
+                flops=0, bytes_accessed=8 * slots * page * head, transcendentals=0
+            ),
+        )(*chunks)
+
+    dest = lax.dynamic_slice_in_dim(move_dest[:, 0], device * slots, slots)
+    slot_iota = jnp.arange(slots, dtype=jnp.int32)
+    earlier = (dest[None, :] == dest[:, None]) & (slot_iota[None, :] < slot_iota[:, None])
+    rank = jnp.sum(earlier.astype(jnp.int32), axis=1)
+    step_near = (dest // (depth * cores) - across) % (near // cores) * cores + (dest % cores ^ core)
+    step_along = (dest // cores - along) % depth
+    keys_sends = gather(paged_keys, (step_near * depth + step_along) * capacity + rank, near)
+    values_sends = gather(paged_values, (step_along * near + step_near) * capacity + rank, depth)
+    terms, keys_sends, values_sends = tie(terms, keys_sends, values_sends)
+    keys_first = [keys_sends[0]] + [
+        lax.ppermute(keys_sends[k], "blk", to_near[k]) for k in range(1, near)
+    ]
+    values_first = [values_sends[0]] + [
+        lax.ppermute(values_sends[k], "blk", to_along[k]) for k in range(1, depth)
+    ]
+
     frequency = jnp.exp(-(2.0 * jnp.arange(head // 2, dtype=F32) / head) * ROPE_LOG)
     position = lax.dynamic_slice_in_dim(positions, device, 1).astype(F32)
     angles = position[:, None] * frequency[None, :]
@@ -245,7 +378,8 @@
         query_norm_gain.reshape(tile),
         key_gain.reshape(tile),
     )
-    every = exchange(every).reshape(requests, columns)
+    every = exchange(every)
+    every, keys_first[1:4], values_first[1:3] = tie(every, keys_first[1:4], values_first[1:3])
 
     slot_ids = device * slots + jnp.arange(slots, dtype=jnp.int32)
     page_starts = jnp.arange(pages_per_seq, dtype=jnp.int32) * page
@@ -259,20 +393,23 @@
         4,
         4 * groups * requests * slots * page * head,
         4 * slots * page * head,
-    )(every, paged_keys, paged_values, limit)
+    )(every.reshape(requests, columns), paged_keys, paged_values, limit)
     parts = exchange(parts.reshape(requests, col_tiles, LANES))
+    parts, keys_first[4:6], values_first[3:6] = tie(parts, keys_first[4:6], values_first[3:6])
     attn_terms = call(
         functools.partial(merge_body, groups),
-        jax.ShapeDtypeStruct((model_tiles, LANES), F32),
+        jax.ShapeDtypeStruct((kv_size, model_tiles, LANES), F32),
         3,
         16 * groups * head * model,
         2 * groups * head * model,
     )(parts, own, output_proj)
 
-    everyone = [attn_terms] + [
-        lax.ppermute(attn_terms, "kv", [(i, (i + d) % kv_size) for i in range(kv_size)])
-        for d in range(1, kv_size)
-    ]
+    attn_terms = lax.all_to_all(attn_terms, "kv", split_axis=0, concat_axis=0, tiled=True)
+    attn_terms, keys_first[6:], values_first[6:] = tie(
+        attn_terms, keys_first[6:], values_first[6:]
+    )
+    keys_sends = regroup(keys_first, depth)
+    values_sends = regroup(values_first, near)
     wide = (model_tiles, LANES)
     residual, ffw_in = call(
         residual_body,
@@ -280,16 +417,23 @@
             jax.ShapeDtypeStruct(wide, F32),
             jax.ShapeDtypeStruct((requests,) + wide, BF16),
         ),
-        kv_size + 3,
+        4,
         model * 16,
         2 * requests * model,
     )(
-        *everyone,
+        attn_terms,
         lax.dynamic_slice_in_dim(hidden, device, 1, 0).reshape(wide),
         attn_gain.reshape(wide),
         ffw_gain.reshape(wide),
     )
     ffw_in = exchange(ffw_in).reshape(requests, model)
+    ffw_in, keys_sends, values_sends = tie(ffw_in, keys_sends, values_sends)
+    keys_second = [keys_sends[0]] + [
+        lax.ppermute(keys_sends[k], "blk", to_along[k]) for k in range(1, depth)
+    ]
+    values_second = [values_sends[0]] + [
+        lax.ppermute(values_sends[k], "blk", to_near[k]) for k in range(1, near)
+    ]
     units = gate_weight.shape[1]
     ffw_terms = call(
         ffw_body,
@@ -299,6 +443,9 @@
         6 * units * model,
     )(ffw_in, gate_weight, up_weight, down_weight)
     ffw_terms = exchange(ffw_terms.reshape((requests,) + wide))
+    ffw_terms, keys_second[1:4], values_second[1:3] = tie(
+        ffw_terms, keys_second[1:4], values_second[1:3]
+    )
     out_rows = call(
         output_body,
         jax.ShapeDtypeStruct((requests,) + wide, BF16),
@@ -308,15 +455,6 @@
     )(ffw_terms, residual, final_gain.reshape(wide))
     out_hidden = exchange(out_rows).reshape(requests, model).astype(F32)
 
-    dest = lax.dynamic_slice_in_dim(move_dest[:, 0], device * slots, slots)
-    slot_iota = jnp.arange(slots, dtype=jnp.int32)
-    earlier = (dest[None, :] == dest[:, None]) & (slot_iota[None, :] < slot_iota[:, None])
-    outgoing = dest * capacity + jnp.sum(earlier.astype(jnp.int32), axis=1)
-    match = outgoing[None, :] == jnp.arange(recv_slots, dtype=jnp.int32)[:, None]
-    source_of = slots + jnp.sum(jnp.where(match, slot_iota[None, :] - slots, 0), axis=1)
-    relocated_keys = migrate(paged_keys, source_of, blocks, capacity)
-    relocated_values = migrate(paged_values, source_of, blocks, capacity)
-
     target = jnp.sum(
         jnp.where(
             jnp.arange(pages_per_seq, dtype=jnp.int32)[None, :] == cache_len[:, None] // page,
@@ -339,13 +477,36 @@
         axis=1,
     )
     arrival = target // slots * capacity + target_rank
-    flat_pos = jnp.where(
-        target_dest == device, arrival * page + cache_len % page, recv_slots * page
-    )
-    fresh_keys = every[:, groups * head : (groups + 1) * head]
-    fresh_values = every[:, (groups + 1) * head :]
-    relocated_keys = patch(relocated_keys, flat_pos, fresh_keys)
-    relocated_values = patch(relocated_values, flat_pos, fresh_values)
+    arrive = jnp.where(target_dest == device, arrival * page + cache_len % page, -1)
+    back_along = jnp.arange(depth, dtype=jnp.int32)
+    back_near = jnp.arange(near, dtype=jnp.int32)
+
+    def source_index(along_step, near_step):
+        return index(
+            across - near_step // cores, along - along_step, core ^ (near_step % cores)
+        ).reshape(-1)
+
+    place = jnp.stack(
+        [
+            source_index(back_along[:, None], back_near[None, :]),
+            source_index(back_along[None, :], back_near[:, None]),
+        ]
+    )
+    moved = jax.ShapeDtypeStruct((recv_slots, page, head), BF16)
+    relocated_keys, relocated_values = pl.pallas_call(
+        functools.partial(assemble_body, (depth, near), capacity),
+        out_shape=[moved] * 2,
+        in_specs=[smem, smem, vmem] + [anywhere] * (depth + near),
+        out_specs=[anywhere] * 2,
+        scratch_shapes=[
+            pltpu.VMEM((2, requests, page, head), BF16),
+            pltpu.SemaphoreType.DMA((2,)),
+            pltpu.SemaphoreType.DMA((2, requests)),
+        ],
+        cost_estimate=pl.CostEstimate(
+            flops=0, bytes_accessed=16 * slots * page * head, transcendentals=0
+        ),
+    )(place, arrive, every, *keys_second, *values_second)
     return (out_hidden, relocated_keys, relocated_values)
 
 

time: 273 us -> 522 us (1.91)
  Pallas kernels: 16.6 us -> 284 us
  starting transfers between devices: 46.5 us -> 131 us
  blocking collectives: 72.5 us -> 0 us
  waiting for transfers between devices: 94.4 us -> 79.2 us
  local copies, waits for them, and re-layouts: 29 us -> 16 us
    pallas_call x1 -> x6, Pallas kernels: 3.33 us -> 271 us  [the longest x1 132 us: local(): pl.pallas_call(functools.partial(assemble_body, (depth, near), capacity),...]
    ppermute x3 -> x28, waiting for transfers between devices: 1.94 us -> 75.6 us  [the longest x7 69.4 us: local(): lax.ppermute(keys_sends[k], 'blk', to_along[k])]
    all_to_all x2 -> x0, blocking collectives: 72.5 us -> none  [the longest x1 57.3 us: migrate(): got = lax.all_to_all(send, 'blk', split_axis=0, concat_axis=0, tiled=True)]
    ppermute x3 -> x28, starting transfers between devices: 3.78 us -> 68.1 us  [the longest x7 23.6 us: local(): lax.ppermute(values_sends[k], 'blk', to_along[k])]
    all_to_all x5 -> x6, waiting for transfers between devices: 47.3 us -> 1.51 us  [exchange(): return lax.all_to_all(x, 'blk', split_axis=0, concat_axis=0, tiled=True)]
    all_to_all x1, waiting for transfers between devices: 45.2 us -> 2.09 us  [local(): lax.all_to_all(attn_terms, 'kv', split_axis=0, concat_axis=0, tiled=True)]
    all_to_all x5 -> x6, starting transfers between devices: 36.8 us -> 58.3 us  [exchange(): return lax.all_to_all(x, 'blk', split_axis=0, concat_axis=0, tiled=True)]
    scatter x2 -> x0, local copies, waits for them, and re-layouts: 6.21 us -> none  [patch(): pages.reshape(count * page, width).at[flat_pos].set(rows, mode='drop')]
  transfers between devices with their start and end apart: 9 -> 35, of which waited for: 8 -> 11; matrix products, arithmetic and copies ran while one was open for 9% -> 3% of each run, Pallas kernels for 0% -> 53%
where the time goes in v2:
time: 522 us; the launch traced here: 521 us
  Pallas kernels  284 us (54%)
  starting transfers between devices  131 us (25%)
  waiting for transfers between devices  79.2 us (15%)
  local copies, waits for them, and re-layouts  16 us (3%)
  other arithmetic  8.06 us (2%)
    pallas_call x1, Pallas kernels, local(): pl.pallas_call(functools.partial(assemble_body, (depth, near), capacity),...  132 us
    pallas_call x2, Pallas kernels, regroup(): pl.pallas_call(functools.partial(regroup_body, len(chunks)), out_shape=bu...  129 us
    ppermute x7, waiting for transfers between devices, local(): lax.ppermute(keys_sends[k], 'blk', to_along[k])  69.4 us
    all_to_all x6, starting transfers between devices, exchange(): return lax.all_to_all(x, 'blk', split_axis=0, concat_axis=0, tiled=True)  58.3 us
    ppermute x7, starting transfers between devices, local(): lax.ppermute(values_sends[k], 'blk', to_along[k])  23.6 us
    ppermute x7, starting transfers between devices, local(): lax.ppermute(values_sends[k], 'blk', to_near[k])  18.3 us
    ppermute x7, starting transfers between devices, local(): lax.ppermute(keys_sends[k], 'blk', to_along[k])  15.2 us
    ppermute x7, starting transfers between devices, local(): lax.ppermute(keys_sends[k], 'blk', to_near[k])  11 us
  transfers between devices with their start and end apart: 35, of which 11 were waited for; matrix products, arithmetic and copies ran while one was open for 3% of the time, Pallas kernels for 53%

profile of v2, /device:TPU:1, one launch (start us, length us, event | category | flops | bytes accessed | tf_op | source)
XLA Modules:
  0.0 520.8 jit_solution(5012528894517019863)
XLA Ops:
  4.3 13.0 %all-to-all-start = ((bf16[64,8,128]{2,1,0:T(8,128)(2,1)}), bf16[64,8,128]{2,1,0:T(8,128)(2,1)S(1)}, u32[]{:S(2)}, u32[]{:S(2)}) async-start(bf16[64,8,128]{2,1,0:T(8,128)(2,1)} %bitcast.10), calls=%async_computation | async-start | bytes 262144 | tf_op jit(solution)/shard_map/all_to_all | solution.py:38
  22.1 3.0 shard_map.193
  25.1 3.1 shard_map.194
  30.7 1.6 collective-permute-start.2
  33.6 2.2 collective-permute-start.4
  35.8 1.8 shard_map.195
  37.5 6.3 %all-to-all-start.1 = ((bf16[64,8,128]{2,1,0:T(8,128)(2,1)}), bf16[64,8,128]{2,1,0:T(8,128)(2,1)S(1)}, u32[]{:S(2)}, u32[]{:S(2)}) async-start(bf16[64,8,128]{2,1,0:T(8,128)(2,1)} %get-tuple-element.115), calls=%async_computation.1 | async-start | bytes 262144 | tf_op jit(solution)/shard_map/all_to_all | solution.py:38
  43.9 3.1 collective-permute-start.5
  47.6 3.1 collective-permute-start.7
  50.6 2.4 collective-permute-start.8
  54.9 4.2 collective-permute-start.9
  59.8 4.1 shard_map.196
  63.9 1.7 copy.29
  65.6 9.5 %all-to-all-start.2 = ((bf16[64,8,128]{2,1,0:T(8,128)(2,1)}), bf16[64,8,128]{2,1,0:T(8,128)(2,1)S(1)}, u32[]{:S(2)}, u32[]{:S(2)}) async-start(bf16[64,8,128]{2,1,0:T(8,128)(2,1)} %bitcast.14), calls=%async_computation.2 | async-start | bytes 262144 | tf_op jit(solution)/shard_map/all_to_all | solution.py:38
  75.1 2.9 collective-permute-start.10
  79.0 10.5 %collective-permute-start.12 = (bf16[16,32,256]{2,1,0:T(8,128)(2,1)}, bf16[16,32,256]{2,1,0:T(8,128)(2,1)}, u32[]{:S(2)}, u32[]{:S(2)}) collective-permute-start(bf16[16,32,256]{2,1,0:T(8,128)(2,1)} %get-tuple-element.131), channel_id=1, source_target_pairs={{0,12},{1,13},{2,14},{3,15},{4,0},{5,1},{6,2},{7,3},{8,4},{9,5},{1... | collective-permute-start | bytes 786440 | tf_op jit(solution)/shard_map/ppermute | solution.py:358
  89.5 1.5 all-to-all-done.2.parts_ref
  91.7 3.4 shard_map.197
  95.2 4.2 all-to-all-start.3
  101.7 2.1 all-to-all-done.3.parts_ref
  104.4 1.8 shard_map.198
  106.2 10.4 %all-to-all-start.4 = ((bf16[64,20,128]{2,1,0:T(8,128)(2,1)}), bf16[64,20,128]{2,1,0:T(8,128)(2,1)S(1)}, u32[]{:S(2)}, u32[]{:S(2)}) async-start(bf16[64,20,128]{2,1,0:T(8,128)(2,1)} %get-tuple-element.134), calls=%async_computation.4 | async-start | bytes 786432 | tf_op jit(solution)/shard_map/all_to_all | solution.py:38
  119.6 64.7 %shard_map.200 = (bf16[16,32,256]{2,1,0:T(8,128)(2,1)}, bf16[16,32,256]{2,1,0:T(8,128)(2,1)}, bf16[16,32,256]{2,1,0:T(8,128)(2,1)}, bf16[16,32,256]{2,1,0:T(8,12...) custom-call(bf16[16,32,256]{2,1,0:T(8,128)(2,1)} %get-tuple-element., ...), custom_call_target="tpu_custom_call" | custom-call | bytes 4194304 | tf_op jit(solution)/shard_map/pallas_call | solution.py:334
  184.3 64.7 %shard_map.199 = (bf16[16,32,256]{2,1,0:T(8,128)(2,1)}, bf16[16,32,256]{2,1,0:T(8,128)(2,1)}, bf16[16,32,256]{2,1,0:T(8,128)(2,1)}, bf16[16,32,256]{2,1,0:T(8,12...) custom-call(bf16[16,32,256]{2,1,0:T(8,128)(2,1)} %get-tuple-element., ...), custom_call_target="tpu_custom_call" | custom-call | bytes 4194304 | tf_op jit(solution)/shard_map/pallas_call | solution.py:334
  249.9 3.7 shard_map.201
  253.6 1.9 reshape.614
  255.5 10.3 %all-to-all-start.5 = ((bf16[64,20,128]{2,1,0:T(8,128)(2,1)}), bf16[64,20,128]{2,1,0:T(8,128)(2,1)S(1)}, u32[]{:S(2)}, u32[]{:S(2)}) async-start(bf16[64,20,128]{2,1,0:T(8,128)(2,1)} %reshape.614), calls=%async_computation.5 | async-start | bytes 786432 | tf_op jit(solution)/shard_map/all_to_all | solution.py:38
  265.9 1.5 collective-permute-start.14
  267.3 2.1 collective-permute-start.15
  269.4 2.4 collective-permute-start.16
  274.4 8.7 %collective-permute-done.14.refs_1_ = bf16[16,32,256]{2,1,0:T(8,128)(2,1)S(1)} collective-permute-done((bf16[16,32,256]{2,1,0:T(8,128)(2,1)S(1)}, bf16[16,32,256]{2,1,0:T(8,128)(2,1)S(1)}, u32[]{:S(2)}, u32[]{:S(2)}) %collective-permute-start.14) | collective-permute-done | bytes 262176 | tf_op jit(solution)/shard_map/ppermute | solution.py:432
  283.1 9.5 %collective-permute-done.15.refs_2_ = bf16[16,32,256]{2,1,0:T(8,128)(2,1)S(1)} collective-permute-done((bf16[16,32,256]{2,1,0:T(8,128)(2,1)S(1)}, bf16[16,32,256]{2,1,0:T(8,128)(2,1)S(1)}, u32[]{:S(2)}, u32[]{:S(2)}) %collective-permute-start.15) | collective-permute-done | bytes 262176 | tf_op jit(solution)/shard_map/ppermute | solution.py:432
  292.6 18.4 %collective-permute-done.16.refs_3_ = bf16[16,32,256]{2,1,0:T(8,128)(2,1)S(1)} collective-permute-done((bf16[16,32,256]{2,1,0:T(8,128)(2,1)S(1)}, bf16[16,32,256]{2,1,0:T(8,128)(2,1)S(1)}, u32[]{:S(2)}, u32[]{:S(2)}) %collective-permute-start.16) | collective-permute-done | bytes 262176 | tf_op jit(solution)/shard_map/ppermute | solution.py:432
  311.8 2.0 shard_map.202
  313.8 8.7 %all-to-all-start.6 = ((bf16[64,20,128]{2,1,0:T(8,128)(2,1)}), bf16[64,20,128]{2,1,0:T(8,128)(2,1)S(1)}, u32[]{:S(2)}, u32[]{:S(2)}) async-start(bf16[64,20,128]{2,1,0:T(8,128)(2,1)} %shard_map.202), calls=%async_computation.6 | async-start | bytes 786432 | tf_op jit(solution)/shard_map/all_to_all | solution.py:38
  323.0 5.4 %collective-permute-start.19 = (bf16[16,32,256]{2,1,0:T(8,128)(2,1)S(1)}, bf16[16,32,256]{2,1,0:T(8,128)(2,1)S(1)}, u32[]{:S(2)}, u32[]{:S(2)}) collective-permute-start(bf16[16,32,256]{2,1,0:T(8,128)(2,1)S(1)} %copy-done.31), channel_id=1, source_target_pairs={{0,8},{1,9},{2,10},{3,11},{4,12},{5,13},{6,14},{7,15},{8,0},{9,1},... | collective-permute-start | bytes 786440 | tf_op jit(solution)/shard_map/ppermute | solution.py:432
  328.7 2.4 collective-permute-start.21
  332.7 2.7 collective-permute-start.23
  335.4 8.8 %collective-permute-done.19.refs_4_ = bf16[16,32,256]{2,1,0:T(8,128)(2,1)S(1)} collective-permute-done((bf16[16,32,256]{2,1,0:T(8,128)(2,1)S(1)}, bf16[16,32,256]{2,1,0:T(8,128)(2,1)S(1)}, u32[]{:S(2)}, u32[]{:S(2)}) %collective-permute-start.19) | collective-permute-done | bytes 262176 | tf_op jit(solution)/shard_map/ppermute | solution.py:432
  344.3 3.1 collective-permute-start.24
  347.3 13.1 %collective-permute-done.20.refs_5_ = bf16[16,32,256]{2,1,0:T(8,128)(2,1)S(1)} collective-permute-done((bf16[16,32,256]{2,1,0:T(8,128)(2,1)}, bf16[16,32,256]{2,1,0:T(8,128)(2,1)S(1)}, u32[]{:S(2)}, u32[]{:S(2)}) %collective-permute-start.20) | collective-permute-done | bytes 262176 | tf_op jit(solution)/shard_map/ppermute | solution.py:432
  360.5 4.0 collective-permute-start.25
  364.5 8.8 %collective-permute-done.21.refs_6_ = bf16[16,32,256]{2,1,0:T(8,128)(2,1)S(1)} collective-permute-done((bf16[16,32,256]{2,1,0:T(8,128)(2,1)}, bf16[16,32,256]{2,1,0:T(8,128)(2,1)S(1)}, u32[]{:S(2)}, u32[]{:S(2)}) %collective-permute-start.21) | collective-permute-done | bytes 262176 | tf_op jit(solution)/shard_map/ppermute | solution.py:432
  373.3 2.6 collective-permute-start.26
  376.0 2.0 collective-permute-done.22.refs_7_
  377.9 3.4 collective-permute-start.27
  382.5 5.3 %collective-permute-done.27.refs_15_ = bf16[16,32,256]{2,1,0:T(8,128)(2,1)} collective-permute-done((bf16[16,32,256]{2,1,0:T(8,128)(2,1)}, bf16[16,32,256]{2,1,0:T(8,128)(2,1)}, u32[]{:S(2)}, u32[]{:S(2)}) %collective-permute-start.27) | collective-permute-done | bytes 262176 | tf_op jit(solution)/shard_map/ppermute | solution.py:435
  387.9 132.0 %shard_map.203 = (bf16[128,32,256]{2,1,0:T(8,128)(2,1)}, bf16[128,32,256]{2,1,0:T(8,128)(2,1)}) custom-call(s32[2,64]{1,0:T(2,128)} %pad_add_fusion.place_ref, s32[64]{0:T(128)} %compare_select_fusion.8.arrive_ref, bf16[64,8,128]{2,1,0:T(8,128)(2,1)} %copy-done.2, bf16[16,32,256]{2,1,0:T(8,128)(2,1)} %get-tuple-element.175.refs_0_, ...), custom_call_target="tpu_custom_call" | custom-call | bytes 8388608 | tf_op jit(solution)/shard_map/pallas_call | solution.py:496
  (147 shorter events, 30.9 us)
Async XLA Ops:
  0.7 52.4 %copy-start.6 = (s32[64,512]{1,0:T(8,128)S(1)}, s32[64,512]{1,0:T(8,128)}, u32[]{:S(2)}) copy-start(s32[64,512]{1,0:T(8,128)} %param.21) | copy-start | bytes 393220
  4.3 24.5 %all-to-all-start = ((bf16[64,8,128]{2,1,0:T(8,128)(2,1)}), bf16[64,8,128]{2,1,0:T(8,128)(2,1)S(1)}, u32[]{:S(2)}, u32[]{:S(2)}) async-start(bf16[64,8,128]{2,1,0:T(8,128)(2,1)} %bitcast.10), calls=%async_computation | async-start | bytes 262144 | tf_op jit(solution)/shard_map/all_to_all | solution.py:38
  28.8 15.0 %collective-permute-start = (bf16[16,32,256]{2,1,0:T(8,128)(2,1)}, bf16[16,32,256]{2,1,0:T(8,128)(2,1)S(1)}, u32[]{:S(2)}, u32[]{:S(2)}) collective-permute-start(bf16[16,32,256]{2,1,0:T(8,128)(2,1)} %get-tuple-element.116), channel_id=1, source_target_pairs={{0,1},{1,0},{2,3},{3,2},{4,5},{5,4},{6,7},{7,6},{8,9},{9,8},{10,11... | collective-permute-start | bytes 786440 | tf_op jit(solution)/shard_map/ppermute | solution.py:355
  29.4 17.6 %collective-permute-start.1 = (bf16[16,32,256]{2,1,0:T(8,128)(2,1)}, bf16[16,32,256]{2,1,0:T(8,128)(2,1)S(1)}, u32[]{:S(2)}, u32[]{:S(2)}) collective-permute-start(bf16[16,32,256]{2,1,0:T(8,128)(2,1)} %get-tuple-element.117), channel_id=1, source_target_pairs={{0,16},{1,17},{2,18},{3,19},{4,20},{5,21},{6,22},{7,23},{8,24},{9,... | collective-permute-start | bytes 786440 | tf_op jit(solution)/shard_map/ppermute | solution.py:355
  30.7 16.9 %collective-permute-start.2 = (bf16[16,32,256]{2,1,0:T(8,128)(2,1)}, bf16[16,32,256]{2,1,0:T(8,128)(2,1)S(1)}, u32[]{:S(2)}, u32[]{:S(2)}) collective-permute-start(bf16[16,32,256]{2,1,0:T(8,128)(2,1)} %get-tuple-element.118), channel_id=1, source_target_pairs={{0,17},{1,16},{2,19},{3,18},{4,21},{5,20},{6,23},{7,22},{8,25},{9,... | collective-permute-start | bytes 786440 | tf_op jit(solution)/shard_map/ppermute | solution.py:355
  32.3 18.4 %collective-permute-start.3 = (bf16[16,32,256]{2,1,0:T(8,128)(2,1)}, bf16[16,32,256]{2,1,0:T(8,128)(2,1)S(1)}, u32[]{:S(2)}, u32[]{:S(2)}) collective-permute-start(bf16[16,32,256]{2,1,0:T(8,128)(2,1)} %get-tuple-element.119), channel_id=1, source_target_pairs={{0,2},{1,3},{2,4},{3,5},{4,6},{5,7},{6,8},{7,9},{8,10},{9,11},{10,... | collective-permute-start | bytes 786440 | tf_op jit(solution)/shard_map/ppermute | solution.py:358
  33.6 21.3 %collective-permute-start.4 = (bf16[16,32,256]{2,1,0:T(8,128)(2,1)}, bf16[16,32,256]{2,1,0:T(8,128)(2,1)S(1)}, u32[]{:S(2)}, u32[]{:S(2)}) collective-permute-start(bf16[16,32,256]{2,1,0:T(8,128)(2,1)} %get-tuple-element.120), channel_id=1, source_target_pairs={{0,4},{1,5},{2,6},{3,7},{4,8},{5,9},{6,10},{7,11},{8,12},{9,13},{1... | collective-permute-start | bytes 786440 | tf_op jit(solution)/shard_map/ppermute | solution.py:358
  37.5 21.6 %all-to-all-start.1 = ((bf16[64,8,128]{2,1,0:T(8,128)(2,1)}), bf16[64,8,128]{2,1,0:T(8,128)(2,1)S(1)}, u32[]{:S(2)}, u32[]{:S(2)}) async-start(bf16[64,8,128]{2,1,0:T(8,128)(2,1)} %get-tuple-element.115), calls=%async_computation.1 | async-start | bytes 262144 | tf_op jit(solution)/shard_map/all_to_all | solution.py:38
  43.9 51.3 %copy-start.19 = (bf16[16,32,256]{2,1,0:T(8,128)(2,1)}, bf16[16,32,256]{2,1,0:T(8,128)(2,1)S(1)}, u32[]{:S(2)}) copy-start(bf16[16,32,256]{2,1,0:T(8,128)(2,1)S(1)} %collective-permute-done.refs_1_) | copy-start | bytes 786436
  43.9 31.2 %collective-permute-start.5 = (bf16[16,32,256]{2,1,0:T(8,128)(2,1)}, bf16[16,32,256]{2,1,0:T(8,128)(2,1)S(1)}, u32[]{:S(2)}, u32[]{:S(2)}) collective-permute-start(bf16[16,32,256]{2,1,0:T(8,128)(2,1)} %get-tuple-element.122), channel_id=1, source_target_pairs={{0,32},{1,33},{2,34},{3,35},{4,36},{5,37},{6,38},{7,39},{8,40},{9,... | collective-permute-start | bytes 786440 | tf_op jit(solution)/shard_map/ppermute | solution.py:355
  46.9 48.2 %copy-start.20 = (bf16[16,32,256]{2,1,0:T(8,128)(2,1)}, bf16[16,32,256]{2,1,0:T(8,128)(2,1)S(1)}, u32[]{:S(2)}) copy-start(bf16[16,32,256]{2,1,0:T(8,128)(2,1)S(1)} %collective-permute-done.1.refs_2_) | copy-start | bytes 786436
  46.9 31.0 %collective-permute-start.6 = (bf16[16,32,256]{2,1,0:T(8,128)(2,1)}, bf16[16,32,256]{2,1,0:T(8,128)(2,1)S(1)}, u32[]{:S(2)}, u32[]{:S(2)}) collective-permute-start(bf16[16,32,256]{2,1,0:T(8,128)(2,1)} %get-tuple-element.123), channel_id=1, source_target_pairs={{0,33},{1,32},{2,35},{3,34},{4,37},{5,36},{6,39},{7,38},{8,41},{9,... | collective-permute-start | bytes 786440 | tf_op jit(solution)/shard_map/ppermute | solution.py:355
  47.5 47.6 %copy-start.21 = (bf16[16,32,256]{2,1,0:T(8,128)(2,1)}, bf16[16,32,256]{2,1,0:T(8,128)(2,1)S(1)}, u32[]{:S(2)}) copy-start(bf16[16,32,256]{2,1,0:T(8,128)(2,1)S(1)} %collective-permute-done.2.refs_3_) | copy-start | bytes 786436
  47.6 31.4 %collective-permute-start.7 = (bf16[16,32,256]{2,1,0:T(8,128)(2,1)}, bf16[16,32,256]{2,1,0:T(8,128)(2,1)S(1)}, u32[]{:S(2)}, u32[]{:S(2)}) collective-permute-start(bf16[16,32,256]{2,1,0:T(8,128)(2,1)} %get-tuple-element.124), channel_id=1, source_target_pairs={{0,6},{1,7},{2,8},{3,9},{4,10},{5,11},{6,12},{7,13},{8,14},{9,15},... | collective-permute-start | bytes 786440 | tf_op jit(solution)/shard_map/ppermute | solution.py:358
  50.6 44.5 %copy-start.22 = (bf16[16,32,256]{2,1,0:T(8,128)(2,1)}, bf16[16,32,256]{2,1,0:T(8,128)(2,1)S(1)}, u32[]{:S(2)}) copy-start(bf16[16,32,256]{2,1,0:T(8,128)(2,1)S(1)} %collective-permute-done.3.refs_1_) | copy-start | bytes 786436
  50.6 38.9 %collective-permute-start.8 = (bf16[16,32,256]{2,1,0:T(8,128)(2,1)}, bf16[16,32,256]{2,1,0:T(8,128)(2,1)S(1)}, u32[]{:S(2)}, u32[]{:S(2)}) collective-permute-start(bf16[16,32,256]{2,1,0:T(8,128)(2,1)} %get-tuple-element.125), channel_id=1, source_target_pairs={{0,8},{1,9},{2,10},{3,11},{4,12},{5,13},{6,14},{7,15},{8,0},{9,1},... | collective-permute-start | bytes 786440 | tf_op jit(solution)/shard_map/ppermute | solution.py:358
  54.9 34.6 %collective-permute-start.9 = (bf16[16,32,256]{2,1,0:T(8,128)(2,1)}, bf16[16,32,256]{2,1,0:T(8,128)(2,1)}, u32[]{:S(2)}, u32[]{:S(2)}) collective-permute-start(bf16[16,32,256]{2,1,0:T(8,128)(2,1)} %get-tuple-element.126), channel_id=1, source_target_pairs={{0,10},{1,11},{2,12},{3,13},{4,14},{5,15},{6,0},{7,1},{8,2},{9,3},... | collective-permute-start | bytes 786440 | tf_op jit(solution)/shard_map/ppermute | solution.py:358
  63.9 52.7 %copy-start.3 = (bf16[2560,160]{0,1:T(8,128)(2,1)S(1)}, bf16[2560,160]{0,1:T(8,128)(2,1)}, u32[]{:S(2)}) copy-start(bf16[2560,160]{0,1:T(8,128)(2,1)} %param.33) | copy-start | bytes 2457604
  65.6 25.5 %all-to-all-start.2 = ((bf16[64,8,128]{2,1,0:T(8,128)(2,1)}), bf16[64,8,128]{2,1,0:T(8,128)(2,1)S(1)}, u32[]{:S(2)}, u32[]{:S(2)}) async-start(bf16[64,8,128]{2,1,0:T(8,128)(2,1)} %bitcast.14), calls=%async_computation.2 | async-start | bytes 262144 | tf_op jit(solution)/shard_map/all_to_all | solution.py:38
  75.1 25.7 %collective-permute-start.10 = (bf16[16,32,256]{2,1,0:T(8,128)(2,1)}, bf16[16,32,256]{2,1,0:T(8,128)(2,1)}, u32[]{:S(2)}, u32[]{:S(2)}) collective-permute-start(bf16[16,32,256]{2,1,0:T(8,128)(2,1)} %get-tuple-element.129), channel_id=1, source_target_pairs={{0,48},{1,49},{2,50},{3,51},{4,52},{5,53},{6,54},{7,55},{8,56},{9,... | collective-permute-start | bytes 786440 | tf_op jit(solution)/shard_map/ppermute | solution.py:355
  78.0 22.8 %collective-permute-start.11 = (bf16[16,32,256]{2,1,0:T(8,128)(2,1)}, bf16[16,32,256]{2,1,0:T(8,128)(2,1)}, u32[]{:S(2)}, u32[]{:S(2)}) collective-permute-start(bf16[16,32,256]{2,1,0:T(8,128)(2,1)} %get-tuple-element.130), channel_id=1, source_target_pairs={{0,49},{1,48},{2,51},{3,50},{4,53},{5,52},{6,55},{7,54},{8,57},{9,... | collective-permute-start | bytes 786440 | tf_op jit(solution)/shard_map/ppermute | solution.py:355
  79.0 21.8 %collective-permute-start.12 = (bf16[16,32,256]{2,1,0:T(8,128)(2,1)}, bf16[16,32,256]{2,1,0:T(8,128)(2,1)}, u32[]{:S(2)}, u32[]{:S(2)}) collective-permute-start(bf16[16,32,256]{2,1,0:T(8,128)(2,1)} %get-tuple-element.131), channel_id=1, source_target_pairs={{0,12},{1,13},{2,14},{3,15},{4,0},{5,1},{6,2},{7,3},{8,4},{9,5},{1... | collective-permute-start | bytes 786440 | tf_op jit(solution)/shard_map/ppermute | solution.py:358
  89.5 12.1 %collective-permute-start.13 = (bf16[16,32,256]{2,1,0:T(8,128)(2,1)}, bf16[16,32,256]{2,1,0:T(8,128)(2,1)}, u32[]{:S(2)}, u32[]{:S(2)}) collective-permute-start(bf16[16,32,256]{2,1,0:T(8,128)(2,1)} %get-tuple-element.132), channel_id=1, source_target_pairs={{0,14},{1,15},{2,0},{3,1},{4,2},{5,3},{6,4},{7,5},{8,6},{9,7},{10,... | collective-permute-start | bytes 786440 | tf_op jit(solution)/shard_map/ppermute | solution.py:358
  95.2 8.6 %all-to-all-start.3 = ((f32[4,20,128]{2,1,0:T(8,128)}), f32[4,20,128]{2,1,0:T(8,128)S(1)}, u32[]{:S(2)}, u32[]{:S(2)}) async-start(f32[4,20,128]{2,1,0:T(8,128)} %shard_map.197), calls=%async_computation.3 | async-start | bytes 98304 | tf_op jit(solution)/shard_map/all_to_all | solution.py:407
  106.2 142.9 %all-to-all-start.4 = ((bf16[64,20,128]{2,1,0:T(8,128)(2,1)}), bf16[64,20,128]{2,1,0:T(8,128)(2,1)S(1)}, u32[]{:S(2)}, u32[]{:S(2)}) async-start(bf16[64,20,128]{2,1,0:T(8,128)(2,1)} %get-tuple-element.134), calls=%async_computation.4 | async-start | bytes 786432 | tf_op jit(solution)/shard_map/all_to_all | solution.py:38
  249.9 72.7 %copy-start.29 = (s32[4096,1]{0,1:T(1,128)S(1)}, s32[4096,1]{0,1:T(1,128)}, u32[]{:S(2)}) copy-start(s32[4096,1]{0,1:T(1,128)} %param.22) | copy-start | bytes 49156
  249.9 73.2 %copy-start.31 = (bf16[16,32,256]{2,1,0:T(8,128)(2,1)S(1)}, bf16[16,32,256]{2,1,0:T(8,128)(2,1)}, u32[]{:S(2)}) copy-start(bf16[16,32,256]{2,1,0:T(8,128)(2,1)} %get-tuple-element.179) | copy-start | bytes 786436
  255.5 55.5 %all-to-all-start.5 = ((bf16[64,20,128]{2,1,0:T(8,128)(2,1)}), bf16[64,20,128]{2,1,0:T(8,128)(2,1)S(1)}, u32[]{:S(2)}, u32[]{:S(2)}) async-start(bf16[64,20,128]{2,1,0:T(8,128)(2,1)} %reshape.614), calls=%async_computation.5 | async-start | bytes 786432 | tf_op jit(solution)/shard_map/all_to_all | solution.py:38
  265.9 17.2 %collective-permute-start.14 = (bf16[16,32,256]{2,1,0:T(8,128)(2,1)S(1)}, bf16[16,32,256]{2,1,0:T(8,128)(2,1)S(1)}, u32[]{:S(2)}, u32[]{:S(2)}) collective-permute-start(bf16[16,32,256]{2,1,0:T(8,128)(2,1)S(1)} %copy-done.36), channel_id=1, source_target_pairs={{0,2},{1,3},{2,4},{3,5},{4,6},{5,7},{6,8},{7,9},{8,10},{9,11},{10,... | collective-permute-start | bytes 786440 | tf_op jit(solution)/shard_map/ppermute | solution.py:432
  267.3 25.3 %collective-permute-start.15 = (bf16[16,32,256]{2,1,0:T(8,128)(2,1)S(1)}, bf16[16,32,256]{2,1,0:T(8,128)(2,1)S(1)}, u32[]{:S(2)}, u32[]{:S(2)}) collective-permute-start(bf16[16,32,256]{2,1,0:T(8,128)(2,1)S(1)} %copy-done.35), channel_id=1, source_target_pairs={{0,4},{1,5},{2,6},{3,7},{4,8},{5,9},{6,10},{7,11},{8,12},{9,13},{1... | collective-permute-start | bytes 786440 | tf_op jit(solution)/shard_map/ppermute | solution.py:432
  269.4 41.6 %collective-permute-start.16 = (bf16[16,32,256]{2,1,0:T(8,128)(2,1)S(1)}, bf16[16,32,256]{2,1,0:T(8,128)(2,1)S(1)}, u32[]{:S(2)}, u32[]{:S(2)}) collective-permute-start(bf16[16,32,256]{2,1,0:T(8,128)(2,1)S(1)} %copy-done.34), channel_id=1, source_target_pairs={{0,6},{1,7},{2,8},{3,9},{4,10},{5,11},{6,12},{7,13},{8,14},{9,15},... | collective-permute-start | bytes 786440 | tf_op jit(solution)/shard_map/ppermute | solution.py:432
  271.8 39.2 %collective-permute-start.17 = (bf16[16,32,256]{2,1,0:T(8,128)(2,1)S(1)}, bf16[16,32,256]{2,1,0:T(8,128)(2,1)S(1)}, u32[]{:S(2)}, u32[]{:S(2)}) collective-permute-start(bf16[16,32,256]{2,1,0:T(8,128)(2,1)S(1)} %copy-done.33), channel_id=1, source_target_pairs={{0,1},{1,0},{2,3},{3,2},{4,5},{5,4},{6,7},{7,6},{8,9},{9,8},{10,11... | collective-permute-start | bytes 786440 | tf_op jit(solution)/shard_map/ppermute | solution.py:435
  273.0 38.0 %collective-permute-start.18 = (bf16[16,32,256]{2,1,0:T(8,128)(2,1)S(1)}, bf16[16,32,256]{2,1,0:T(8,128)(2,1)S(1)}, u32[]{:S(2)}, u32[]{:S(2)}) collective-permute-start(bf16[16,32,256]{2,1,0:T(8,128)(2,1)S(1)} %copy-done.32), channel_id=1, source_target_pairs={{0,16},{1,17},{2,18},{3,19},{4,20},{5,21},{6,22},{7,23},{8,24},{9,... | collective-permute-start | bytes 786440 | tf_op jit(solution)/shard_map/ppermute | solution.py:435
  283.1 104.8 %copy-start.8 = (bf16[16,32,256]{2,1,0:T(8,128)(2,1)}, bf16[16,32,256]{2,1,0:T(8,128)(2,1)S(1)}, u32[]{:S(2)}) copy-start(bf16[16,32,256]{2,1,0:T(8,128)(2,1)S(1)} %collective-permute-done.14.refs_1_) | copy-start | bytes 786436
  292.6 95.2 %copy-start.9 = (bf16[16,32,256]{2,1,0:T(8,128)(2,1)}, bf16[16,32,256]{2,1,0:T(8,128)(2,1)S(1)}, u32[]{:S(2)}) copy-start(bf16[16,32,256]{2,1,0:T(8,128)(2,1)S(1)} %collective-permute-done.15.refs_2_) | copy-start | bytes 786436
  311.0 76.8 %copy-start.10 = (bf16[16,32,256]{2,1,0:T(8,128)(2,1)}, bf16[16,32,256]{2,1,0:T(8,128)(2,1)S(1)}, u32[]{:S(2)}) copy-start(bf16[16,32,256]{2,1,0:T(8,128)(2,1)S(1)} %collective-permute-done.16.refs_3_) | copy-start | bytes 786436
  311.0 76.8 %copy-start.11 = (bf16[16,32,256]{2,1,0:T(8,128)(2,1)}, bf16[16,32,256]{2,1,0:T(8,128)(2,1)S(1)}, u32[]{:S(2)}) copy-start(bf16[16,32,256]{2,1,0:T(8,128)(2,1)S(1)} %collective-permute-done.17.refs_9_) | copy-start | bytes 786436
  311.0 76.8 %copy-start.12 = (bf16[16,32,256]{2,1,0:T(8,128)(2,1)}, bf16[16,32,256]{2,1,0:T(8,128)(2,1)S(1)}, u32[]{:S(2)}) copy-start(bf16[16,32,256]{2,1,0:T(8,128)(2,1)S(1)} %collective-permute-done.18.refs_10_) | copy-start | bytes 786436
  313.8 206.1 %all-to-all-start.6 = ((bf16[64,20,128]{2,1,0:T(8,128)(2,1)}), bf16[64,20,128]{2,1,0:T(8,128)(2,1)S(1)}, u32[]{:S(2)}, u32[]{:S(2)}) async-start(bf16[64,20,128]{2,1,0:T(8,128)(2,1)} %shard_map.202), calls=%async_computation.6 | async-start | bytes 786432 | tf_op jit(solution)/shard_map/all_to_all | solution.py:38
  323.0 21.2 %collective-permute-start.19 = (bf16[16,32,256]{2,1,0:T(8,128)(2,1)S(1)}, bf16[16,32,256]{2,1,0:T(8,128)(2,1)S(1)}, u32[]{:S(2)}, u32[]{:S(2)}) collective-permute-start(bf16[16,32,256]{2,1,0:T(8,128)(2,1)S(1)} %copy-done.31), channel_id=1, source_target_pairs={{0,8},{1,9},{2,10},{3,11},{4,12},{5,13},{6,14},{7,15},{8,0},{9,1},... | collective-permute-start | bytes 786440 | tf_op jit(solution)/shard_map/ppermute | solution.py:432
  328.4 32.0 %collective-permute-start.20 = (bf16[16,32,256]{2,1,0:T(8,128)(2,1)}, bf16[16,32,256]{2,1,0:T(8,128)(2,1)S(1)}, u32[]{:S(2)}, u32[]{:S(2)}) collective-permute-start(bf16[16,32,256]{2,1,0:T(8,128)(2,1)} %get-tuple-element.180), channel_id=1, source_target_pairs={{0,10},{1,11},{2,12},{3,13},{4,14},{5,15},{6,0},{7,1},{8,2},{9,3},... | collective-permute-start | bytes 786440 | tf_op jit(solution)/shard_map/ppermute | solution.py:432
  328.7 44.6 %collective-permute-start.21 = (bf16[16,32,256]{2,1,0:T(8,128)(2,1)}, bf16[16,32,256]{2,1,0:T(8,128)(2,1)S(1)}, u32[]{:S(2)}, u32[]{:S(2)}) collective-permute-start(bf16[16,32,256]{2,1,0:T(8,128)(2,1)} %get-tuple-element.181), channel_id=1, source_target_pairs={{0,12},{1,13},{2,14},{3,15},{4,0},{5,1},{6,2},{7,3},{8,4},{9,5},{1... | collective-permute-start | bytes 786440 | tf_op jit(solution)/shard_map/ppermute | solution.py:432
  331.1 46.8 %collective-permute-start.22 = (bf16[16,32,256]{2,1,0:T(8,128)(2,1)}, bf16[16,32,256]{2,1,0:T(8,128)(2,1)S(1)}, u32[]{:S(2)}, u32[]{:S(2)}) collective-permute-start(bf16[16,32,256]{2,1,0:T(8,128)(2,1)} %get-tuple-element.182), channel_id=1, source_target_pairs={{0,14},{1,15},{2,0},{3,1},{4,2},{5,3},{6,4},{7,5},{8,6},{9,7},{10,... | collective-permute-start | bytes 786440 | tf_op jit(solution)/shard_map/ppermute | solution.py:432
  332.7 49.7 %collective-permute-start.23 = (bf16[16,32,256]{2,1,0:T(8,128)(2,1)}, bf16[16,32,256]{2,1,0:T(8,128)(2,1)S(1)}, u32[]{:S(2)}, u32[]{:S(2)}) collective-permute-start(bf16[16,32,256]{2,1,0:T(8,128)(2,1)} %get-tuple-element.186), channel_id=1, source_target_pairs={{0,17},{1,16},{2,19},{3,18},{4,21},{5,20},{6,23},{7,22},{8,25},{9,... | collective-permute-start | bytes 786440 | tf_op jit(solution)/shard_map/ppermute | solution.py:435
  344.3 38.2 %collective-permute-start.24 = (bf16[16,32,256]{2,1,0:T(8,128)(2,1)}, bf16[16,32,256]{2,1,0:T(8,128)(2,1)S(1)}, u32[]{:S(2)}, u32[]{:S(2)}) collective-permute-start(bf16[16,32,256]{2,1,0:T(8,128)(2,1)} %get-tuple-element.187), channel_id=1, source_target_pairs={{0,32},{1,33},{2,34},{3,35},{4,36},{5,37},{6,38},{7,39},{8,40},{9,... | collective-permute-start | bytes 786440 | tf_op jit(solution)/shard_map/ppermute | solution.py:435
  360.5 22.0 %collective-permute-start.25 = (bf16[16,32,256]{2,1,0:T(8,128)(2,1)}, bf16[16,32,256]{2,1,0:T(8,128)(2,1)}, u32[]{:S(2)}, u32[]{:S(2)}) collective-permute-start(bf16[16,32,256]{2,1,0:T(8,128)(2,1)} %get-tuple-element.188), channel_id=1, source_target_pairs={{0,33},{1,32},{2,35},{3,34},{4,37},{5,36},{6,39},{7,38},{8,41},{9,... | collective-permute-start | bytes 786440 | tf_op jit(solution)/shard_map/ppermute | solution.py:435
  373.3 9.2 %collective-permute-start.26 = (bf16[16,32,256]{2,1,0:T(8,128)(2,1)}, bf16[16,32,256]{2,1,0:T(8,128)(2,1)}, u32[]{:S(2)}, u32[]{:S(2)}) collective-permute-start(bf16[16,32,256]{2,1,0:T(8,128)(2,1)} %get-tuple-element.189), channel_id=1, source_target_pairs={{0,48},{1,49},{2,50},{3,51},{4,52},{5,53},{6,54},{7,55},{8,56},{9,... | collective-permute-start | bytes 786440 | tf_op jit(solution)/shard_map/ppermute | solution.py:435
  377.9 9.9 %collective-permute-start.27 = (bf16[16,32,256]{2,1,0:T(8,128)(2,1)}, bf16[16,32,256]{2,1,0:T(8,128)(2,1)}, u32[]{:S(2)}, u32[]{:S(2)}) collective-permute-start(bf16[16,32,256]{2,1,0:T(8,128)(2,1)} %get-tuple-element.190), channel_id=1, source_target_pairs={{0,49},{1,48},{2,51},{3,50},{4,53},{5,52},{6,55},{7,54},{8,57},{9,... | collective-permute-start | bytes 786440 | tf_op jit(solution)/shard_map/ppermute | solution.py:435
  (24 other events, 373.4 us)

commit v3 on v2

--- a/solution.py
+++ b/solution.py
@@ -180,67 +180,58 @@
 
 
 def regroup_body(count, *refs):
-    ins, outs, sem = refs[:count], refs[count:-1], refs[-1]
+    ins, outs = refs[:count], refs[count:-3]
+    held, in_sem, out_sem = refs[-3:]
     cap = outs[0].shape[0] // count
-    for j, out in enumerate(outs):
+    for j in range(len(outs)):
         for i, chunk in enumerate(ins):
             pltpu.make_async_copy(
-                chunk.at[j * cap : (j + 1) * cap], out.at[i * cap : (i + 1) * cap], sem.at[j]
+                chunk.at[j * cap : (j + 1) * cap], held.at[j, i * cap : (i + 1) * cap], in_sem.at[j]
             ).start()
     for j, out in enumerate(outs):
-        pltpu.make_async_copy(out, out, sem.at[j]).wait()
+        pltpu.make_async_copy(out, held.at[j], in_sem.at[j]).wait()
+        pltpu.make_async_copy(held.at[j], out, out_sem.at[j]).start()
+    for j, out in enumerate(outs):
+        pltpu.make_async_copy(held.at[j], out, out_sem.at[j]).wait()
 
 
 def assemble_body(counts, cap, place_ref, arrive_ref, fresh_ref, *refs):
     arrays = len(counts)
     chunks, outs = refs[: sum(counts)], refs[sum(counts) : -3]
-    pages, copy_sem, patch_sem = refs[-3:]
+    held, in_sem, out_sem = refs[-3:]
     page = outs[0].shape[1]
     requests, tiles = fresh_ref.shape[:2]
     first = 0
-    for p, out in enumerate(outs):
+    for p in range(arrays):
         inner = chunks[first].shape[0] // cap
         for j in range(counts[p]):
             for i in range(inner):
                 at = place_ref[p, j * inner + i] * cap
                 pltpu.make_async_copy(
                     chunks[first + j].at[i * cap : (i + 1) * cap],
-                    out.at[pl.ds(at, cap)],
-                    copy_sem.at[p],
+                    held.at[p, pl.ds(at, cap)],
+                    in_sem.at[p],
                 ).start()
         first += counts[p]
     for p, out in enumerate(outs):
-        pltpu.make_async_copy(out, out, copy_sem.at[p]).wait()
-
-    def each(act):
+        pltpu.make_async_copy(out, held.at[p], in_sem.at[p]).wait()
+
         @pl.loop(0, requests)
-        def _(r):
+        def _(r, p=p):
             where = arrive_ref[r]
 
             @pl.when(where >= 0)
             def _():
-                for p, out in enumerate(outs):
-                    act(p, r, out.at[where // page], where % page)
-
-    def fetch(p, r, slot):
-        return pltpu.make_async_copy(slot, pages.at[p, r], patch_sem.at[p, r])
-
-    def put(p, r, slot):
-        return pltpu.make_async_copy(pages.at[p, r], slot, patch_sem.at[p, r])
-
-    def change(p, r, slot, offset):
-        fetch(p, r, slot).wait()
-        at = tiles - 2 * arrays + 2 * p
-        new = fresh_ref[r].astype(F32)
-        row = jnp.concatenate([new[at : at + 1], new[at + 1 : at + 2]], axis=1)
-        old = pages[p, r].astype(F32)
-        here = lax.broadcasted_iota(jnp.int32, old.shape, 0) == offset
-        pages[p, r] = jnp.where(here, row, old).astype(BF16)
-        put(p, r, slot).start()
-
-    each(lambda p, r, slot, _: fetch(p, r, slot).start())
-    each(change)
-    each(lambda p, r, slot, _: put(p, r, slot).wait())
+                at = tiles - 2 * arrays + 2 * p
+                new = fresh_ref[r].astype(F32)
+                row = jnp.concatenate([new[at : at + 1], new[at + 1 : at + 2]], axis=1)
+                old = held[p, where // page].astype(F32)
+                here = lax.broadcasted_iota(jnp.int32, old.shape, 0) == where % page
+                held[p, where // page] = jnp.where(here, row, old).astype(BF16)
+
+        pltpu.make_async_copy(held.at[p], out, out_sem.at[p]).start()
+    for p, out in enumerate(outs):
+        pltpu.make_async_copy(held.at[p], out, out_sem.at[p]).wait()
 
 
 def local(
@@ -336,7 +327,11 @@
             out_shape=buffers(count),
             in_specs=[anywhere] * len(chunks),
             out_specs=[anywhere] * count,
-            scratch_shapes=[pltpu.SemaphoreType.DMA((count,))],
+            scratch_shapes=[
+                pltpu.VMEM((count, recv_slots // count, page, head), BF16),
+                pltpu.SemaphoreType.DMA((count,)),
+                pltpu.SemaphoreType.DMA((count,)),
+            ],
             cost_estimate=pl.CostEstimate(
                 flops=0, bytes_accessed=8 * slots * page * head, transcendentals=0
             ),
@@ -351,12 +346,22 @@
     keys_sends = gather(paged_keys, (step_near * depth + step_along) * capacity + rank, near)
     values_sends = gather(paged_values, (step_along * near + step_near) * capacity + rank, depth)
     terms, keys_sends, values_sends = tie(terms, keys_sends, values_sends)
-    keys_first = [keys_sends[0]] + [
-        lax.ppermute(keys_sends[k], "blk", to_near[k]) for k in range(1, near)
-    ]
-    values_first = [values_sends[0]] + [
-        lax.ppermute(values_sends[k], "blk", to_along[k]) for k in range(1, depth)
-    ]
+
+    def permutes(sends, targets):
+        return [sends[0]] + [
+            lax.ppermute(sends[k], "blk", targets[k]) for k in range(1, len(sends))
+        ]
+
+    def due(value, *wanted):
+        done = tie(value, *[moves[k] for moves, steps in wanted for k in steps])
+        rest = iter(done[1:])
+        for moves, steps in wanted:
+            for k in steps:
+                moves[k] = next(rest)
+        return done[0]
+
+    keys_first = permutes(keys_sends, to_near)
+    values_first = permutes(values_sends, to_along)
 
     frequency = jnp.exp(-(2.0 * jnp.arange(head // 2, dtype=F32) / head) * ROPE_LOG)
     position = lax.dynamic_slice_in_dim(positions, device, 1).astype(F32)
@@ -379,7 +384,7 @@
         key_gain.reshape(tile),
     )
     every = exchange(every)
-    every, keys_first[1:4], values_first[1:3] = tie(every, keys_first[1:4], values_first[1:3])
+    every = due(every, (values_first, (4, 1)), (keys_first, (4, 2, 6)))
 
     slot_ids = device * slots + jnp.arange(slots, dtype=jnp.int32)
     page_starts = jnp.arange(pages_per_seq, dtype=jnp.int32) * page
@@ -395,7 +400,8 @@
         4 * slots * page * head,
     )(every.reshape(requests, columns), paged_keys, paged_values, limit)
     parts = exchange(parts.reshape(requests, col_tiles, LANES))
-    parts, keys_first[4:6], values_first[3:6] = tie(parts, keys_first[4:6], values_first[3:6])
+    parts = due(parts, (values_first, (3, 5)), (keys_first, (5, 3, 7, 1)))
+    keys_sends = regroup(keys_first, depth)
     attn_terms = call(
         functools.partial(merge_body, groups),
         jax.ShapeDtypeStruct((kv_size, model_tiles, LANES), F32),
@@ -405,10 +411,9 @@
     )(parts, own, output_proj)
 
     attn_terms = lax.all_to_all(attn_terms, "kv", split_axis=0, concat_axis=0, tiled=True)
-    attn_terms, keys_first[6:], values_first[6:] = tie(
-        attn_terms, keys_first[6:], values_first[6:]
-    )
-    keys_sends = regroup(keys_first, depth)
+    attn_terms = due(attn_terms, (values_first, (2, 6, 7)))
+    attn_terms, keys_sends = tie(attn_terms, keys_sends)
+    keys_second = permutes(keys_sends, to_along)
     values_sends = regroup(values_first, near)
     wide = (model_tiles, LANES)
     residual, ffw_in = call(
@@ -427,13 +432,9 @@
         ffw_gain.reshape(wide),
     )
     ffw_in = exchange(ffw_in).reshape(requests, model)
-    ffw_in, keys_sends, values_sends = tie(ffw_in, keys_sends, values_sends)
-    keys_second = [keys_sends[0]] + [
-        lax.ppermute(keys_sends[k], "blk", to_along[k]) for k in range(1, depth)
-    ]
-    values_second = [values_sends[0]] + [
-        lax.ppermute(values_sends[k], "blk", to_near[k]) for k in range(1, near)
-    ]
+    ffw_in = due(ffw_in, (keys_second, (3, 5)))
+    ffw_in, values_sends = tie(ffw_in, values_sends)
+    values_second = permutes(values_sends, to_near)
     units = gate_weight.shape[1]
     ffw_terms = call(
         ffw_body,
@@ -443,9 +444,7 @@
         6 * units * model,
     )(ffw_in, gate_weight, up_weight, down_weight)
     ffw_terms = exchange(ffw_terms.reshape((requests,) + wide))
-    ffw_terms, keys_second[1:4], values_second[1:3] = tie(
-        ffw_terms, keys_second[1:4], values_second[1:3]
-    )
+    ffw_terms = due(ffw_terms, (keys_second, (2, 6, 4)), (values_second, (4, 2)))
     out_rows = call(
         output_body,
         jax.ShapeDtypeStruct((requests,) + wide, BF16),
@@ -499,9 +498,9 @@
         in_specs=[smem, smem, vmem] + [anywhere] * (depth + near),
         out_specs=[anywhere] * 2,
         scratch_shapes=[
-            pltpu.VMEM((2, requests, page, head), BF16),
+            pltpu.VMEM((2, recv_slots, page, head), BF16),
             pltpu.SemaphoreType.DMA((2,)),
-            pltpu.SemaphoreType.DMA((2, requests)),
+            pltpu.SemaphoreType.DMA((2,)),
         ],
         cost_estimate=pl.CostEstimate(
             flops=0, bytes_accessed=16 * slots * page * head, transcendentals=0

time: 522 us -> 240 us (0.46)
  Pallas kernels: 284 us -> 32.2 us
  starting transfers between devices: 131 us -> 115 us
  waiting for transfers between devices: 79.2 us -> 64.4 us
    pallas_call x1, Pallas kernels: 132 us -> 4.46 us  [local(): pl.pallas_call(functools.partial(assemble_body, (depth, near), capacity),...]
    pallas_call x2, Pallas kernels: 129 us -> 4.8 us  [regroup(): pl.pallas_call(functools.partial(regroup_body, len(chunks)), out_shape=bu...]
    ppermute x28, waiting for transfers between devices: 75.6 us -> 50.5 us  [permutes(): lax.ppermute(sends[k], 'blk', targets[k])]
    all_to_all x6, waiting for transfers between devices: 1.51 us -> 13.4 us  [exchange(): return lax.all_to_all(x, 'blk', split_axis=0, concat_axis=0, tiled=True)]
    ppermute x28, starting transfers between devices: 68.1 us -> 57.6 us  [permutes(): lax.ppermute(sends[k], 'blk', targets[k])]
    all_to_all x6, starting transfers between devices: 58.3 us -> 52.6 us  [exchange(): return lax.all_to_all(x, 'blk', split_axis=0, concat_axis=0, tiled=True)]
  transfers between devices with their start and end apart: 35 -> 35, of which waited for: 11 -> 12; matrix products, arithmetic and copies ran while one was open for 3% -> 7% of each run, Pallas kernels for 53% -> 10%
where the time goes in v3:
time: 240 us; the launch traced here: 238 us
  starting transfers between devices  115 us (48%)
  waiting for transfers between devices  64.4 us (27%)
  Pallas kernels  32.2 us (13%)
  local copies, waits for them, and re-layouts  15.9 us (7%)
  other arithmetic  8.1 us (3%)
    ppermute x28, starting transfers between devices, permutes(): lax.ppermute(sends[k], 'blk', targets[k])  57.6 us
    all_to_all x6, starting transfers between devices, exchange(): return lax.all_to_all(x, 'blk', split_axis=0, concat_axis=0, tiled=True)  52.6 us
    ppermute x28, waiting for transfers between devices, permutes(): lax.ppermute(sends[k], 'blk', targets[k])  50.5 us
    all_to_all x6, waiting for transfers between devices, exchange(): return lax.all_to_all(x, 'blk', split_axis=0, concat_axis=0, tiled=True)  13.4 us
    unnamed x87, local copies, waits for them, and re-layouts  9.66 us
    pallas_call x2, Pallas kernels, gather(): pl.pallas_call(gather_body, out_shape=buffers(count), in_specs=[smem, vme...  6.09 us
  transfers between devices with their start and end apart: 35, of which 12 were waited for; matrix products, arithmetic and copies ran while one was open for 7% of the time, Pallas kernels for 10%

profile of v3, /device:TPU:1, one launch (start us, length us, event | category | flops | bytes accessed | tf_op | source)
XLA Modules:
  0.0 238.0 jit_solution(7259953968331630793)
XLA Ops:
  4.3 13.0 %all-to-all-start = ((bf16[64,8,128]{2,1,0:T(8,128)(2,1)}), bf16[64,8,128]{2,1,0:T(8,128)(2,1)S(1)}, u32[]{:S(2)}, u32[]{:S(2)}) async-start(bf16[64,8,128]{2,1,0:T(8,128)(2,1)} %bitcast.10), calls=%async_computation | async-start | bytes 262144 | tf_op jit(solution)/shard_map/all_to_all | solution.py:38
  22.2 3.0 %shard_map.193 = (bf16[16,32,256]{2,1,0:T(8,128)(2,1)}, bf16[16,32,256]{2,1,0:T(8,128)(2,1)}, bf16[16,32,256]{2,1,0:T(8,128)(2,1)}, bf16[16,32,256]{2,1,0:T(8,12...) custom-call(s32[128]{0:T(128)} %broadcast_add_fusion.1.source_ref, ...), custom_call_target="tpu_custom_call" | custom-call | bytes 3145728 | tf_op jit(solution)/shard_map/pallas_call | solution.py:314
  25.2 3.1 %shard_map.194 = (bf16[16,32,256]{2,1,0:T(8,128)(2,1)}, bf16[16,32,256]{2,1,0:T(8,128)(2,1)}, bf16[16,32,256]{2,1,0:T(8,128)(2,1)}, bf16[16,32,256]{2,1,0:T(8,12...) custom-call(s32[128]{0:T(128)} %broadcast_add_fusion.source_ref, ...), custom_call_target="tpu_custom_call" | custom-call | bytes 3145728 | tf_op jit(solution)/shard_map/pallas_call | solution.py:314
  28.9 5.4 %collective-permute-start = (bf16[16,32,256]{2,1,0:T(8,128)(2,1)}, bf16[16,32,256]{2,1,0:T(8,128)(2,1)S(1)}, u32[]{:S(2)}, u32[]{:S(2)}) collective-permute-start(bf16[16,32,256]{2,1,0:T(8,128)(2,1)} %get-tuple-element.120), channel_id=1, source_target_pairs={{0,8},{1,9},{2,10},{3,11},{4,12},{5,13},{6,14},{7,15},{8,0},{9,1},... | collective-permute-start | bytes 786440 | tf_op jit(solution)/shard_map/ppermute | solution.py:352
  34.6 2.9 %collective-permute-start.2 = (bf16[16,32,256]{2,1,0:T(8,128)(2,1)}, bf16[16,32,256]{2,1,0:T(8,128)(2,1)S(1)}, u32[]{:S(2)}, u32[]{:S(2)}) collective-permute-start(bf16[16,32,256]{2,1,0:T(8,128)(2,1)} %get-tuple-element.122), channel_id=1, source_target_pairs={{0,32},{1,33},{2,34},{3,35},{4,36},{5,37},{6,38},{7,39},{8,40},{9,... | collective-permute-start | bytes 786440 | tf_op jit(solution)/shard_map/ppermute | solution.py:352
  37.9 2.4 collective-permute-start.4
  40.3 1.8 shard_map.195
  42.0 6.3 %all-to-all-start.1 = ((bf16[64,8,128]{2,1,0:T(8,128)(2,1)}), bf16[64,8,128]{2,1,0:T(8,128)(2,1)S(1)}, u32[]{:S(2)}, u32[]{:S(2)}) async-start(bf16[64,8,128]{2,1,0:T(8,128)(2,1)} %get-tuple-element.119), calls=%async_computation.1 | async-start | bytes 262144 | tf_op jit(solution)/shard_map/all_to_all | solution.py:38
  48.9 3.7 %collective-permute-done.1.refs_1_ = bf16[16,32,256]{2,1,0:T(8,128)(2,1)S(1)} collective-permute-done((bf16[16,32,256]{2,1,0:T(8,128)(2,1)}, bf16[16,32,256]{2,1,0:T(8,128)(2,1)S(1)}, u32[]{:S(2)}, u32[]{:S(2)}) %collective-permute-start.1) | collective-permute-done | bytes 262176 | tf_op jit(solution)/shard_map/ppermute | solution.py:352
  53.3 3.7 %collective-permute-start.6 = (bf16[16,32,256]{2,1,0:T(8,128)(2,1)}, bf16[16,32,256]{2,1,0:T(8,128)(2,1)S(1)}, u32[]{:S(2)}, u32[]{:S(2)}) collective-permute-start(bf16[16,32,256]{2,1,0:T(8,128)(2,1)} %get-tuple-element.127), channel_id=1, source_target_pairs={{0,10},{1,11},{2,12},{3,13},{4,14},{5,15},{6,0},{7,1},{8,2},{9,3},... | collective-permute-start | bytes 786440 | tf_op jit(solution)/shard_map/ppermute | solution.py:352
  57.1 4.4 %collective-permute-start.7 = (bf16[16,32,256]{2,1,0:T(8,128)(2,1)}, bf16[16,32,256]{2,1,0:T(8,128)(2,1)S(1)}, u32[]{:S(2)}, u32[]{:S(2)}) collective-permute-start(bf16[16,32,256]{2,1,0:T(8,128)(2,1)} %get-tuple-element.128), channel_id=1, source_target_pairs={{0,33},{1,32},{2,35},{3,34},{4,37},{5,36},{6,39},{7,38},{8,41},{9,... | collective-permute-start | bytes 786440 | tf_op jit(solution)/shard_map/ppermute | solution.py:352
  64.2 2.9 %collective-permute-start.9 = (bf16[16,32,256]{2,1,0:T(8,128)(2,1)}, bf16[16,32,256]{2,1,0:T(8,128)(2,1)}, u32[]{:S(2)}, u32[]{:S(2)}) collective-permute-start(bf16[16,32,256]{2,1,0:T(8,128)(2,1)} %get-tuple-element.130), channel_id=1, source_target_pairs={{0,49},{1,48},{2,51},{3,50},{4,53},{5,52},{6,55},{7,54},{8,57},{9,... | collective-permute-start | bytes 786440 | tf_op jit(solution)/shard_map/ppermute | solution.py:352
  67.0 4.1 %shard_map.196 = bf16[64,1024]{1,0:T(8,128)(2,1)} custom-call(bf16[64,1024]{1,0:T(8,128)(2,1)} %bitcast.36, bf16[64,32,256]{2,1,0:T(8,128)(2,1)} %keys_ref.1, bf16[64,32,256]{2,1,0:T(8,128)(2,1)} %values_ref.1, bf16[64,64]{1,0:T(8,128)(2,1)} %convert_element_type.36.limit_ref), custom_call_target="tpu_custom_call" | custom-call | flops 268435456 | bytes 2097152 | tf_op jit(solution)/shard_map/pallas_call | solution.py:395
  71.1 1.6 copy.29
  72.7 5.2 %all-to-all-start.2 = ((bf16[64,8,128]{2,1,0:T(8,128)(2,1)}), bf16[64,8,128]{2,1,0:T(8,128)(2,1)S(1)}, u32[]{:S(2)}, u32[]{:S(2)}) async-start(bf16[64,8,128]{2,1,0:T(8,128)(2,1)} %bitcast.14), calls=%async_computation.2 | async-start | bytes 262144 | tf_op jit(solution)/shard_map/all_to_all | solution.py:38
  77.9 2.4 collective-permute-start.11
  83.0 5.3 %all-to-all-done.2.parts_ref = bf16[64,8,128]{2,1,0:T(8,128)(2,1)S(1)} async-done(((bf16[64,8,128]{2,1,0:T(8,128)(2,1)}), bf16[64,8,128]{2,1,0:T(8,128)(2,1)S(1)}, u32[]{:S(2)}, u32[]{:S(2)}) %all-to-all-start.2) | async-done | bytes 131104 | tf_op jit(solution)/shard_map/all_to_all | solution.py:38
  88.9 3.4 %shard_map.197 = f32[4,20,128]{2,1,0:T(8,128)} custom-call(bf16[64,8,128]{2,1,0:T(8,128)(2,1)} %copy-done.5, bf16[8,128]{1,0:T(8,128)(2,1)} %get-tuple-element.133.own_ref, bf16[512,2560]{1,0:T(8,128)(2,1)} %proj_ref.1), custom_call_target="tpu_custom_call" | custom-call | flops 20971520 | bytes 2621440 | tf_op jit(solution)/shard_map/pallas_call | solution.py:405
  92.4 4.3 %all-to-all-start.3 = ((f32[4,20,128]{2,1,0:T(8,128)}), f32[4,20,128]{2,1,0:T(8,128)S(1)}, u32[]{:S(2)}, u32[]{:S(2)}) async-start(f32[4,20,128]{2,1,0:T(8,128)} %shard_map.197), calls=%async_computation.3 | async-start | bytes 98304 | tf_op jit(solution)/shard_map/all_to_all | solution.py:413
  96.7 1.4 dynamic-slice_reduce_fusion
  98.1 2.4 %shard_map.198 = (bf16[16,32,256]{2,1,0:T(8,128)(2,1)}, bf16[16,32,256]{2,1,0:T(8,128)(2,1)}, bf16[16,32,256]{2,1,0:T(8,128)(2,1)}, bf16[16,32,256]{2,1,0:T(8,12...) custom-call(bf16[16,32,256]{2,1,0:T(8,128)(2,1)} %get-tuple-element., ...), custom_call_target="tpu_custom_call" | custom-call | bytes 4194304 | tf_op jit(solution)/shard_map/pallas_call | solution.py:325
  101.7 1.8 shard_map.199
  103.5 9.5 %all-to-all-start.4 = ((bf16[64,20,128]{2,1,0:T(8,128)(2,1)}), bf16[64,20,128]{2,1,0:T(8,128)(2,1)S(1)}, u32[]{:S(2)}, u32[]{:S(2)}) async-start(bf16[64,20,128]{2,1,0:T(8,128)(2,1)} %get-tuple-element.155), calls=%async_computation.4 | async-start | bytes 786432 | tf_op jit(solution)/shard_map/all_to_all | solution.py:38
  113.0 3.3 %collective-permute-start.14 = (bf16[16,32,256]{2,1,0:T(8,128)(2,1)}, bf16[16,32,256]{2,1,0:T(8,128)(2,1)S(1)}, u32[]{:S(2)}, u32[]{:S(2)}) collective-permute-start(bf16[16,32,256]{2,1,0:T(8,128)(2,1)} %get-tuple-element.156), channel_id=1, source_target_pairs={{0,6},{1,7},{2,8},{3,9},{4,10},{5,11},{6,12},{7,13},{8,14},{9,15},... | collective-permute-start | bytes 786440 | tf_op jit(solution)/shard_map/ppermute | solution.py:352
  117.6 1.4 copy.25.gate_ref
  120.6 2.4 shard_map.200
  123.0 8.1 %all-to-all-done.4 = bf16[64,20,128]{2,1,0:T(8,128)(2,1)S(1)} async-done(((bf16[64,20,128]{2,1,0:T(8,128)(2,1)}), bf16[64,20,128]{2,1,0:T(8,128)(2,1)S(1)}, u32[]{:S(2)}, u32[]{:S(2)}) %all-to-all-start.4) | async-done | bytes 327712 | tf_op jit(solution)/shard_map/all_to_all | solution.py:38
  131.8 9.5 %collective-permute-done.14.refs_3_ = bf16[16,32,256]{2,1,0:T(8,128)(2,1)S(1)} collective-permute-done((bf16[16,32,256]{2,1,0:T(8,128)(2,1)}, bf16[16,32,256]{2,1,0:T(8,128)(2,1)S(1)}, u32[]{:S(2)}, u32[]{:S(2)}) %collective-permute-start.14) | collective-permute-done | bytes 262176 | tf_op jit(solution)/shard_map/ppermute | solution.py:352
  141.4 3.8 %shard_map.201 = bf16[64,2560]{1,0:T(8,128)(2,1)} custom-call(bf16[64,2560]{1,0:T(8,128)(2,1)} %bitcast.33, bf16[2560,160]{1,0:T(8,128)(2,1)} %copy.25.gate_ref, bf16[2560,160]{1,0:T(8,128)(2,1)} %copy.26.up_ref, bf16[160,2560]{1,0:T(8,128)(2,1)} %down_ref.1), custom_call_target="tpu_custom_call" | custom-call | flops 157286400 | bytes 2457600 | tf_op jit(solution)/shard_map/pallas_call | solution.py:439
  145.2 1.9 reshape.614
  147.1 8.8 %all-to-all-start.5 = ((bf16[64,20,128]{2,1,0:T(8,128)(2,1)}), bf16[64,20,128]{2,1,0:T(8,128)(2,1)S(1)}, u32[]{:S(2)}, u32[]{:S(2)}) async-start(bf16[64,20,128]{2,1,0:T(8,128)(2,1)} %reshape.614), calls=%async_computation.5 | async-start | bytes 786432 | tf_op jit(solution)/shard_map/all_to_all | solution.py:38
  155.9 2.4 collective-permute-start.16
  158.3 1.5 collective-permute-start.17
  159.8 5.1 %collective-permute-start.18 = (bf16[16,32,256]{2,1,0:T(8,128)(2,1)S(1)}, bf16[16,32,256]{2,1,0:T(8,128)(2,1)S(1)}, u32[]{:S(2)}, u32[]{:S(2)}) collective-permute-start(bf16[16,32,256]{2,1,0:T(8,128)(2,1)S(1)} %copy-done.35), channel_id=1, source_target_pairs={{0,8},{1,9},{2,10},{3,11},{4,12},{5,13},{6,14},{7,15},{8,0},{9,1},... | collective-permute-start | bytes 786440 | tf_op jit(solution)/shard_map/ppermute | solution.py:352
  164.9 2.8 %collective-permute-start.19 = (bf16[16,32,256]{2,1,0:T(8,128)(2,1)S(1)}, bf16[16,32,256]{2,1,0:T(8,128)(2,1)S(1)}, u32[]{:S(2)}, u32[]{:S(2)}) collective-permute-start(bf16[16,32,256]{2,1,0:T(8,128)(2,1)S(1)} %copy-done.39), channel_id=1, source_target_pairs={{0,32},{1,33},{2,34},{3,35},{4,36},{5,37},{6,38},{7,39},{8,40},{9,... | collective-permute-start | bytes 786440 | tf_op jit(solution)/shard_map/ppermute | solution.py:352
  168.2 8.7 %collective-permute-done.16.refs_2_ = bf16[16,32,256]{2,1,0:T(8,128)(2,1)S(1)} collective-permute-done((bf16[16,32,256]{2,1,0:T(8,128)(2,1)S(1)}, bf16[16,32,256]{2,1,0:T(8,128)(2,1)S(1)}, u32[]{:S(2)}, u32[]{:S(2)}) %collective-permute-start.16) | collective-permute-done | bytes 262176 | tf_op jit(solution)/shard_map/ppermute | solution.py:352
  176.9 3.3 %collective-permute-done.17.refs_6_ = bf16[16,32,256]{2,1,0:T(8,128)(2,1)S(1)} collective-permute-done((bf16[16,32,256]{2,1,0:T(8,128)(2,1)S(1)}, bf16[16,32,256]{2,1,0:T(8,128)(2,1)S(1)}, u32[]{:S(2)}, u32[]{:S(2)}) %collective-permute-start.17) | collective-permute-done | bytes 262176 | tf_op jit(solution)/shard_map/ppermute | solution.py:352
  180.2 8.4 %collective-permute-done.18.refs_4_ = bf16[16,32,256]{2,1,0:T(8,128)(2,1)S(1)} collective-permute-done((bf16[16,32,256]{2,1,0:T(8,128)(2,1)S(1)}, bf16[16,32,256]{2,1,0:T(8,128)(2,1)S(1)}, u32[]{:S(2)}, u32[]{:S(2)}) %collective-permute-start.18) | collective-permute-done | bytes 262176 | tf_op jit(solution)/shard_map/ppermute | solution.py:352
  189.4 2.0 shard_map.202
  191.4 9.9 %all-to-all-start.6 = ((bf16[64,20,128]{2,1,0:T(8,128)(2,1)}), bf16[64,20,128]{2,1,0:T(8,128)(2,1)S(1)}, u32[]{:S(2)}, u32[]{:S(2)}) async-start(bf16[64,20,128]{2,1,0:T(8,128)(2,1)} %shard_map.202), calls=%async_computation.6 | async-start | bytes 786432 | tf_op jit(solution)/shard_map/all_to_all | solution.py:38
  201.8 1.5 collective-permute-start.21
  207.4 2.9 %collective-permute-start.25 = (bf16[16,32,256]{2,1,0:T(8,128)(2,1)}, bf16[16,32,256]{2,1,0:T(8,128)(2,1)S(1)}, u32[]{:S(2)}, u32[]{:S(2)}) collective-permute-start(bf16[16,32,256]{2,1,0:T(8,128)(2,1)} %get-tuple-element.196), channel_id=1, source_target_pairs={{0,33},{1,32},{2,35},{3,34},{4,37},{5,36},{6,39},{7,38},{8,41},{9,... | collective-permute-start | bytes 786440 | tf_op jit(solution)/shard_map/ppermute | solution.py:352
  210.3 8.3 %collective-permute-done.21.refs_1_ = bf16[16,32,256]{2,1,0:T(8,128)(2,1)S(1)} collective-permute-done((bf16[16,32,256]{2,1,0:T(8,128)(2,1)S(1)}, bf16[16,32,256]{2,1,0:T(8,128)(2,1)S(1)}, u32[]{:S(2)}, u32[]{:S(2)}) %collective-permute-start.21) | collective-permute-done | bytes 262176 | tf_op jit(solution)/shard_map/ppermute | solution.py:352
  218.6 2.7 %collective-permute-start.26 = (bf16[16,32,256]{2,1,0:T(8,128)(2,1)}, bf16[16,32,256]{2,1,0:T(8,128)(2,1)S(1)}, u32[]{:S(2)}, u32[]{:S(2)}) collective-permute-start(bf16[16,32,256]{2,1,0:T(8,128)(2,1)} %get-tuple-element.197), channel_id=1, source_target_pairs={{0,48},{1,49},{2,50},{3,51},{4,52},{5,53},{6,54},{7,55},{8,56},{9,... | collective-permute-start | bytes 786440 | tf_op jit(solution)/shard_map/ppermute | solution.py:352
  221.3 1.5 collective-permute-start.27
  224.5 1.9 collective-permute-done.26.refs_14_
  226.4 6.2 %collective-permute-done.27.refs_15_ = bf16[16,32,256]{2,1,0:T(8,128)(2,1)} collective-permute-done((bf16[16,32,256]{2,1,0:T(8,128)(2,1)}, bf16[16,32,256]{2,1,0:T(8,128)(2,1)}, u32[]{:S(2)}, u32[]{:S(2)}) %collective-permute-start.27) | collective-permute-done | bytes 262176 | tf_op jit(solution)/shard_map/ppermute | solution.py:352
  232.7 4.5 %shard_map.203 = (bf16[128,32,256]{2,1,0:T(8,128)(2,1)}, bf16[128,32,256]{2,1,0:T(8,128)(2,1)}) custom-call(s32[2,64]{1,0:T(2,128)} %pad_add_fusion.place_ref, s32[64]{0:T(128)} %compare_select_fusion.8.arrive_ref, bf16[64,8,128]{2,1,0:T(8,128)(2,1)} %copy-done.2, bf16[16,32,256]{2,1,0:T(8,128)(2,1)} %get-tuple-element.183.refs_0_, ...), custom_call_target="tpu_custom_call" | custom-call | bytes 8388608 | tf_op jit(solution)/shard_map/pallas_call | solution.py:495
  (153 shorter events, 29.8 us)
Async XLA Ops:
  0.6 37.2 %copy-start.33 = (s32[64]{0:T(128)S(1)}, s32[64]{0:T(128)}, u32[]{:S(2)}) copy-start(s32[64]{0:T(128)} %param.20) | copy-start | bytes 772
  0.7 60.8 %copy-start.6 = (s32[64,512]{1,0:T(8,128)S(1)}, s32[64,512]{1,0:T(8,128)}, u32[]{:S(2)}) copy-start(s32[64,512]{1,0:T(8,128)} %param.21) | copy-start | bytes 393220
  4.3 24.6 %all-to-all-start = ((bf16[64,8,128]{2,1,0:T(8,128)(2,1)}), bf16[64,8,128]{2,1,0:T(8,128)(2,1)S(1)}, u32[]{:S(2)}, u32[]{:S(2)}) async-start(bf16[64,8,128]{2,1,0:T(8,128)(2,1)} %bitcast.10), calls=%async_computation | async-start | bytes 262144 | tf_op jit(solution)/shard_map/all_to_all | solution.py:38
  28.9 19.4 %collective-permute-start = (bf16[16,32,256]{2,1,0:T(8,128)(2,1)}, bf16[16,32,256]{2,1,0:T(8,128)(2,1)S(1)}, u32[]{:S(2)}, u32[]{:S(2)}) collective-permute-start(bf16[16,32,256]{2,1,0:T(8,128)(2,1)} %get-tuple-element.120), channel_id=1, source_target_pairs={{0,8},{1,9},{2,10},{3,11},{4,12},{5,13},{6,14},{7,15},{8,0},{9,1},... | collective-permute-start | bytes 786440 | tf_op jit(solution)/shard_map/ppermute | solution.py:352
  34.3 18.3 %collective-permute-start.1 = (bf16[16,32,256]{2,1,0:T(8,128)(2,1)}, bf16[16,32,256]{2,1,0:T(8,128)(2,1)S(1)}, u32[]{:S(2)}, u32[]{:S(2)}) collective-permute-start(bf16[16,32,256]{2,1,0:T(8,128)(2,1)} %get-tuple-element.121), channel_id=1, source_target_pairs={{0,2},{1,3},{2,4},{3,5},{4,6},{5,7},{6,8},{7,9},{8,10},{9,11},{10,... | collective-permute-start | bytes 786440 | tf_op jit(solution)/shard_map/ppermute | solution.py:352
  34.6 18.7 %collective-permute-start.2 = (bf16[16,32,256]{2,1,0:T(8,128)(2,1)}, bf16[16,32,256]{2,1,0:T(8,128)(2,1)S(1)}, u32[]{:S(2)}, u32[]{:S(2)}) collective-permute-start(bf16[16,32,256]{2,1,0:T(8,128)(2,1)} %get-tuple-element.122), channel_id=1, source_target_pairs={{0,32},{1,33},{2,34},{3,35},{4,36},{5,37},{6,38},{7,39},{8,40},{9,... | collective-permute-start | bytes 786440 | tf_op jit(solution)/shard_map/ppermute | solution.py:352
  37.4 19.6 %collective-permute-start.3 = (bf16[16,32,256]{2,1,0:T(8,128)(2,1)}, bf16[16,32,256]{2,1,0:T(8,128)(2,1)S(1)}, u32[]{:S(2)}, u32[]{:S(2)}) collective-permute-start(bf16[16,32,256]{2,1,0:T(8,128)(2,1)} %get-tuple-element.123), channel_id=1, source_target_pairs={{0,16},{1,17},{2,18},{3,19},{4,20},{5,21},{6,22},{7,23},{8,24},{9,... | collective-permute-start | bytes 786440 | tf_op jit(solution)/shard_map/ppermute | solution.py:352
  37.9 25.4 %collective-permute-start.4 = (bf16[16,32,256]{2,1,0:T(8,128)(2,1)}, bf16[16,32,256]{2,1,0:T(8,128)(2,1)S(1)}, u32[]{:S(2)}, u32[]{:S(2)}) collective-permute-start(bf16[16,32,256]{2,1,0:T(8,128)(2,1)} %get-tuple-element.124), channel_id=1, source_target_pairs={{0,48},{1,49},{2,50},{3,51},{4,52},{5,53},{6,54},{7,55},{8,56},{9,... | collective-permute-start | bytes 786440 | tf_op jit(solution)/shard_map/ppermute | solution.py:352
  42.0 21.3 %all-to-all-start.1 = ((bf16[64,8,128]{2,1,0:T(8,128)(2,1)}), bf16[64,8,128]{2,1,0:T(8,128)(2,1)S(1)}, u32[]{:S(2)}, u32[]{:S(2)}) async-start(bf16[64,8,128]{2,1,0:T(8,128)(2,1)} %get-tuple-element.119), calls=%async_computation.1 | async-start | bytes 262144 | tf_op jit(solution)/shard_map/all_to_all | solution.py:38
  48.3 44.0 %copy-start.21 = (bf16[16,32,256]{2,1,0:T(8,128)(2,1)}, bf16[16,32,256]{2,1,0:T(8,128)(2,1)S(1)}, u32[]{:S(2)}) copy-start(bf16[16,32,256]{2,1,0:T(8,128)(2,1)S(1)} %collective-permute-done.refs_4_) | copy-start | bytes 786436
  48.3 15.8 %collective-permute-start.10 = (bf16[16,32,256]{2,1,0:T(8,128)(2,1)}, bf16[16,32,256]{2,1,0:T(8,128)(2,1)S(1)}, u32[]{:S(2)}, u32[]{:S(2)}) collective-permute-start(bf16[16,32,256]{2,1,0:T(8,128)(2,1)} %get-tuple-element.131), channel_id=1, source_target_pairs={{0,1},{1,0},{2,3},{3,2},{4,5},{5,4},{6,7},{7,6},{8,9},{9,8},{10,11... | collective-permute-start | bytes 786440 | tf_op jit(solution)/shard_map/ppermute | solution.py:352
  52.6 39.7 %copy-start.22 = (bf16[16,32,256]{2,1,0:T(8,128)(2,1)}, bf16[16,32,256]{2,1,0:T(8,128)(2,1)S(1)}, u32[]{:S(2)}) copy-start(bf16[16,32,256]{2,1,0:T(8,128)(2,1)S(1)} %collective-permute-done.1.refs_1_) | copy-start | bytes 786436
  52.6 25.3 %collective-permute-start.5 = (bf16[16,32,256]{2,1,0:T(8,128)(2,1)}, bf16[16,32,256]{2,1,0:T(8,128)(2,1)S(1)}, u32[]{:S(2)}, u32[]{:S(2)}) collective-permute-start(bf16[16,32,256]{2,1,0:T(8,128)(2,1)} %get-tuple-element.126), channel_id=1, source_target_pairs={{0,6},{1,7},{2,8},{3,9},{4,10},{5,11},{6,12},{7,13},{8,14},{9,15},... | collective-permute-start | bytes 786440 | tf_op jit(solution)/shard_map/ppermute | solution.py:352
  53.3 39.0 %copy-start.25 = (bf16[16,32,256]{2,1,0:T(8,128)(2,1)}, bf16[16,32,256]{2,1,0:T(8,128)(2,1)S(1)}, u32[]{:S(2)}) copy-start(bf16[16,32,256]{2,1,0:T(8,128)(2,1)S(1)} %collective-permute-done.2.refs_4_) | copy-start | bytes 786436
  53.3 26.9 %collective-permute-start.6 = (bf16[16,32,256]{2,1,0:T(8,128)(2,1)}, bf16[16,32,256]{2,1,0:T(8,128)(2,1)S(1)}, u32[]{:S(2)}, u32[]{:S(2)}) collective-permute-start(bf16[16,32,256]{2,1,0:T(8,128)(2,1)} %get-tuple-element.127), channel_id=1, source_target_pairs={{0,10},{1,11},{2,12},{3,13},{4,14},{5,15},{6,0},{7,1},{8,2},{9,3},... | collective-permute-start | bytes 786440 | tf_op jit(solution)/shard_map/ppermute | solution.py:352
  57.1 35.3 %copy-start.26 = (bf16[16,32,256]{2,1,0:T(8,128)(2,1)}, bf16[16,32,256]{2,1,0:T(8,128)(2,1)S(1)}, u32[]{:S(2)}) copy-start(bf16[16,32,256]{2,1,0:T(8,128)(2,1)S(1)} %collective-permute-done.3.refs_2_) | copy-start | bytes 786436
  57.1 24.5 %collective-permute-start.7 = (bf16[16,32,256]{2,1,0:T(8,128)(2,1)}, bf16[16,32,256]{2,1,0:T(8,128)(2,1)S(1)}, u32[]{:S(2)}, u32[]{:S(2)}) collective-permute-start(bf16[16,32,256]{2,1,0:T(8,128)(2,1)} %get-tuple-element.128), channel_id=1, source_target_pairs={{0,33},{1,32},{2,35},{3,34},{4,37},{5,36},{6,39},{7,38},{8,41},{9,... | collective-permute-start | bytes 786440 | tf_op jit(solution)/shard_map/ppermute | solution.py:352
  63.4 19.6 %collective-permute-start.8 = (bf16[16,32,256]{2,1,0:T(8,128)(2,1)}, bf16[16,32,256]{2,1,0:T(8,128)(2,1)S(1)}, u32[]{:S(2)}, u32[]{:S(2)}) collective-permute-start(bf16[16,32,256]{2,1,0:T(8,128)(2,1)} %get-tuple-element.129), channel_id=1, source_target_pairs={{0,17},{1,16},{2,19},{3,18},{4,21},{5,20},{6,23},{7,22},{8,25},{9,... | collective-permute-start | bytes 786440 | tf_op jit(solution)/shard_map/ppermute | solution.py:352
  64.2 18.8 %collective-permute-start.9 = (bf16[16,32,256]{2,1,0:T(8,128)(2,1)}, bf16[16,32,256]{2,1,0:T(8,128)(2,1)}, u32[]{:S(2)}, u32[]{:S(2)}) collective-permute-start(bf16[16,32,256]{2,1,0:T(8,128)(2,1)} %get-tuple-element.130), channel_id=1, source_target_pairs={{0,49},{1,48},{2,51},{3,50},{4,53},{5,52},{6,55},{7,54},{8,57},{9,... | collective-permute-start | bytes 786440 | tf_op jit(solution)/shard_map/ppermute | solution.py:352
  72.7 15.6 %all-to-all-start.2 = ((bf16[64,8,128]{2,1,0:T(8,128)(2,1)}), bf16[64,8,128]{2,1,0:T(8,128)(2,1)S(1)}, u32[]{:S(2)}, u32[]{:S(2)}) async-start(bf16[64,8,128]{2,1,0:T(8,128)(2,1)} %bitcast.14), calls=%async_computation.2 | async-start | bytes 262144 | tf_op jit(solution)/shard_map/all_to_all | solution.py:38
  77.9 22.6 %collective-permute-start.11 = (bf16[16,32,256]{2,1,0:T(8,128)(2,1)}, bf16[16,32,256]{2,1,0:T(8,128)(2,1)}, u32[]{:S(2)}, u32[]{:S(2)}) collective-permute-start(bf16[16,32,256]{2,1,0:T(8,128)(2,1)} %get-tuple-element.134), channel_id=1, source_target_pairs={{0,4},{1,5},{2,6},{3,7},{4,8},{5,9},{6,10},{7,11},{8,12},{9,13},{1... | collective-permute-start | bytes 786440 | tf_op jit(solution)/shard_map/ppermute | solution.py:352
  80.3 20.3 %collective-permute-start.12 = (bf16[16,32,256]{2,1,0:T(8,128)(2,1)}, bf16[16,32,256]{2,1,0:T(8,128)(2,1)}, u32[]{:S(2)}, u32[]{:S(2)}) collective-permute-start(bf16[16,32,256]{2,1,0:T(8,128)(2,1)} %get-tuple-element.135), channel_id=1, source_target_pairs={{0,12},{1,13},{2,14},{3,15},{4,0},{5,1},{6,2},{7,3},{8,4},{9,5},{1... | collective-permute-start | bytes 786440 | tf_op jit(solution)/shard_map/ppermute | solution.py:352
  81.6 19.0 %collective-permute-start.13 = (bf16[16,32,256]{2,1,0:T(8,128)(2,1)}, bf16[16,32,256]{2,1,0:T(8,128)(2,1)}, u32[]{:S(2)}, u32[]{:S(2)}) collective-permute-start(bf16[16,32,256]{2,1,0:T(8,128)(2,1)} %get-tuple-element.136), channel_id=1, source_target_pairs={{0,14},{1,15},{2,0},{3,1},{4,2},{5,3},{6,4},{7,5},{8,6},{9,7},{10,... | collective-permute-start | bytes 786440 | tf_op jit(solution)/shard_map/ppermute | solution.py:352
  92.4 8.7 %all-to-all-start.3 = ((f32[4,20,128]{2,1,0:T(8,128)}), f32[4,20,128]{2,1,0:T(8,128)S(1)}, u32[]{:S(2)}, u32[]{:S(2)}) async-start(f32[4,20,128]{2,1,0:T(8,128)} %shard_map.197), calls=%async_computation.3 | async-start | bytes 98304 | tf_op jit(solution)/shard_map/all_to_all | solution.py:413
  103.5 27.5 %all-to-all-start.4 = ((bf16[64,20,128]{2,1,0:T(8,128)(2,1)}), bf16[64,20,128]{2,1,0:T(8,128)(2,1)S(1)}, u32[]{:S(2)}, u32[]{:S(2)}) async-start(bf16[64,20,128]{2,1,0:T(8,128)(2,1)} %get-tuple-element.155), calls=%async_computation.4 | async-start | bytes 786432 | tf_op jit(solution)/shard_map/all_to_all | solution.py:38
  113.0 28.2 %collective-permute-start.14 = (bf16[16,32,256]{2,1,0:T(8,128)(2,1)}, bf16[16,32,256]{2,1,0:T(8,128)(2,1)S(1)}, u32[]{:S(2)}, u32[]{:S(2)}) collective-permute-start(bf16[16,32,256]{2,1,0:T(8,128)(2,1)} %get-tuple-element.156), channel_id=1, source_target_pairs={{0,6},{1,7},{2,8},{3,9},{4,10},{5,11},{6,12},{7,13},{8,14},{9,15},... | collective-permute-start | bytes 786440 | tf_op jit(solution)/shard_map/ppermute | solution.py:352
  116.3 25.0 %collective-permute-start.15 = (bf16[16,32,256]{2,1,0:T(8,128)(2,1)}, bf16[16,32,256]{2,1,0:T(8,128)(2,1)S(1)}, u32[]{:S(2)}, u32[]{:S(2)}) collective-permute-start(bf16[16,32,256]{2,1,0:T(8,128)(2,1)} %get-tuple-element.157), channel_id=1, source_target_pairs={{0,10},{1,11},{2,12},{3,13},{4,14},{5,15},{6,0},{7,1},{8,2},{9,3},... | collective-permute-start | bytes 786440 | tf_op jit(solution)/shard_map/ppermute | solution.py:352
  141.3 60.0 %copy-start.32 = (s32[4096,1]{0,1:T(1,128)S(1)}, s32[4096,1]{0,1:T(1,128)}, u32[]{:S(2)}) copy-start(s32[4096,1]{0,1:T(1,128)} %param.22) | copy-start | bytes 49156
  141.4 60.5 %copy-start.34 = (bf16[16,32,256]{2,1,0:T(8,128)(2,1)S(1)}, bf16[16,32,256]{2,1,0:T(8,128)(2,1)}, u32[]{:S(2)}) copy-start(bf16[16,32,256]{2,1,0:T(8,128)(2,1)} %get-tuple-element.184) | copy-start | bytes 786436
  147.1 41.5 %all-to-all-start.5 = ((bf16[64,20,128]{2,1,0:T(8,128)(2,1)}), bf16[64,20,128]{2,1,0:T(8,128)(2,1)S(1)}, u32[]{:S(2)}, u32[]{:S(2)}) async-start(bf16[64,20,128]{2,1,0:T(8,128)(2,1)} %reshape.614), calls=%async_computation.5 | async-start | bytes 786432 | tf_op jit(solution)/shard_map/all_to_all | solution.py:38
  155.9 21.0 %collective-permute-start.16 = (bf16[16,32,256]{2,1,0:T(8,128)(2,1)S(1)}, bf16[16,32,256]{2,1,0:T(8,128)(2,1)S(1)}, u32[]{:S(2)}, u32[]{:S(2)}) collective-permute-start(bf16[16,32,256]{2,1,0:T(8,128)(2,1)S(1)} %copy-done.37), channel_id=1, source_target_pairs={{0,4},{1,5},{2,6},{3,7},{4,8},{5,9},{6,10},{7,11},{8,12},{9,13},{1... | collective-permute-start | bytes 786440 | tf_op jit(solution)/shard_map/ppermute | solution.py:352
  158.3 21.9 %collective-permute-start.17 = (bf16[16,32,256]{2,1,0:T(8,128)(2,1)S(1)}, bf16[16,32,256]{2,1,0:T(8,128)(2,1)S(1)}, u32[]{:S(2)}, u32[]{:S(2)}) collective-permute-start(bf16[16,32,256]{2,1,0:T(8,128)(2,1)S(1)} %copy-done.36), channel_id=1, source_target_pairs={{0,12},{1,13},{2,14},{3,15},{4,0},{5,1},{6,2},{7,3},{8,4},{9,5},{1... | collective-permute-start | bytes 786440 | tf_op jit(solution)/shard_map/ppermute | solution.py:352
  159.8 28.8 %collective-permute-start.18 = (bf16[16,32,256]{2,1,0:T(8,128)(2,1)S(1)}, bf16[16,32,256]{2,1,0:T(8,128)(2,1)S(1)}, u32[]{:S(2)}, u32[]{:S(2)}) collective-permute-start(bf16[16,32,256]{2,1,0:T(8,128)(2,1)S(1)} %copy-done.35), channel_id=1, source_target_pairs={{0,8},{1,9},{2,10},{3,11},{4,12},{5,13},{6,14},{7,15},{8,0},{9,1},... | collective-permute-start | bytes 786440 | tf_op jit(solution)/shard_map/ppermute | solution.py:352
  164.9 23.7 %collective-permute-start.19 = (bf16[16,32,256]{2,1,0:T(8,128)(2,1)S(1)}, bf16[16,32,256]{2,1,0:T(8,128)(2,1)S(1)}, u32[]{:S(2)}, u32[]{:S(2)}) collective-permute-start(bf16[16,32,256]{2,1,0:T(8,128)(2,1)S(1)} %copy-done.39), channel_id=1, source_target_pairs={{0,32},{1,33},{2,34},{3,35},{4,36},{5,37},{6,38},{7,39},{8,40},{9,... | collective-permute-start | bytes 786440 | tf_op jit(solution)/shard_map/ppermute | solution.py:352
  167.7 20.9 %collective-permute-start.20 = (bf16[16,32,256]{2,1,0:T(8,128)(2,1)S(1)}, bf16[16,32,256]{2,1,0:T(8,128)(2,1)S(1)}, u32[]{:S(2)}, u32[]{:S(2)}) collective-permute-start(bf16[16,32,256]{2,1,0:T(8,128)(2,1)S(1)} %copy-done.38), channel_id=1, source_target_pairs={{0,16},{1,17},{2,18},{3,19},{4,20},{5,21},{6,22},{7,23},{8,24},{9,... | collective-permute-start | bytes 786440 | tf_op jit(solution)/shard_map/ppermute | solution.py:352
  176.9 55.7 %copy-start.10 = (bf16[16,32,256]{2,1,0:T(8,128)(2,1)}, bf16[16,32,256]{2,1,0:T(8,128)(2,1)S(1)}, u32[]{:S(2)}) copy-start(bf16[16,32,256]{2,1,0:T(8,128)(2,1)S(1)} %collective-permute-done.16.refs_2_) | copy-start | bytes 786436
  180.2 52.4 %copy-start.11 = (bf16[16,32,256]{2,1,0:T(8,128)(2,1)}, bf16[16,32,256]{2,1,0:T(8,128)(2,1)S(1)}, u32[]{:S(2)}) copy-start(bf16[16,32,256]{2,1,0:T(8,128)(2,1)S(1)} %collective-permute-done.17.refs_6_) | copy-start | bytes 786436
  188.6 44.0 %copy-start.12 = (bf16[16,32,256]{2,1,0:T(8,128)(2,1)}, bf16[16,32,256]{2,1,0:T(8,128)(2,1)S(1)}, u32[]{:S(2)}) copy-start(bf16[16,32,256]{2,1,0:T(8,128)(2,1)S(1)} %collective-permute-done.18.refs_4_) | copy-start | bytes 786436
  188.6 44.0 %copy-start.13 = (bf16[16,32,256]{2,1,0:T(8,128)(2,1)}, bf16[16,32,256]{2,1,0:T(8,128)(2,1)S(1)}, u32[]{:S(2)}) copy-start(bf16[16,32,256]{2,1,0:T(8,128)(2,1)S(1)} %collective-permute-done.19.refs_12_) | copy-start | bytes 786436
  188.6 44.0 %copy-start.14 = (bf16[16,32,256]{2,1,0:T(8,128)(2,1)}, bf16[16,32,256]{2,1,0:T(8,128)(2,1)S(1)}, u32[]{:S(2)}) copy-start(bf16[16,32,256]{2,1,0:T(8,128)(2,1)S(1)} %collective-permute-done.20.refs_10_) | copy-start | bytes 786436
  191.4 45.7 %all-to-all-start.6 = ((bf16[64,20,128]{2,1,0:T(8,128)(2,1)}), bf16[64,20,128]{2,1,0:T(8,128)(2,1)S(1)}, u32[]{:S(2)}, u32[]{:S(2)}) async-start(bf16[64,20,128]{2,1,0:T(8,128)(2,1)} %shard_map.202), calls=%async_computation.6 | async-start | bytes 786432 | tf_op jit(solution)/shard_map/all_to_all | solution.py:38
  201.8 16.8 %collective-permute-start.21 = (bf16[16,32,256]{2,1,0:T(8,128)(2,1)S(1)}, bf16[16,32,256]{2,1,0:T(8,128)(2,1)S(1)}, u32[]{:S(2)}, u32[]{:S(2)}) collective-permute-start(bf16[16,32,256]{2,1,0:T(8,128)(2,1)S(1)} %copy-done.34), channel_id=1, source_target_pairs={{0,2},{1,3},{2,4},{3,5},{4,6},{5,7},{6,8},{7,9},{8,10},{9,11},{10,... | collective-permute-start | bytes 786440 | tf_op jit(solution)/shard_map/ppermute | solution.py:352
  203.3 18.0 %collective-permute-start.22 = (bf16[16,32,256]{2,1,0:T(8,128)(2,1)}, bf16[16,32,256]{2,1,0:T(8,128)(2,1)S(1)}, u32[]{:S(2)}, u32[]{:S(2)}) collective-permute-start(bf16[16,32,256]{2,1,0:T(8,128)(2,1)} %get-tuple-element.190), channel_id=1, source_target_pairs={{0,14},{1,15},{2,0},{3,1},{4,2},{5,3},{6,4},{7,5},{8,6},{9,7},{10,... | collective-permute-start | bytes 786440 | tf_op jit(solution)/shard_map/ppermute | solution.py:352
  205.1 18.9 %collective-permute-start.23 = (bf16[16,32,256]{2,1,0:T(8,128)(2,1)}, bf16[16,32,256]{2,1,0:T(8,128)(2,1)S(1)}, u32[]{:S(2)}, u32[]{:S(2)}) collective-permute-start(bf16[16,32,256]{2,1,0:T(8,128)(2,1)} %get-tuple-element.192), channel_id=1, source_target_pairs={{0,1},{1,0},{2,3},{3,2},{4,5},{5,4},{6,7},{7,6},{8,9},{9,8},{10,11... | collective-permute-start | bytes 786440 | tf_op jit(solution)/shard_map/ppermute | solution.py:352
  206.2 17.8 %collective-permute-start.24 = (bf16[16,32,256]{2,1,0:T(8,128)(2,1)}, bf16[16,32,256]{2,1,0:T(8,128)(2,1)S(1)}, u32[]{:S(2)}, u32[]{:S(2)}) collective-permute-start(bf16[16,32,256]{2,1,0:T(8,128)(2,1)} %get-tuple-element.194), channel_id=1, source_target_pairs={{0,17},{1,16},{2,19},{3,18},{4,21},{5,20},{6,23},{7,22},{8,25},{9,... | collective-permute-start | bytes 786440 | tf_op jit(solution)/shard_map/ppermute | solution.py:352
  207.4 17.1 %collective-permute-start.25 = (bf16[16,32,256]{2,1,0:T(8,128)(2,1)}, bf16[16,32,256]{2,1,0:T(8,128)(2,1)S(1)}, u32[]{:S(2)}, u32[]{:S(2)}) collective-permute-start(bf16[16,32,256]{2,1,0:T(8,128)(2,1)} %get-tuple-element.196), channel_id=1, source_target_pairs={{0,33},{1,32},{2,35},{3,34},{4,37},{5,36},{6,39},{7,38},{8,41},{9,... | collective-permute-start | bytes 786440 | tf_op jit(solution)/shard_map/ppermute | solution.py:352
  218.6 7.8 %collective-permute-start.26 = (bf16[16,32,256]{2,1,0:T(8,128)(2,1)}, bf16[16,32,256]{2,1,0:T(8,128)(2,1)S(1)}, u32[]{:S(2)}, u32[]{:S(2)}) collective-permute-start(bf16[16,32,256]{2,1,0:T(8,128)(2,1)} %get-tuple-element.197), channel_id=1, source_target_pairs={{0,48},{1,49},{2,50},{3,51},{4,52},{5,53},{6,54},{7,55},{8,56},{9,... | collective-permute-start | bytes 786440 | tf_op jit(solution)/shard_map/ppermute | solution.py:352
  221.3 11.3 %collective-permute-start.27 = (bf16[16,32,256]{2,1,0:T(8,128)(2,1)}, bf16[16,32,256]{2,1,0:T(8,128)(2,1)}, u32[]{:S(2)}, u32[]{:S(2)}) collective-permute-start(bf16[16,32,256]{2,1,0:T(8,128)(2,1)} %get-tuple-element.198), channel_id=1, source_target_pairs={{0,49},{1,48},{2,51},{3,50},{4,53},{5,52},{6,55},{7,54},{8,57},{9,... | collective-permute-start | bytes 786440 | tf_op jit(solution)/shard_map/ppermute | solution.py:352
  (27 other events, 336.5 us)

commit v4 on v3

--- a/solution.py
+++ b/solution.py
@@ -15,6 +15,7 @@
 LANES = 128
 BF16 = jnp.bfloat16
 F32 = jnp.float32
+PARAMS = pltpu.CompilerParams(vmem_limit_bytes=16 << 20)
 
 
 def call(body, out_shape, n_in, flops, bytes_accessed):
@@ -27,6 +28,7 @@
         cost_estimate=pl.CostEstimate(
             flops=flops, bytes_accessed=bytes_accessed, transcendentals=0
         ),
+        compiler_params=PARAMS,
     )
 
 
@@ -154,8 +156,9 @@
 
 def ffw_body(x_ref, gate_ref, up_ref, down_ref, out_ref):
     x = x_ref[...]
-    gate = jnp.dot(x, gate_ref[...], preferred_element_type=F32)
-    up = jnp.dot(x, up_ref[...], preferred_element_type=F32)
+    across = (((1,), (1,)), ((), ()))
+    gate = lax.dot_general(x, gate_ref[...], across, preferred_element_type=F32)
+    up = lax.dot_general(x, up_ref[...], across, preferred_element_type=F32)
     units = (jax.nn.gelu(gate, approximate=True) * up).astype(BF16)
     out_ref[...] = jnp.dot(units, down_ref[...], preferred_element_type=F32).astype(BF16)
 
@@ -319,6 +322,7 @@
             cost_estimate=pl.CostEstimate(
                 flops=0, bytes_accessed=6 * slots * page * head, transcendentals=0
             ),
+compiler_params=PARAMS,
         )(source_of, pages)
 
     def regroup(chunks, count):
@@ -335,6 +339,7 @@
             cost_estimate=pl.CostEstimate(
                 flops=0, bytes_accessed=8 * slots * page * head, transcendentals=0
             ),
+compiler_params=PARAMS,
         )(*chunks)
 
     dest = lax.dynamic_slice_in_dim(move_dest[:, 0], device * slots, slots)
@@ -359,9 +364,6 @@
             for k in steps:
                 moves[k] = next(rest)
         return done[0]
-
-    keys_first = permutes(keys_sends, to_near)
-    values_first = permutes(values_sends, to_along)
 
     frequency = jnp.exp(-(2.0 * jnp.arange(head // 2, dtype=F32) / head) * ROPE_LOG)
     position = lax.dynamic_slice_in_dim(positions, device, 1).astype(F32)
@@ -383,6 +385,9 @@
         query_norm_gain.reshape(tile),
         key_gain.reshape(tile),
     )
+    every, *sends = tie(every, *keys_sends, *values_sends)
+    keys_first = permutes(sends[:near], to_near)
+    values_first = permutes(sends[near:], to_along)
     every = exchange(every)
     every = due(every, (values_first, (4, 1)), (keys_first, (4, 2, 6)))
 
@@ -432,7 +437,7 @@
         ffw_gain.reshape(wide),
     )
     ffw_in = exchange(ffw_in).reshape(requests, model)
-    ffw_in = due(ffw_in, (keys_second, (3, 5)))
+    ffw_in = due(ffw_in, (keys_second, (2, 6)))
     ffw_in, values_sends = tie(ffw_in, values_sends)
     values_second = permutes(values_sends, to_near)
     units = gate_weight.shape[1]
@@ -442,9 +447,9 @@
         4,
         6 * requests * units * model,
         6 * units * model,
-    )(ffw_in, gate_weight, up_weight, down_weight)
+    )(ffw_in, gate_weight.T, up_weight.T, down_weight)
     ffw_terms = exchange(ffw_terms.reshape((requests,) + wide))
-    ffw_terms = due(ffw_terms, (keys_second, (2, 6, 4)), (values_second, (4, 2)))
+    ffw_terms = due(ffw_terms, (keys_second, (3, 5)), (values_second, (4, 2, 6)))
     out_rows = call(
         output_body,
         jax.ShapeDtypeStruct((requests,) + wide, BF16),
@@ -505,6 +510,7 @@
         cost_estimate=pl.CostEstimate(
             flops=0, bytes_accessed=16 * slots * page * head, transcendentals=0
         ),
+compiler_params=PARAMS,
     )(place, arrive, every, *keys_second, *values_second)
     return (out_hidden, relocated_keys, relocated_values)
 

time: 240 us -> 238 us (level)
  local copies, waits for them, and re-layouts: 15.9 us -> 36.9 us
  waiting for transfers between devices: 64.4 us -> 50.8 us
  Pallas kernels: 32.2 us -> 25.3 us
    unnamed x87 -> x123, local copies, waits for them, and re-layouts: 9.66 us -> 32.2 us
    all_to_all x6, waiting for transfers between devices: 13.4 us -> 5.41 us  [exchange(): return lax.all_to_all(x, 'blk', split_axis=0, concat_axis=0, tiled=True)]
    pallas_call x1, Pallas kernels: 4.46 us -> 9.58 us  [local(): pl.pallas_call(functools.partial(assemble_body, (depth, near), capacity),...]
    ppermute x28, waiting for transfers between devices: 50.5 us -> 45.4 us  [permutes(): lax.ppermute(sends[k], 'blk', targets[k])]
    all_to_all x6, starting transfers between devices: 52.6 us -> 48.9 us  [exchange(): return lax.all_to_all(x, 'blk', split_axis=0, concat_axis=0, tiled=True)]
    pallas_call x1, Pallas kernels: 3.81 us -> 0.91 us  [local(): call(ffw_body, jax.ShapeDtypeStruct((requests, model), BF16), 4, 6 * requ...]
  transfers between devices with their start and end apart: 35 -> 35, of which waited for: 12 -> 8; matrix products, arithmetic and copies ran while one was open for 7% -> 4% of each run, Pallas kernels for 10% -> 9%
where the time goes in v4:
time: 238 us; the launch traced here: 235 us
  starting transfers between devices  113 us (47%)
  waiting for transfers between devices  50.8 us (21%)
  local copies, waits for them, and re-layouts  36.9 us (16%)
  Pallas kernels  25.3 us (11%)
  other arithmetic  6.33 us (3%)
    ppermute x28, starting transfers between devices, permutes(): lax.ppermute(sends[k], 'blk', targets[k])  59.9 us
    all_to_all x6, starting transfers between devices, exchange(): return lax.all_to_all(x, 'blk', split_axis=0, concat_axis=0, tiled=True)  48.9 us
    ppermute x28, waiting for transfers between devices, permutes(): lax.ppermute(sends[k], 'blk', targets[k])  45.4 us
    unnamed x123, local copies, waits for them, and re-layouts  32.2 us
    pallas_call x1, Pallas kernels, local(): pl.pallas_call(functools.partial(assemble_body, (depth, near), capacity),...  9.58 us
    all_to_all x6, waiting for transfers between devices, exchange(): return lax.all_to_all(x, 'blk', split_axis=0, concat_axis=0, tiled=True)  5.41 us
    pallas_call x2, Pallas kernels, regroup(): pl.pallas_call(functools.partial(regroup_body, len(chunks)), out_shape=bu...  4.87 us
  transfers between devices with their start and end apart: 35, of which 8 were waited for; matrix products, arithmetic and copies ran while one was open for 4% of the time, Pallas kernels for 9%

profile of v4, /device:TPU:1, one launch (start us, length us, event | category | flops | bytes accessed | tf_op | source)
XLA Modules:
  0.0 235.2 jit_solution(12833721063996057920)
XLA Ops:
  0.7 1.2 multiply_reduce_fusion
  4.4 13.0 %all-to-all-start = ((bf16[64,8,128]{2,1,0:T(8,128)(2,1)}), bf16[64,8,128]{2,1,0:T(8,128)(2,1)S(1)}, u32[]{:S(2)}, u32[]{:S(2)}) async-start(bf16[64,8,128]{2,1,0:T(8,128)(2,1)} %bitcast.12), calls=%async_computation | async-start | bytes 262144 | tf_op jit(solution)/shard_map/all_to_all | solution.py:40
  19.3 1.2 dynamic_slice.21
  21.2 1.2 copy-done.1
  22.4 2.0 shard_map.193
  27.3 1.2 copy-done.3
  28.5 1.8 shard_map.194
  34.2 5.3 %collective-permute-start = (bf16[16,32,256]{2,1,0:T(8,128)(2,1)}, bf16[16,32,256]{2,1,0:T(8,128)(2,1)S(1)}, u32[]{:S(2)}, u32[]{:S(2)}) collective-permute-start(bf16[16,32,256]{2,1,0:T(8,128)(2,1)} %get-tuple-element.154), channel_id=1, source_target_pairs={{0,8},{1,9},{2,10},{3,11},{4,12},{5,13},{6,14},{7,15},{8,0},{9,1},... | collective-permute-start | bytes 786440 | tf_op jit(solution)/shard_map/ppermute | solution.py:357
  39.7 2.9 %collective-permute-start.2 = (bf16[16,32,256]{2,1,0:T(8,128)(2,1)}, bf16[16,32,256]{2,1,0:T(8,128)(2,1)S(1)}, u32[]{:S(2)}, u32[]{:S(2)}) collective-permute-start(bf16[16,32,256]{2,1,0:T(8,128)(2,1)} %get-tuple-element.156), channel_id=1, source_target_pairs={{0,32},{1,33},{2,34},{3,35},{4,36},{5,37},{6,38},{7,39},{8,40},{9,... | collective-permute-start | bytes 786440 | tf_op jit(solution)/shard_map/ppermute | solution.py:357
  43.7 2.3 collective-permute-start.4
  46.0 6.3 %all-to-all-start.1 = ((bf16[64,8,128]{2,1,0:T(8,128)(2,1)}), bf16[64,8,128]{2,1,0:T(8,128)(2,1)S(1)}, u32[]{:S(2)}, u32[]{:S(2)}) async-start(bf16[64,8,128]{2,1,0:T(8,128)(2,1)} %get-tuple-element.153), calls=%async_computation.1 | async-start | bytes 262144 | tf_op jit(solution)/shard_map/all_to_all | solution.py:40
  52.8 4.9 %collective-permute-done.1.refs_1_ = bf16[16,32,256]{2,1,0:T(8,128)(2,1)S(1)} collective-permute-done((bf16[16,32,256]{2,1,0:T(8,128)(2,1)S(1)}, bf16[16,32,256]{2,1,0:T(8,128)(2,1)S(1)}, u32[]{:S(2)}, u32[]{:S(2)}) %collective-permute-start.1) | collective-permute-done | bytes 262176 | tf_op jit(solution)/shard_map/ppermute | solution.py:357
  59.2 3.7 %collective-permute-start.6 = (bf16[16,32,256]{2,1,0:T(8,128)(2,1)}, bf16[16,32,256]{2,1,0:T(8,128)(2,1)S(1)}, u32[]{:S(2)}, u32[]{:S(2)}) collective-permute-start(bf16[16,32,256]{2,1,0:T(8,128)(2,1)} %copy-done.48), channel_id=1, source_target_pairs={{0,10},{1,11},{2,12},{3,13},{4,14},{5,15},{6,0},{7,1},{8,2},{9,3},... | collective-permute-start | bytes 786440 | tf_op jit(solution)/shard_map/ppermute | solution.py:357
  62.9 4.0 %collective-permute-start.7 = (bf16[16,32,256]{2,1,0:T(8,128)(2,1)}, bf16[16,32,256]{2,1,0:T(8,128)(2,1)}, u32[]{:S(2)}, u32[]{:S(2)}) collective-permute-start(bf16[16,32,256]{2,1,0:T(8,128)(2,1)} %copy-done.46), channel_id=1, source_target_pairs={{0,33},{1,32},{2,35},{3,34},{4,37},{5,36},{6,39},{7,38},{8,41},{9,... | collective-permute-start | bytes 786440 | tf_op jit(solution)/shard_map/ppermute | solution.py:357
  67.0 2.1 select_reduce_fusion
  69.3 3.2 %collective-permute-start.9 = (bf16[16,32,256]{2,1,0:T(8,128)(2,1)}, bf16[16,32,256]{2,1,0:T(8,128)(2,1)}, u32[]{:S(2)}, u32[]{:S(2)}) collective-permute-start(bf16[16,32,256]{2,1,0:T(8,128)(2,1)} %copy-done.44), channel_id=1, source_target_pairs={{0,49},{1,48},{2,51},{3,50},{4,53},{5,52},{6,55},{7,54},{8,57},{9,... | collective-permute-start | bytes 786440 | tf_op jit(solution)/shard_map/ppermute | solution.py:357
  72.5 1.8 shard_map.196
  75.0 5.5 %all-to-all-start.2 = ((bf16[64,8,128]{2,1,0:T(8,128)(2,1)}), bf16[64,8,128]{2,1,0:T(8,128)(2,1)S(1)}, u32[]{:S(2)}, u32[]{:S(2)}) async-start(bf16[64,8,128]{2,1,0:T(8,128)(2,1)} %bitcast.16), calls=%async_computation.2 | async-start | bytes 262144 | tf_op jit(solution)/shard_map/all_to_all | solution.py:40
  80.5 2.4 %collective-permute-start.11 = (bf16[16,32,256]{2,1,0:T(8,128)(2,1)}, bf16[16,32,256]{2,1,0:T(8,128)(2,1)}, u32[]{:S(2)}, u32[]{:S(2)}) collective-permute-start(bf16[16,32,256]{2,1,0:T(8,128)(2,1)} %copy-done.39), channel_id=1, source_target_pairs={{0,4},{1,5},{2,6},{3,7},{4,8},{5,9},{6,10},{7,11},{8,12},{9,13},{1... | collective-permute-start | bytes 786440 | tf_op jit(solution)/shard_map/ppermute | solution.py:357
  82.9 1.3 collective-permute-start.12
  84.2 1.4 collective-permute-start.13
  85.5 5.4 %all-to-all-done.2.parts_ref = bf16[64,8,128]{2,1,0:T(8,128)(2,1)S(1)} async-done(((bf16[64,8,128]{2,1,0:T(8,128)(2,1)}), bf16[64,8,128]{2,1,0:T(8,128)(2,1)S(1)}, u32[]{:S(2)}, u32[]{:S(2)}) %all-to-all-start.2) | async-done | bytes 131104 | tf_op jit(solution)/shard_map/all_to_all | solution.py:40
  90.9 1.7 copy-done.5
  92.7 1.5 shard_map.197
  94.2 4.2 %all-to-all-start.3 = ((f32[4,20,128]{2,1,0:T(8,128)}), f32[4,20,128]{2,1,0:T(8,128)S(1)}, u32[]{:S(2)}, u32[]{:S(2)}) async-start(f32[4,20,128]{2,1,0:T(8,128)} %shard_map.197), calls=%async_computation.3 | async-start | bytes 98304 | tf_op jit(solution)/shard_map/all_to_all | solution.py:418
  101.1 2.2 shard_map.198
  108.6 5.8 %all-to-all-start.4 = ((bf16[64,20,128]{2,1,0:T(8,128)(2,1)}), bf16[64,20,128]{2,1,0:T(8,128)(2,1)}, u32[]{:S(2)}, u32[]{:S(2)}) async-start(bf16[64,20,128]{2,1,0:T(8,128)(2,1)} %get-tuple-element.189), calls=%async_computation.4 | async-start | bytes 786432 | tf_op jit(solution)/shard_map/all_to_all | solution.py:40
  114.4 2.4 %collective-permute-start.14 = (bf16[16,32,256]{2,1,0:T(8,128)(2,1)}, bf16[16,32,256]{2,1,0:T(8,128)(2,1)S(1)}, u32[]{:S(2)}, u32[]{:S(2)}) collective-permute-start(bf16[16,32,256]{2,1,0:T(8,128)(2,1)} %copy-done.55), channel_id=1, source_target_pairs={{0,4},{1,5},{2,6},{3,7},{4,8},{5,9},{6,10},{7,11},{8,12},{9,13},{1... | collective-permute-start | bytes 786440 | tf_op jit(solution)/shard_map/ppermute | solution.py:357
  116.7 1.3 collective-permute-start.15
  123.0 2.7 %shard_map.200 = (bf16[16,32,256]{2,1,0:T(8,128)(2,1)S(1)}, bf16[16,32,256]{2,1,0:T(8,128)(2,1)S(1)}, bf16[16,32,256]{2,1,0:T(8,128)(2,1)S(1)}, bf16[16,32,256]{...) custom-call(bf16[16,32,256]{2,1,0:T(8,128)(2,1)S(1)} %copy-done.14, ...), custom_call_target="tpu_custom_call" | custom-call | bytes 4194304 | tf_op jit(solution)/shard_map/pallas_call | solution.py:329
  132.4 2.9 %collective-permute-done.14.refs_2_ = bf16[16,32,256]{2,1,0:T(8,128)(2,1)S(1)} collective-permute-done((bf16[16,32,256]{2,1,0:T(8,128)(2,1)}, bf16[16,32,256]{2,1,0:T(8,128)(2,1)S(1)}, u32[]{:S(2)}, u32[]{:S(2)}) %collective-permute-start.14) | collective-permute-done | bytes 262176 | tf_op jit(solution)/shard_map/ppermute | solution.py:357
  138.8 9.4 %all-to-all-start.5 = ((bf16[64,20,128]{2,1,0:T(8,128)(2,1)}), bf16[64,20,128]{2,1,0:T(8,128)(2,1)S(1)}, u32[]{:S(2)}, u32[]{:S(2)}) async-start(bf16[64,20,128]{2,1,0:T(8,128)(2,1)} %reshape.614), calls=%async_computation.5 | async-start | bytes 786432 | tf_op jit(solution)/shard_map/all_to_all | solution.py:40
  148.3 3.3 %collective-permute-start.16 = (bf16[16,32,256]{2,1,0:T(8,128)(2,1)}, bf16[16,32,256]{2,1,0:T(8,128)(2,1)S(1)}, u32[]{:S(2)}, u32[]{:S(2)}) collective-permute-start(bf16[16,32,256]{2,1,0:T(8,128)(2,1)} %copy-done.49), channel_id=1, source_target_pairs={{0,6},{1,7},{2,8},{3,9},{4,10},{5,11},{6,12},{7,13},{8,14},{9,15},... | collective-permute-start | bytes 786440 | tf_op jit(solution)/shard_map/ppermute | solution.py:357
  151.6 1.5 collective-permute-start.17
  153.1 2.9 %collective-permute-start.18 = (bf16[16,32,256]{2,1,0:T(8,128)(2,1)}, bf16[16,32,256]{2,1,0:T(8,128)(2,1)S(1)}, u32[]{:S(2)}, u32[]{:S(2)}) collective-permute-start(bf16[16,32,256]{2,1,0:T(8,128)(2,1)} %copy-done.53), channel_id=1, source_target_pairs={{0,32},{1,33},{2,34},{3,35},{4,36},{5,37},{6,38},{7,39},{8,40},{9,... | collective-permute-start | bytes 786440 | tf_op jit(solution)/shard_map/ppermute | solution.py:357
  156.3 2.3 collective-permute-start.20
  158.7 17.8 %collective-permute-done.16.refs_3_ = bf16[16,32,256]{2,1,0:T(8,128)(2,1)S(1)} collective-permute-done((bf16[16,32,256]{2,1,0:T(8,128)(2,1)}, bf16[16,32,256]{2,1,0:T(8,128)(2,1)S(1)}, u32[]{:S(2)}, u32[]{:S(2)}) %collective-permute-start.16) | collective-permute-done | bytes 262176 | tf_op jit(solution)/shard_map/ppermute | solution.py:357
  177.5 8.9 %all-to-all-start.6 = ((bf16[64,20,128]{2,1,0:T(8,128)(2,1)}), bf16[64,20,128]{2,1,0:T(8,128)(2,1)}, u32[]{:S(2)}, u32[]{:S(2)}) async-start(bf16[64,20,128]{2,1,0:T(8,128)(2,1)} %shard_map.202), calls=%async_computation.6 | async-start | bytes 786432 | tf_op jit(solution)/shard_map/all_to_all | solution.py:40
  186.9 1.4 collective-permute-start.21
  188.4 4.2 %collective-permute-start.22 = (bf16[16,32,256]{2,1,0:T(8,128)(2,1)S(1)}, bf16[16,32,256]{2,1,0:T(8,128)(2,1)S(1)}, u32[]{:S(2)}, u32[]{:S(2)}) collective-permute-start(bf16[16,32,256]{2,1,0:T(8,128)(2,1)S(1)} %copy-done.35), channel_id=1, source_target_pairs={{0,8},{1,9},{2,10},{3,11},{4,12},{5,13},{6,14},{7,15},{8,0},{9,1},... | collective-permute-start | bytes 786440 | tf_op jit(solution)/shard_map/ppermute | solution.py:357
  193.0 2.5 %collective-permute-start.23 = (bf16[16,32,256]{2,1,0:T(8,128)(2,1)S(1)}, bf16[16,32,256]{2,1,0:T(8,128)(2,1)S(1)}, u32[]{:S(2)}, u32[]{:S(2)}) collective-permute-start(bf16[16,32,256]{2,1,0:T(8,128)(2,1)S(1)} %copy-done.33), channel_id=1, source_target_pairs={{0,14},{1,15},{2,0},{3,1},{4,2},{5,3},{6,4},{7,5},{8,6},{9,7},{10,... | collective-permute-start | bytes 786440 | tf_op jit(solution)/shard_map/ppermute | solution.py:357
  197.8 5.8 %collective-permute-done.21.refs_1_ = bf16[16,32,256]{2,1,0:T(8,128)(2,1)S(1)} collective-permute-done((bf16[16,32,256]{2,1,0:T(8,128)(2,1)}, bf16[16,32,256]{2,1,0:T(8,128)(2,1)S(1)}, u32[]{:S(2)}, u32[]{:S(2)}) %collective-permute-start.21) | collective-permute-done | bytes 262176 | tf_op jit(solution)/shard_map/ppermute | solution.py:357
  203.6 3.6 %collective-permute-start.26 = (bf16[16,32,256]{2,1,0:T(8,128)(2,1)}, bf16[16,32,256]{2,1,0:T(8,128)(2,1)S(1)}, u32[]{:S(2)}, u32[]{:S(2)}) collective-permute-start(bf16[16,32,256]{2,1,0:T(8,128)(2,1)} %copy-done.41), channel_id=1, source_target_pairs={{0,33},{1,32},{2,35},{3,34},{4,37},{5,36},{6,39},{7,38},{8,41},{9,... | collective-permute-start | bytes 786440 | tf_op jit(solution)/shard_map/ppermute | solution.py:357
  207.2 6.7 %collective-permute-done.22.refs_4_ = bf16[16,32,256]{2,1,0:T(8,128)(2,1)S(1)} collective-permute-done((bf16[16,32,256]{2,1,0:T(8,128)(2,1)S(1)}, bf16[16,32,256]{2,1,0:T(8,128)(2,1)S(1)}, u32[]{:S(2)}, u32[]{:S(2)}) %collective-permute-start.22) | collective-permute-done | bytes 262176 | tf_op jit(solution)/shard_map/ppermute | solution.py:357
  213.9 3.4 %collective-permute-start.27 = (bf16[16,32,256]{2,1,0:T(8,128)(2,1)}, bf16[16,32,256]{2,1,0:T(8,128)(2,1)S(1)}, u32[]{:S(2)}, u32[]{:S(2)}) collective-permute-start(bf16[16,32,256]{2,1,0:T(8,128)(2,1)} %copy-done.40), channel_id=1, source_target_pairs={{0,49},{1,48},{2,51},{3,50},{4,53},{5,52},{6,55},{7,54},{8,57},{9,... | collective-permute-start | bytes 786440 | tf_op jit(solution)/shard_map/ppermute | solution.py:357
  217.4 6.4 %collective-permute-done.27.refs_15_ = bf16[16,32,256]{2,1,0:T(8,128)(2,1)S(1)} collective-permute-done((bf16[16,32,256]{2,1,0:T(8,128)(2,1)}, bf16[16,32,256]{2,1,0:T(8,128)(2,1)S(1)}, u32[]{:S(2)}, u32[]{:S(2)}) %collective-permute-start.27) | collective-permute-done | bytes 262176 | tf_op jit(solution)/shard_map/ppermute | solution.py:357
  223.7 9.6 %shard_map.203 = (bf16[128,32,256]{2,1,0:T(8,128)(2,1)}, bf16[128,32,256]{2,1,0:T(8,128)(2,1)}) custom-call(s32[2,64]{1,0:T(2,128)S(1)} %pad_add_fusion.place_ref, s32[64]{0:T(128)S(1)} %compare_select_fusion.8.arrive_ref, bf16[64,8,128]{2,1,0:T(8,128)(2,1)S(1)} %all-to-all-done.1.fresh_ref, bf16[16,32,256]{2,1,0:T(8,128)(2,1)S(1)} %get-tuple-element.217.refs_0_, ...), custom_call_target="tpu_custom_call" | custom-call | bytes 8388608 | tf_op jit(solution)/shard_map/pallas_call | solution.py:500
  233.3 1.9 copy.29
  (189 shorter events, 43.0 us)
Async XLA Ops:
  0.6 42.3 %copy-start.58 = (s32[64]{0:T(128)S(1)}, s32[64]{0:T(128)}, u32[]{:S(2)}) copy-start(s32[64]{0:T(128)} %param.20) | copy-start | bytes 772
  0.7 71.8 %copy-start.2 = (bf16[64,32,256]{2,1,0:T(8,128)(2,1)S(1)}, bf16[64,32,256]{2,1,0:T(8,128)(2,1)}, u32[]{:S(2)}) copy-start(bf16[64,32,256]{2,1,0:T(8,128)(2,1)} %keys_ref.1) | copy-start | bytes 3145732
  0.7 66.3 %copy-start.56 = (s32[64,512]{1,0:T(8,128)S(1)}, s32[64,512]{1,0:T(8,128)}, u32[]{:S(2)}) copy-start(s32[64,512]{1,0:T(8,128)} %param.21) | copy-start | bytes 393220
  4.4 28.9 %all-to-all-start = ((bf16[64,8,128]{2,1,0:T(8,128)(2,1)}), bf16[64,8,128]{2,1,0:T(8,128)(2,1)S(1)}, u32[]{:S(2)}, u32[]{:S(2)}) async-start(bf16[64,8,128]{2,1,0:T(8,128)(2,1)} %bitcast.12), calls=%async_computation | async-start | bytes 262144 | tf_op jit(solution)/shard_map/all_to_all | solution.py:40
  22.4 50.0 %copy-start.4 = (bf16[64,32,256]{2,1,0:T(8,128)(2,1)S(1)}, bf16[64,32,256]{2,1,0:T(8,128)(2,1)}, u32[]{:S(2)}) copy-start(bf16[64,32,256]{2,1,0:T(8,128)(2,1)} %values_ref.1) | copy-start | bytes 3145732
  34.2 18.1 %collective-permute-start = (bf16[16,32,256]{2,1,0:T(8,128)(2,1)}, bf16[16,32,256]{2,1,0:T(8,128)(2,1)S(1)}, u32[]{:S(2)}, u32[]{:S(2)}) collective-permute-start(bf16[16,32,256]{2,1,0:T(8,128)(2,1)} %get-tuple-element.154), channel_id=1, source_target_pairs={{0,8},{1,9},{2,10},{3,11},{4,12},{5,13},{6,14},{7,15},{8,0},{9,1},... | collective-permute-start | bytes 786440 | tf_op jit(solution)/shard_map/ppermute | solution.py:357
  39.4 18.3 %collective-permute-start.1 = (bf16[16,32,256]{2,1,0:T(8,128)(2,1)S(1)}, bf16[16,32,256]{2,1,0:T(8,128)(2,1)S(1)}, u32[]{:S(2)}, u32[]{:S(2)}) collective-permute-start(bf16[16,32,256]{2,1,0:T(8,128)(2,1)S(1)} %get-tuple-element.155), channel_id=1, source_target_pairs={{0,2},{1,3},{2,4},{3,5},{4,6},{5,7},{6,8},{7,9},{8,10},{9,11},{10,... | collective-permute-start | bytes 786440 | tf_op jit(solution)/shard_map/ppermute | solution.py:357
  39.7 18.7 %collective-permute-start.2 = (bf16[16,32,256]{2,1,0:T(8,128)(2,1)}, bf16[16,32,256]{2,1,0:T(8,128)(2,1)S(1)}, u32[]{:S(2)}, u32[]{:S(2)}) collective-permute-start(bf16[16,32,256]{2,1,0:T(8,128)(2,1)} %get-tuple-element.156), channel_id=1, source_target_pairs={{0,32},{1,33},{2,34},{3,35},{4,36},{5,37},{6,38},{7,39},{8,40},{9,... | collective-permute-start | bytes 786440 | tf_op jit(solution)/shard_map/ppermute | solution.py:357
  42.6 20.3 %collective-permute-start.3 = (bf16[16,32,256]{2,1,0:T(8,128)(2,1)}, bf16[16,32,256]{2,1,0:T(8,128)(2,1)}, u32[]{:S(2)}, u32[]{:S(2)}) collective-permute-start(bf16[16,32,256]{2,1,0:T(8,128)(2,1)} %get-tuple-element.157), channel_id=1, source_target_pairs={{0,16},{1,17},{2,18},{3,19},{4,20},{5,21},{6,22},{7,23},{8,24},{9,... | collective-permute-start | bytes 786440 | tf_op jit(solution)/shard_map/ppermute | solution.py:357
  43.7 25.4 %collective-permute-start.4 = (bf16[16,32,256]{2,1,0:T(8,128)(2,1)}, bf16[16,32,256]{2,1,0:T(8,128)(2,1)}, u32[]{:S(2)}, u32[]{:S(2)}) collective-permute-start(bf16[16,32,256]{2,1,0:T(8,128)(2,1)} %get-tuple-element.158), channel_id=1, source_target_pairs={{0,48},{1,49},{2,50},{3,51},{4,52},{5,53},{6,54},{7,55},{8,56},{9,... | collective-permute-start | bytes 786440 | tf_op jit(solution)/shard_map/ppermute | solution.py:357
  46.0 23.2 %all-to-all-start.1 = ((bf16[64,8,128]{2,1,0:T(8,128)(2,1)}), bf16[64,8,128]{2,1,0:T(8,128)(2,1)S(1)}, u32[]{:S(2)}, u32[]{:S(2)}) async-start(bf16[64,8,128]{2,1,0:T(8,128)(2,1)} %get-tuple-element.153), calls=%async_computation.1 | async-start | bytes 262144 | tf_op jit(solution)/shard_map/all_to_all | solution.py:40
  52.3 41.9 %copy-start.15 = (bf16[16,32,256]{2,1,0:T(8,128)(2,1)}, bf16[16,32,256]{2,1,0:T(8,128)(2,1)S(1)}, u32[]{:S(2)}) copy-start(bf16[16,32,256]{2,1,0:T(8,128)(2,1)S(1)} %collective-permute-done.refs_4_) | copy-start | bytes 786436
  52.3 17.0 %collective-permute-start.10 = (bf16[16,32,256]{2,1,0:T(8,128)(2,1)}, bf16[16,32,256]{2,1,0:T(8,128)(2,1)}, u32[]{:S(2)}, u32[]{:S(2)}) collective-permute-start(bf16[16,32,256]{2,1,0:T(8,128)(2,1)} %get-tuple-element.165), channel_id=1, source_target_pairs={{0,1},{1,0},{2,3},{3,2},{4,5},{5,4},{6,7},{7,6},{8,9},{9,8},{10,11... | collective-permute-start | bytes 786440 | tf_op jit(solution)/shard_map/ppermute | solution.py:357
  57.7 36.5 %copy-start.17 = (bf16[16,32,256]{2,1,0:T(8,128)(2,1)}, bf16[16,32,256]{2,1,0:T(8,128)(2,1)S(1)}, u32[]{:S(2)}) copy-start(bf16[16,32,256]{2,1,0:T(8,128)(2,1)S(1)} %collective-permute-done.1.refs_1_) | copy-start | bytes 786436
  57.7 22.7 %collective-permute-start.5 = (bf16[16,32,256]{2,1,0:T(8,128)(2,1)}, bf16[16,32,256]{2,1,0:T(8,128)(2,1)S(1)}, u32[]{:S(2)}, u32[]{:S(2)}) collective-permute-start(bf16[16,32,256]{2,1,0:T(8,128)(2,1)} %copy-done.50), channel_id=1, source_target_pairs={{0,6},{1,7},{2,8},{3,9},{4,10},{5,11},{6,12},{7,13},{8,14},{9,15},... | collective-permute-start | bytes 786440 | tf_op jit(solution)/shard_map/ppermute | solution.py:357
  59.2 23.7 %collective-permute-start.6 = (bf16[16,32,256]{2,1,0:T(8,128)(2,1)}, bf16[16,32,256]{2,1,0:T(8,128)(2,1)S(1)}, u32[]{:S(2)}, u32[]{:S(2)}) collective-permute-start(bf16[16,32,256]{2,1,0:T(8,128)(2,1)} %copy-done.48), channel_id=1, source_target_pairs={{0,10},{1,11},{2,12},{3,13},{4,14},{5,15},{6,0},{7,1},{8,2},{9,3},... | collective-permute-start | bytes 786440 | tf_op jit(solution)/shard_map/ppermute | solution.py:357
  62.9 21.3 %collective-permute-start.7 = (bf16[16,32,256]{2,1,0:T(8,128)(2,1)}, bf16[16,32,256]{2,1,0:T(8,128)(2,1)}, u32[]{:S(2)}, u32[]{:S(2)}) collective-permute-start(bf16[16,32,256]{2,1,0:T(8,128)(2,1)} %copy-done.46), channel_id=1, source_target_pairs={{0,33},{1,32},{2,35},{3,34},{4,37},{5,36},{6,39},{7,38},{8,41},{9,... | collective-permute-start | bytes 786440 | tf_op jit(solution)/shard_map/ppermute | solution.py:357
  69.1 16.4 %collective-permute-start.8 = (bf16[16,32,256]{2,1,0:T(8,128)(2,1)}, bf16[16,32,256]{2,1,0:T(8,128)(2,1)}, u32[]{:S(2)}, u32[]{:S(2)}) collective-permute-start(bf16[16,32,256]{2,1,0:T(8,128)(2,1)} %copy-done.45), channel_id=1, source_target_pairs={{0,17},{1,16},{2,19},{3,18},{4,21},{5,20},{6,23},{7,22},{8,25},{9,... | collective-permute-start | bytes 786440 | tf_op jit(solution)/shard_map/ppermute | solution.py:357
  69.3 16.3 %collective-permute-start.9 = (bf16[16,32,256]{2,1,0:T(8,128)(2,1)}, bf16[16,32,256]{2,1,0:T(8,128)(2,1)}, u32[]{:S(2)}, u32[]{:S(2)}) collective-permute-start(bf16[16,32,256]{2,1,0:T(8,128)(2,1)} %copy-done.44), channel_id=1, source_target_pairs={{0,49},{1,48},{2,51},{3,50},{4,53},{5,52},{6,55},{7,54},{8,57},{9,... | collective-permute-start | bytes 786440 | tf_op jit(solution)/shard_map/ppermute | solution.py:357
  75.0 16.0 %all-to-all-start.2 = ((bf16[64,8,128]{2,1,0:T(8,128)(2,1)}), bf16[64,8,128]{2,1,0:T(8,128)(2,1)S(1)}, u32[]{:S(2)}, u32[]{:S(2)}) async-start(bf16[64,8,128]{2,1,0:T(8,128)(2,1)} %bitcast.16), calls=%async_computation.2 | async-start | bytes 262144 | tf_op jit(solution)/shard_map/all_to_all | solution.py:40
  80.5 26.4 %collective-permute-start.11 = (bf16[16,32,256]{2,1,0:T(8,128)(2,1)}, bf16[16,32,256]{2,1,0:T(8,128)(2,1)}, u32[]{:S(2)}, u32[]{:S(2)}) collective-permute-start(bf16[16,32,256]{2,1,0:T(8,128)(2,1)} %copy-done.39), channel_id=1, source_target_pairs={{0,4},{1,5},{2,6},{3,7},{4,8},{5,9},{6,10},{7,11},{8,12},{9,13},{1... | collective-permute-start | bytes 786440 | tf_op jit(solution)/shard_map/ppermute | solution.py:357
  82.9 24.0 %collective-permute-start.12 = (bf16[16,32,256]{2,1,0:T(8,128)(2,1)}, bf16[16,32,256]{2,1,0:T(8,128)(2,1)}, u32[]{:S(2)}, u32[]{:S(2)}) collective-permute-start(bf16[16,32,256]{2,1,0:T(8,128)(2,1)} %copy-done.38), channel_id=1, source_target_pairs={{0,12},{1,13},{2,14},{3,15},{4,0},{5,1},{6,2},{7,3},{8,4},{9,5},{1... | collective-permute-start | bytes 786440 | tf_op jit(solution)/shard_map/ppermute | solution.py:357
  84.2 23.4 %collective-permute-start.13 = (bf16[16,32,256]{2,1,0:T(8,128)(2,1)}, bf16[16,32,256]{2,1,0:T(8,128)(2,1)}, u32[]{:S(2)}, u32[]{:S(2)}) collective-permute-start(bf16[16,32,256]{2,1,0:T(8,128)(2,1)} %copy-done.36), channel_id=1, source_target_pairs={{0,14},{1,15},{2,0},{3,1},{4,2},{5,3},{6,4},{7,5},{8,6},{9,7},{10,... | collective-permute-start | bytes 786440 | tf_op jit(solution)/shard_map/ppermute | solution.py:357
  94.2 13.3 %all-to-all-start.3 = ((f32[4,20,128]{2,1,0:T(8,128)}), f32[4,20,128]{2,1,0:T(8,128)S(1)}, u32[]{:S(2)}, u32[]{:S(2)}) async-start(f32[4,20,128]{2,1,0:T(8,128)} %shard_map.197), calls=%async_computation.3 | async-start | bytes 98304 | tf_op jit(solution)/shard_map/all_to_all | solution.py:418
  101.1 35.8 %copy-start.8 = (bf16[160,2560]{1,0:T(8,128)(2,1)S(1)}, bf16[160,2560]{1,0:T(8,128)(2,1)}, u32[]{:S(2)}) copy-start(bf16[160,2560]{1,0:T(8,128)(2,1)} %down_ref.1) | copy-start | bytes 2457604
  108.6 22.7 %all-to-all-start.4 = ((bf16[64,20,128]{2,1,0:T(8,128)(2,1)}), bf16[64,20,128]{2,1,0:T(8,128)(2,1)}, u32[]{:S(2)}, u32[]{:S(2)}) async-start(bf16[64,20,128]{2,1,0:T(8,128)(2,1)} %get-tuple-element.189), calls=%async_computation.4 | async-start | bytes 786432 | tf_op jit(solution)/shard_map/all_to_all | solution.py:40
  114.4 20.9 %collective-permute-start.14 = (bf16[16,32,256]{2,1,0:T(8,128)(2,1)}, bf16[16,32,256]{2,1,0:T(8,128)(2,1)S(1)}, u32[]{:S(2)}, u32[]{:S(2)}) collective-permute-start(bf16[16,32,256]{2,1,0:T(8,128)(2,1)} %copy-done.55), channel_id=1, source_target_pairs={{0,4},{1,5},{2,6},{3,7},{4,8},{5,9},{6,10},{7,11},{8,12},{9,13},{1... | collective-permute-start | bytes 786440 | tf_op jit(solution)/shard_map/ppermute | solution.py:357
  116.7 20.1 %collective-permute-start.15 = (bf16[16,32,256]{2,1,0:T(8,128)(2,1)}, bf16[16,32,256]{2,1,0:T(8,128)(2,1)}, u32[]{:S(2)}, u32[]{:S(2)}) collective-permute-start(bf16[16,32,256]{2,1,0:T(8,128)(2,1)} %copy-done.54), channel_id=1, source_target_pairs={{0,12},{1,13},{2,14},{3,15},{4,0},{5,1},{6,2},{7,3},{8,4},{9,5},{1... | collective-permute-start | bytes 786440 | tf_op jit(solution)/shard_map/ppermute | solution.py:357
  131.3 45.2 %copy-start.29 = (f32[2560]{0:T(1024)S(1)}, f32[2560]{0:T(1024)}, u32[]{:S(2)}) copy-start(f32[2560]{0:T(1024)} %param.32) | copy-start | bytes 30724
  136.9 49.6 %copy-start.57 = (s32[4096,1]{0,1:T(1,128)S(1)}, s32[4096,1]{0,1:T(1,128)}, u32[]{:S(2)}) copy-start(s32[4096,1]{0,1:T(1,128)} %param.22) | copy-start | bytes 49156
  137.8 50.5 %copy-start.35 = (bf16[16,32,256]{2,1,0:T(8,128)(2,1)S(1)}, bf16[16,32,256]{2,1,0:T(8,128)(2,1)}, u32[]{:S(2)}) copy-start(bf16[16,32,256]{2,1,0:T(8,128)(2,1)} %copy-done.34) | copy-start | bytes 786436
  137.8 55.2 %copy-start.33 = (bf16[16,32,256]{2,1,0:T(8,128)(2,1)S(1)}, bf16[16,32,256]{2,1,0:T(8,128)(2,1)}, u32[]{:S(2)}) copy-start(bf16[16,32,256]{2,1,0:T(8,128)(2,1)} %copy-done.32) | copy-start | bytes 786436
  137.8 85.9 %copy-start.10 = (bf16[16,32,256]{2,1,0:T(8,128)(2,1)S(1)}, bf16[16,32,256]{2,1,0:T(8,128)(2,1)}, u32[]{:S(2)}) copy-start(bf16[16,32,256]{2,1,0:T(8,128)(2,1)} %copy-done.9) | copy-start | bytes 786436
  137.9 85.9 %copy-start.12 = (bf16[16,32,256]{2,1,0:T(8,128)(2,1)S(1)}, bf16[16,32,256]{2,1,0:T(8,128)(2,1)}, u32[]{:S(2)}) copy-start(bf16[16,32,256]{2,1,0:T(8,128)(2,1)} %copy-done.11) | copy-start | bytes 786436
  138.8 37.7 %all-to-all-start.5 = ((bf16[64,20,128]{2,1,0:T(8,128)(2,1)}), bf16[64,20,128]{2,1,0:T(8,128)(2,1)S(1)}, u32[]{:S(2)}, u32[]{:S(2)}) async-start(bf16[64,20,128]{2,1,0:T(8,128)(2,1)} %reshape.614), calls=%async_computation.5 | async-start | bytes 786432 | tf_op jit(solution)/shard_map/all_to_all | solution.py:40
  148.3 28.2 %collective-permute-start.16 = (bf16[16,32,256]{2,1,0:T(8,128)(2,1)}, bf16[16,32,256]{2,1,0:T(8,128)(2,1)S(1)}, u32[]{:S(2)}, u32[]{:S(2)}) collective-permute-start(bf16[16,32,256]{2,1,0:T(8,128)(2,1)} %copy-done.49), channel_id=1, source_target_pairs={{0,6},{1,7},{2,8},{3,9},{4,10},{5,11},{6,12},{7,13},{8,14},{9,15},... | collective-permute-start | bytes 786440 | tf_op jit(solution)/shard_map/ppermute | solution.py:357
  151.6 25.0 %collective-permute-start.17 = (bf16[16,32,256]{2,1,0:T(8,128)(2,1)}, bf16[16,32,256]{2,1,0:T(8,128)(2,1)S(1)}, u32[]{:S(2)}, u32[]{:S(2)}) collective-permute-start(bf16[16,32,256]{2,1,0:T(8,128)(2,1)} %copy-done.47), channel_id=1, source_target_pairs={{0,10},{1,11},{2,12},{3,13},{4,14},{5,15},{6,0},{7,1},{8,2},{9,3},... | collective-permute-start | bytes 786440 | tf_op jit(solution)/shard_map/ppermute | solution.py:357
  153.1 23.4 %collective-permute-start.18 = (bf16[16,32,256]{2,1,0:T(8,128)(2,1)}, bf16[16,32,256]{2,1,0:T(8,128)(2,1)S(1)}, u32[]{:S(2)}, u32[]{:S(2)}) collective-permute-start(bf16[16,32,256]{2,1,0:T(8,128)(2,1)} %copy-done.53), channel_id=1, source_target_pairs={{0,32},{1,33},{2,34},{3,35},{4,36},{5,37},{6,38},{7,39},{8,40},{9,... | collective-permute-start | bytes 786440 | tf_op jit(solution)/shard_map/ppermute | solution.py:357
  155.9 20.6 %collective-permute-start.19 = (bf16[16,32,256]{2,1,0:T(8,128)(2,1)}, bf16[16,32,256]{2,1,0:T(8,128)(2,1)S(1)}, u32[]{:S(2)}, u32[]{:S(2)}) collective-permute-start(bf16[16,32,256]{2,1,0:T(8,128)(2,1)} %copy-done.52), channel_id=1, source_target_pairs={{0,16},{1,17},{2,18},{3,19},{4,20},{5,21},{6,22},{7,23},{8,24},{9,... | collective-permute-start | bytes 786440 | tf_op jit(solution)/shard_map/ppermute | solution.py:357
  156.3 20.2 %collective-permute-start.20 = (bf16[16,32,256]{2,1,0:T(8,128)(2,1)}, bf16[16,32,256]{2,1,0:T(8,128)(2,1)S(1)}, u32[]{:S(2)}, u32[]{:S(2)}) collective-permute-start(bf16[16,32,256]{2,1,0:T(8,128)(2,1)} %copy-done.51), channel_id=1, source_target_pairs={{0,48},{1,49},{2,50},{3,51},{4,52},{5,53},{6,54},{7,55},{8,56},{9,... | collective-permute-start | bytes 786440 | tf_op jit(solution)/shard_map/ppermute | solution.py:357
  177.5 55.8 %all-to-all-start.6 = ((bf16[64,20,128]{2,1,0:T(8,128)(2,1)}), bf16[64,20,128]{2,1,0:T(8,128)(2,1)}, u32[]{:S(2)}, u32[]{:S(2)}) async-start(bf16[64,20,128]{2,1,0:T(8,128)(2,1)} %shard_map.202), calls=%async_computation.6 | async-start | bytes 786432 | tf_op jit(solution)/shard_map/all_to_all | solution.py:40
  186.9 16.6 %collective-permute-start.21 = (bf16[16,32,256]{2,1,0:T(8,128)(2,1)}, bf16[16,32,256]{2,1,0:T(8,128)(2,1)S(1)}, u32[]{:S(2)}, u32[]{:S(2)}) collective-permute-start(bf16[16,32,256]{2,1,0:T(8,128)(2,1)} %copy-done.37), channel_id=1, source_target_pairs={{0,2},{1,3},{2,4},{3,5},{4,6},{5,7},{6,8},{7,9},{8,10},{9,11},{10,... | collective-permute-start | bytes 786440 | tf_op jit(solution)/shard_map/ppermute | solution.py:357
  188.4 25.5 %collective-permute-start.22 = (bf16[16,32,256]{2,1,0:T(8,128)(2,1)S(1)}, bf16[16,32,256]{2,1,0:T(8,128)(2,1)S(1)}, u32[]{:S(2)}, u32[]{:S(2)}) collective-permute-start(bf16[16,32,256]{2,1,0:T(8,128)(2,1)S(1)} %copy-done.35), channel_id=1, source_target_pairs={{0,8},{1,9},{2,10},{3,11},{4,12},{5,13},{6,14},{7,15},{8,0},{9,1},... | collective-permute-start | bytes 786440 | tf_op jit(solution)/shard_map/ppermute | solution.py:357
  193.0 24.3 %collective-permute-start.23 = (bf16[16,32,256]{2,1,0:T(8,128)(2,1)S(1)}, bf16[16,32,256]{2,1,0:T(8,128)(2,1)S(1)}, u32[]{:S(2)}, u32[]{:S(2)}) collective-permute-start(bf16[16,32,256]{2,1,0:T(8,128)(2,1)S(1)} %copy-done.33), channel_id=1, source_target_pairs={{0,14},{1,15},{2,0},{3,1},{4,2},{5,3},{6,4},{7,5},{8,6},{9,7},{10,... | collective-permute-start | bytes 786440 | tf_op jit(solution)/shard_map/ppermute | solution.py:357
  195.5 21.8 %collective-permute-start.24 = (bf16[16,32,256]{2,1,0:T(8,128)(2,1)}, bf16[16,32,256]{2,1,0:T(8,128)(2,1)S(1)}, u32[]{:S(2)}, u32[]{:S(2)}) collective-permute-start(bf16[16,32,256]{2,1,0:T(8,128)(2,1)} %copy-done.43), channel_id=1, source_target_pairs={{0,1},{1,0},{2,3},{3,2},{4,5},{5,4},{6,7},{7,6},{8,9},{9,8},{10,11... | collective-permute-start | bytes 786440 | tf_op jit(solution)/shard_map/ppermute | solution.py:357
  196.7 20.6 %collective-permute-start.25 = (bf16[16,32,256]{2,1,0:T(8,128)(2,1)}, bf16[16,32,256]{2,1,0:T(8,128)(2,1)S(1)}, u32[]{:S(2)}, u32[]{:S(2)}) collective-permute-start(bf16[16,32,256]{2,1,0:T(8,128)(2,1)} %copy-done.42), channel_id=1, source_target_pairs={{0,17},{1,16},{2,19},{3,18},{4,21},{5,20},{6,23},{7,22},{8,25},{9,... | collective-permute-start | bytes 786440 | tf_op jit(solution)/shard_map/ppermute | solution.py:357
  203.6 13.8 %collective-permute-start.26 = (bf16[16,32,256]{2,1,0:T(8,128)(2,1)}, bf16[16,32,256]{2,1,0:T(8,128)(2,1)S(1)}, u32[]{:S(2)}, u32[]{:S(2)}) collective-permute-start(bf16[16,32,256]{2,1,0:T(8,128)(2,1)} %copy-done.41), channel_id=1, source_target_pairs={{0,33},{1,32},{2,35},{3,34},{4,37},{5,36},{6,39},{7,38},{8,41},{9,... | collective-permute-start | bytes 786440 | tf_op jit(solution)/shard_map/ppermute | solution.py:357
  213.9 9.8 %collective-permute-start.27 = (bf16[16,32,256]{2,1,0:T(8,128)(2,1)}, bf16[16,32,256]{2,1,0:T(8,128)(2,1)S(1)}, u32[]{:S(2)}, u32[]{:S(2)}) collective-permute-start(bf16[16,32,256]{2,1,0:T(8,128)(2,1)} %copy-done.40), channel_id=1, source_target_pairs={{0,49},{1,48},{2,51},{3,50},{4,53},{5,52},{6,55},{7,54},{8,57},{9,... | collective-permute-start | bytes 786440 | tf_op jit(solution)/shard_map/ppermute | solution.py:357
  (46 other events, 268.6 us)

commit v5 on v1

--- a/solution.py
+++ b/solution.py
@@ -15,6 +15,7 @@
 LANES = 128
 BF16 = jnp.bfloat16
 F32 = jnp.float32
+PARAMS = pltpu.CompilerParams(vmem_limit_bytes=16 << 20)
 
 
 def call(body, out_shape, n_in, flops, bytes_accessed):
@@ -27,7 +28,12 @@
         cost_estimate=pl.CostEstimate(
             flops=flops, bytes_accessed=bytes_accessed, transcendentals=0
         ),
-    )
+        compiler_params=PARAMS,
+    )
+
+
+def tie(*values):
+    return lax.optimization_barrier(values)
 
 
 def exchange(x):
@@ -134,9 +140,8 @@
 
 
 def residual_body(*refs):
-    part_refs = refs[:-5]
     hidden_ref, attn_gain_ref, ffw_gain_ref, residual_ref, all_ref = refs[-5:]
-    parts = [ref[...] for ref in part_refs]
+    parts = [ref[...] for ref in refs[:-5]]
     while len(parts) > 1:
         half = len(parts) // 2
         parts = [parts[i] + parts[i + half] for i in range(half)]
@@ -153,8 +158,9 @@
 
 def ffw_body(x_ref, gate_ref, up_ref, down_ref, out_ref):
     x = x_ref[...]
-    gate = jnp.dot(x, gate_ref[...], preferred_element_type=F32)
-    up = jnp.dot(x, up_ref[...], preferred_element_type=F32)
+    across = (((1,), (1,)), ((), ()))
+    gate = lax.dot_general(x, gate_ref[...], across, preferred_element_type=F32)
+    up = lax.dot_general(x, up_ref[...], across, preferred_element_type=F32)
     units = (jax.nn.gelu(gate, approximate=True) * up).astype(BF16)
     out_ref[...] = jnp.dot(units, down_ref[...], preferred_element_type=F32).astype(BF16)
 
@@ -166,17 +172,30 @@
     all_ref[...] = jnp.broadcast_to(row.astype(BF16)[None], all_ref.shape)
 
 
-def migrate(pages, source_of, blocks, capacity):
-    send = jnp.take(pages, source_of, axis=0, mode="fill", fill_value=0)
-    send = send.reshape((blocks, capacity) + pages.shape[1:])
-    got = lax.all_to_all(send, "blk", split_axis=0, concat_axis=0, tiled=True)
-    return got.reshape((blocks * capacity,) + pages.shape[1:])
-
-
-def patch(pages, flat_pos, rows):
-    count, page, width = pages.shape
-    flat = pages.reshape(count * page, width).at[flat_pos].set(rows, mode="drop")
-    return flat.reshape(count, page, width)
+def send_body(tile, source_ref, fresh_at_ref, fresh_ref, pages_ref, out_ref):
+    slots, page, _ = pages_ref.shape
+
+    @pl.loop(0, out_ref.shape[0], unroll=4)
+    def _(q):
+        source = source_ref[q]
+        old = pages_ref[jnp.minimum(source, slots - 1)]
+        out_ref[q] = jnp.where(source < slots, old, jnp.zeros_like(old))
+
+    @pl.loop(0, fresh_ref.shape[0])
+    def _(r):
+        where = fresh_at_ref[r]
+
+        @pl.when(where >= 0)
+        def _():
+            new = fresh_ref[r].astype(F32)
+            row = jnp.concatenate([new[tile : tile + 1], new[tile + 1 : tile + 2]], axis=1)
+            old = out_ref[where // page].astype(F32)
+            here = lax.broadcasted_iota(jnp.int32, old.shape, 0) == where % page
+            out_ref[where // page] = jnp.where(here, row, old).astype(BF16)
+
+
+def copy_body(in_ref, out_ref):
+    out_ref[...] = in_ref[...]
 
 
 def local(
@@ -245,7 +264,43 @@
         query_norm_gain.reshape(tile),
         key_gain.reshape(tile),
     )
-    every = exchange(every).reshape(requests, columns)
+    every = exchange(every)
+
+    dest = lax.dynamic_slice_in_dim(move_dest[:, 0], device * slots, slots)
+    slot_iota = jnp.arange(slots, dtype=jnp.int32)
+    earlier = (dest[None, :] == dest[:, None]) & (slot_iota[None, :] < slot_iota[:, None])
+    order = dest * capacity + jnp.sum(earlier.astype(jnp.int32), axis=1)
+    match = order[None, :] == jnp.arange(recv_slots, dtype=jnp.int32)[:, None]
+    source_of = slots + jnp.sum(jnp.where(match, slot_iota[None, :] - slots, 0), axis=1)
+    target = jnp.sum(
+        jnp.where(
+            jnp.arange(pages_per_seq, dtype=jnp.int32)[None, :] == cache_len[:, None] // page,
+            page_table,
+            0,
+        ),
+        axis=1,
+    )
+    mine = (target - device * slots)[:, None] == slot_iota[None, :]
+    fresh_at = jnp.sum(
+        jnp.where(mine, order[None, :] * page + cache_len[:, None] % page + 1, 0), axis=1
+    ) - 1
+    vmem = pl.BlockSpec(memory_space=pltpu.VMEM)
+    smem = pl.BlockSpec(memory_space=pltpu.SMEM)
+
+    def sends(pages, tile):
+        out = pl.pallas_call(
+            functools.partial(send_body, tile),
+            out_shape=jax.ShapeDtypeStruct((recv_slots, page, head), BF16),
+            in_specs=[smem, smem, vmem, vmem],
+            out_specs=vmem,
+            cost_estimate=pl.CostEstimate(
+                flops=0, bytes_accessed=6 * slots * page * head, transcendentals=0
+            ),
+        )(source_of, fresh_at, every, pages)
+        return out.reshape(blocks, capacity, page, head)
+
+    keys_send = sends(paged_keys, 2 * groups)
+    values_send = sends(paged_values, 2 * groups + 2)
 
     slot_ids = device * slots + jnp.arange(slots, dtype=jnp.int32)
     page_starts = jnp.arange(pages_per_seq, dtype=jnp.int32) * page
@@ -259,8 +314,10 @@
         4,
         4 * groups * requests * slots * page * head,
         4 * slots * page * head,
-    )(every, paged_keys, paged_values, limit)
+    )(every.reshape(requests, columns), paged_keys, paged_values, limit)
     parts = exchange(parts.reshape(requests, col_tiles, LANES))
+    parts, keys_send = tie(parts, keys_send)
+    relocated_keys = exchange(keys_send)
     attn_terms = call(
         functools.partial(merge_body, groups),
         jax.ShapeDtypeStruct((model_tiles, LANES), F32),
@@ -289,6 +346,7 @@
         attn_gain.reshape(wide),
         ffw_gain.reshape(wide),
     )
+    ffw_in, relocated_keys = tie(ffw_in, relocated_keys)
     ffw_in = exchange(ffw_in).reshape(requests, model)
     units = gate_weight.shape[1]
     ffw_terms = call(
@@ -297,7 +355,7 @@
         4,
         6 * requests * units * model,
         6 * units * model,
-    )(ffw_in, gate_weight, up_weight, down_weight)
+    )(ffw_in, gate_weight.T, up_weight.T, down_weight)
     ffw_terms = exchange(ffw_terms.reshape((requests,) + wide))
     out_rows = call(
         output_body,
@@ -306,46 +364,18 @@
         requests * model,
         4 * requests * model,
     )(ffw_terms, residual, final_gain.reshape(wide))
-    out_hidden = exchange(out_rows).reshape(requests, model).astype(F32)
-
-    dest = lax.dynamic_slice_in_dim(move_dest[:, 0], device * slots, slots)
-    slot_iota = jnp.arange(slots, dtype=jnp.int32)
-    earlier = (dest[None, :] == dest[:, None]) & (slot_iota[None, :] < slot_iota[:, None])
-    outgoing = dest * capacity + jnp.sum(earlier.astype(jnp.int32), axis=1)
-    match = outgoing[None, :] == jnp.arange(recv_slots, dtype=jnp.int32)[:, None]
-    source_of = slots + jnp.sum(jnp.where(match, slot_iota[None, :] - slots, 0), axis=1)
-    relocated_keys = migrate(paged_keys, source_of, blocks, capacity)
-    relocated_values = migrate(paged_values, source_of, blocks, capacity)
-
-    target = jnp.sum(
-        jnp.where(
-            jnp.arange(pages_per_seq, dtype=jnp.int32)[None, :] == cache_len[:, None] // page,
-            page_table,
-            0,
-        ),
-        axis=1,
-    )
-    all_dest = move_dest[:, 0]
-    all_slots = jnp.arange(all_dest.shape[0], dtype=jnp.int32)
-    target_dest = jnp.sum(
-        jnp.where(all_slots[None, :] == target[:, None], all_dest[None, :], 0), axis=1
-    )
-    target_rank = jnp.sum(
-        (
-            (all_slots[None, :] // slots == target[:, None] // slots)
-            & (all_slots[None, :] < target[:, None])
-            & (all_dest[None, :] == target_dest[:, None])
-        ).astype(jnp.int32),
-        axis=1,
-    )
-    arrival = target // slots * capacity + target_rank
-    flat_pos = jnp.where(
-        target_dest == device, arrival * page + cache_len % page, recv_slots * page
-    )
-    fresh_keys = every[:, groups * head : (groups + 1) * head]
-    fresh_values = every[:, (groups + 1) * head :]
-    relocated_keys = patch(relocated_keys, flat_pos, fresh_keys)
-    relocated_values = patch(relocated_values, flat_pos, fresh_values)
+    out_rows = exchange(out_rows)
+    out_rows, values_send = tie(out_rows, values_send)
+    out_hidden = out_rows.reshape(requests, model).astype(F32)
+    moved = (recv_slots, page, head)
+    relocated_keys = call(
+        copy_body,
+        jax.ShapeDtypeStruct(moved, BF16),
+        1,
+        0,
+        8 * slots * page * head,
+    )(relocated_keys.reshape(moved))
+    relocated_values = exchange(values_send).reshape(moved)
     return (out_hidden, relocated_keys, relocated_values)
 
 

time: 273 us -> 251 us (0.919)
  blocking collectives: 72.5 us -> 41 us
  waiting for transfers between devices: 94.4 us -> 121 us
  local copies, waits for them, and re-layouts: 29 us -> 14.6 us
    all_to_all x5 -> x6, waiting for transfers between devices: 47.3 us -> 118 us  [exchange(): return lax.all_to_all(x, 'blk', split_axis=0, concat_axis=0, tiled=True)]
    all_to_all x1 -> x0, blocking collectives: 57.3 us -> none  [migrate(): got = lax.all_to_all(send, 'blk', split_axis=0, concat_axis=0, tiled=True)]
    all_to_all x1 -> x0, waiting for transfers between devices: 45.2 us -> none  [migrate(): got = lax.all_to_all(send, 'blk', split_axis=0, concat_axis=0, tiled=True)]
    all_to_all x1 -> x2, blocking collectives: 15.1 us -> 41 us  [exchange(): return lax.all_to_all(x, 'blk', split_axis=0, concat_axis=0, tiled=True)]
    pallas_call x0 -> x3, Pallas kernels: none -> 9.5 us  [the longest x2 8.04 us: sends(): pl.pallas_call(functools.partial(send_body, tile), out_shape=jax.ShapeDty...]
    all_to_all x5 -> x6, starting transfers between devices: 36.8 us -> 43.6 us  [exchange(): return lax.all_to_all(x, 'blk', split_axis=0, concat_axis=0, tiled=True)]
    scatter x2 -> x0, local copies, waits for them, and re-layouts: 6.21 us -> none  [patch(): pages.reshape(count * page, width).at[flat_pos].set(rows, mode='drop')]
    all_to_all x1 -> x0, starting transfers between devices: 5.95 us -> none  [migrate(): got = lax.all_to_all(send, 'blk', split_axis=0, concat_axis=0, tiled=True)]
  transfers between devices with their start and end apart: 9 -> 9, of which waited for: 8 -> 8; matrix products, arithmetic and copies ran while one was open for 9% -> 4% of each run, Pallas kernels for 0% -> 4%
where the time goes in v5:
time: 251 us; the launch traced here: 250 us
  waiting for transfers between devices  121 us (48%)
  starting transfers between devices  47.4 us (19%)
  blocking collectives  41 us (16%)
  Pallas kernels  15.2 us (6%)
  local copies, waits for them, and re-layouts  14.6 us (6%)
  other arithmetic  8.27 us (3%)
    all_to_all x6, waiting for transfers between devices, exchange(): return lax.all_to_all(x, 'blk', split_axis=0, concat_axis=0, tiled=True)  118 us
    all_to_all x6, starting transfers between devices, exchange(): return lax.all_to_all(x, 'blk', split_axis=0, concat_axis=0, tiled=True)  43.6 us
    all_to_all x2, blocking collectives, exchange(): return lax.all_to_all(x, 'blk', split_axis=0, concat_axis=0, tiled=True)  41 us
    unnamed x32, local copies, waits for them, and re-layouts  10.8 us
    pallas_call x2, Pallas kernels, sends(): pl.pallas_call(functools.partial(send_body, tile), out_shape=jax.ShapeDty...  8.04 us
  transfers between devices with their start and end apart: 9, of which 8 were waited for; matrix products, arithmetic and copies ran while one was open for 4% of the time, Pallas kernels for 4%

profile of v5, /device:TPU:1, one launch (start us, length us, event | category | flops | bytes accessed | tf_op | source)
XLA Modules:
  0.0 249.5 jit_solution(4633682257795500759)
XLA Ops:
  0.7 1.3 multiply_reduce_fusion
  2.0 0.8 dynamic_slice.18
  2.8 1.0 fusion
  3.8 0.7 copy.21
  4.4 13.0 %all-to-all-start = ((bf16[64,8,128]{2,1,0:T(8,128)(2,1)}), bf16[64,8,128]{2,1,0:T(8,128)(2,1)S(1)}, u32[]{:S(2)}, u32[]{:S(2)}) async-start(bf16[64,8,128]{2,1,0:T(8,128)(2,1)} %bitcast.15), calls=%async_computation | async-start | bytes 262144 | tf_op jit(solution)/shard_map/all_to_all | solution.py:40
  17.4 1.2 dynamic_slice.19
  19.3 0.7 fusion.6
  20.2 0.7 and_select_fusion.1
  20.9 1.1 select_reduce_fusion.1
  22.0 0.7 subtract_clamp_fusion
  22.8 2.1 select_reduce_fusion
  25.0 0.7 broadcast_multiply_fusion
  25.7 2.1 all-to-all-done.terms_ref
  27.8 0.7 copy-done.10
  28.5 0.7 copy-done.11
  29.1 0.8 shard_map.193
  30.0 8.3 %all-to-all-start.1 = ((bf16[64,8,128]{2,1,0:T(8,128)(2,1)}), bf16[64,8,128]{2,1,0:T(8,128)(2,1)S(1)}, u32[]{:S(2)}, u32[]{:S(2)}) async-start(bf16[64,8,128]{2,1,0:T(8,128)(2,1)} %get-tuple-element.13), calls=%async_computation.1 | async-start | bytes 262144 | tf_op jit(solution)/shard_map/all_to_all | solution.py:40
  38.4 0.5 broadcast_add_fusion.1.source_ref
  38.9 9.7 %all-to-all-done.1.fresh_ref = bf16[64,8,128]{2,1,0:T(8,128)(2,1)S(1)} async-done(((bf16[64,8,128]{2,1,0:T(8,128)(2,1)}), bf16[64,8,128]{2,1,0:T(8,128)(2,1)S(1)}, u32[]{:S(2)}, u32[]{:S(2)}) %all-to-all-start.1) | async-done | bytes 131104 | tf_op jit(solution)/shard_map/all_to_all | solution.py:40
  48.7 1.8 shard_map.194
  50.5 0.7 copy.23
  51.2 4.9 %all-to-all-start.2 = ((bf16[64,8,128]{2,1,0:T(8,128)(2,1)}), bf16[64,8,128]{2,1,0:T(8,128)(2,1)S(1)}, u32[]{:S(2)}, u32[]{:S(2)}) async-start(bf16[64,8,128]{2,1,0:T(8,128)(2,1)} %bitcast.19), calls=%async_computation.2 | async-start | bytes 262144 | tf_op jit(solution)/shard_map/all_to_all | solution.py:40
  56.3 0.6 broadcast_add_fusion.fresh_at_ref
  56.8 4.0 %shard_map.195 = bf16[128,32,256]{2,1,0:T(8,128)(2,1)} custom-call(s32[128]{0:T(128)} %broadcast_add_fusion.1.source_ref, s32[64]{0:T(128)} %broadcast_add_fusion.fresh_at_ref, bf16[64,8,128]{2,1,0:T(8,128)(2,1)} %copy-done.12, bf16[64,32,256]{2,1,0:T(8,128)(2,1)} %pages_ref.2), custom_call_target="tpu_custom_call" | custom-call | bytes 3145728 | tf_op jit(solution)/shard_map/pallas_call | solution.py:291
  60.8 5.6 %all-to-all-done.2.parts_ref = bf16[64,8,128]{2,1,0:T(8,128)(2,1)S(1)} async-done(((bf16[64,8,128]{2,1,0:T(8,128)(2,1)}), bf16[64,8,128]{2,1,0:T(8,128)(2,1)S(1)}, u32[]{:S(2)}, u32[]{:S(2)}) %all-to-all-start.2) | async-done | bytes 131104 | tf_op jit(solution)/shard_map/all_to_all | solution.py:40
  66.4 4.9 %all-to-all-start.3 = ((bf16[64,2,32,256]{3,2,1,0:T(8,128)(2,1)}), bf16[64,2,32,256]{3,2,1,0:T(8,128)(2,1)S(1)}, u32[]{:S(2)}, u32[]{:S(2)}) async-start(bf16[64,2,32,256]{3,2,1,0:T(8,128)(2,1)} %bitcast.48), calls=%async_computation.3 | async-start | bytes 4194304 | tf_op jit(solution)/shard_map/all_to_all | solution.py:40
  71.3 1.7 copy-done.3
  73.1 0.9 shard_map.196.refs_0_
  74.0 2.7 %collective-permute-start.2 = (f32[20,128]{1,0:T(8,128)S(1)}, f32[20,128]{1,0:T(8,128)S(1)}, u32[]{:S(2)}, u32[]{:S(2)}) collective-permute-start(f32[20,128]{1,0:T(8,128)S(1)} %shard_map.196.refs_0_), channel_id=1, source_target_pairs={{0,192},{64,0},{128,64},{192,128},{1,193},{65,1},{129,65},{193,129... | collective-permute-start | bytes 30728 | tf_op jit(solution)/shard_map/ppermute | solution.py:330
  76.7 0.3 collective-permute-start.1
  77.1 0.7 collective-permute-start
  77.8 0.8 dynamic-slice_reduce_fusion
  78.6 2.5 collective-permute-done.1.refs_2_
  81.4 41.1 %all-to-all-done.3 = bf16[64,2,32,256]{3,2,1,0:T(8,128)(2,1)S(1)} async-done(((bf16[64,2,32,256]{3,2,1,0:T(8,128)(2,1)}), bf16[64,2,32,256]{3,2,1,0:T(8,128)(2,1)S(1)}, u32[]{:S(2)}, u32[]{:S(2)}) %all-to-all-start.3) | async-done | bytes 2097184 | tf_op jit(solution)/shard_map/all_to_all | solution.py:40
  122.6 20.2 %all_to_all.40 = bf16[64,20,128]{2,1,0:T(8,128)(2,1)S(1)} all-to-all(bf16[64,20,128]{2,1,0:T(8,128)(2,1)S(1)} %get-tuple-element.18), channel_id=1, replica_groups=mesh['kv'=4,'blk'=64] {'blk'}, dimensions={0} | all-to-all | bytes 655360 | tf_op jit(solution)/shard_map/all_to_all | solution.py:40
  142.9 1.1 copy-done.5
  144.0 1.1 copy-done.6
  145.1 0.9 shard_map.198
  146.3 20.8 %all_to_all.41.terms_ref = bf16[64,20,128]{2,1,0:T(8,128)(2,1)S(1)} all-to-all(bf16[64,20,128]{2,1,0:T(8,128)(2,1)S(1)} %reshape.191), channel_id=1, replica_groups=mesh['kv'=4,'blk'=64] {'blk'}, dimensions={0} | all-to-all | bytes 655360 | tf_op jit(solution)/shard_map/all_to_all | solution.py:40
  167.1 1.0 shard_map.199
  168.1 6.2 %all-to-all-start.6 = ((bf16[64,20,128]{2,1,0:T(8,128)(2,1)}), bf16[64,20,128]{2,1,0:T(8,128)(2,1)S(1)}, u32[]{:S(2)}, u32[]{:S(2)}) async-start(bf16[64,20,128]{2,1,0:T(8,128)(2,1)} %shard_map.199), calls=%async_computation.6 | async-start | bytes 786432 | tf_op jit(solution)/shard_map/all_to_all | solution.py:40
  174.3 4.0 %shard_map.200 = bf16[128,32,256]{2,1,0:T(8,128)(2,1)} custom-call(s32[128]{0:T(128)} %broadcast_add_fusion.1.source_ref, s32[64]{0:T(128)} %broadcast_add_fusion.fresh_at_ref, bf16[64,8,128]{2,1,0:T(8,128)(2,1)} %copy-done.12, bf16[64,32,256]{2,1,0:T(8,128)(2,1)} %pages_ref.3), custom_call_target="tpu_custom_call" | custom-call | bytes 3145728 | tf_op jit(solution)/shard_map/pallas_call | solution.py:291
  178.3 10.6 %all-to-all-done.6 = bf16[64,20,128]{2,1,0:T(8,128)(2,1)S(1)} async-done(((bf16[64,20,128]{2,1,0:T(8,128)(2,1)}), bf16[64,20,128]{2,1,0:T(8,128)(2,1)S(1)}, u32[]{:S(2)}, u32[]{:S(2)}) %all-to-all-start.6) | async-done | bytes 327712 | tf_op jit(solution)/shard_map/all_to_all | solution.py:40
  188.9 6.4 %all-to-all-start.7 = ((bf16[64,2,32,256]{3,2,1,0:T(8,128)(2,1)}), bf16[64,2,32,256]{3,2,1,0:T(8,128)(2,1)}, u32[]{:S(2)}, u32[]{:S(2)}) async-start(bf16[64,2,32,256]{3,2,1,0:T(8,128)(2,1)} %bitcast.49), calls=%async_computation.7 | async-start | bytes 4194304 | tf_op jit(solution)/shard_map/all_to_all | solution.py:40
  195.3 1.5 shard_map.201
  196.7 0.9 copy.29
  197.6 48.8 %all-to-all-done.7 = bf16[64,2,32,256]{3,2,1,0:T(8,128)(2,1)} async-done(((bf16[64,2,32,256]{3,2,1,0:T(8,128)(2,1)}), bf16[64,2,32,256]{3,2,1,0:T(8,128)(2,1)}, u32[]{:S(2)}, u32[]{:S(2)}) %all-to-all-start.7) | async-done | bytes 2097184 | tf_op jit(solution)/shard_map/all_to_all | solution.py:40
  246.4 3.1 %copy.33 = bf16[128,32,256]{2,1,0:T(8,128)(2,1)} copy(bf16[128,32,256]{2,1,0:T(8,128)(2,1)} %bitcast.12) | data formatting | bytes 4194304
  (35 shorter events, 1.2 us)
Async XLA Ops:
  0.6 2.1 copy-start
  0.6 48.0 %copy-start.2 = (bf16[64,32,256]{2,1,0:T(8,128)(2,1)S(1)}, bf16[64,32,256]{2,1,0:T(8,128)(2,1)}, u32[]{:S(2)}) copy-start(bf16[64,32,256]{2,1,0:T(8,128)(2,1)} %pages_ref.3) | copy-start | bytes 3145732
  0.7 48.0 %copy-start.1 = (bf16[64,32,256]{2,1,0:T(8,128)(2,1)S(1)}, bf16[64,32,256]{2,1,0:T(8,128)(2,1)}, u32[]{:S(2)}) copy-start(bf16[64,32,256]{2,1,0:T(8,128)(2,1)} %pages_ref.2) | copy-start | bytes 3145732
  4.4 23.4 %all-to-all-start = ((bf16[64,8,128]{2,1,0:T(8,128)(2,1)}), bf16[64,8,128]{2,1,0:T(8,128)(2,1)S(1)}, u32[]{:S(2)}, u32[]{:S(2)}) async-start(bf16[64,8,128]{2,1,0:T(8,128)(2,1)} %bitcast.15), calls=%async_computation | async-start | bytes 262144 | tf_op jit(solution)/shard_map/all_to_all | solution.py:40
  27.8 0.7 copy-start.10
  28.5 0.7 copy-start.11
  30.0 18.6 %all-to-all-start.1 = ((bf16[64,8,128]{2,1,0:T(8,128)(2,1)}), bf16[64,8,128]{2,1,0:T(8,128)(2,1)S(1)}, u32[]{:S(2)}, u32[]{:S(2)}) async-start(bf16[64,8,128]{2,1,0:T(8,128)(2,1)} %get-tuple-element.13), calls=%async_computation.1 | async-start | bytes 262144 | tf_op jit(solution)/shard_map/all_to_all | solution.py:40
  48.6 8.2 %copy-start.12 = (bf16[64,8,128]{2,1,0:T(8,128)(2,1)}, bf16[64,8,128]{2,1,0:T(8,128)(2,1)S(1)}, u32[]{:S(2)}) copy-start(bf16[64,8,128]{2,1,0:T(8,128)(2,1)S(1)} %all-to-all-done.1.fresh_ref) | copy-start | bytes 393220
  51.2 15.2 %all-to-all-start.2 = ((bf16[64,8,128]{2,1,0:T(8,128)(2,1)}), bf16[64,8,128]{2,1,0:T(8,128)(2,1)S(1)}, u32[]{:S(2)}, u32[]{:S(2)}) async-start(bf16[64,8,128]{2,1,0:T(8,128)(2,1)} %bitcast.19), calls=%async_computation.2 | async-start | bytes 262144 | tf_op jit(solution)/shard_map/all_to_all | solution.py:40
  66.4 56.1 %all-to-all-start.3 = ((bf16[64,2,32,256]{3,2,1,0:T(8,128)(2,1)}), bf16[64,2,32,256]{3,2,1,0:T(8,128)(2,1)S(1)}, u32[]{:S(2)}, u32[]{:S(2)}) async-start(bf16[64,2,32,256]{3,2,1,0:T(8,128)(2,1)} %bitcast.48), calls=%async_computation.3 | async-start | bytes 4194304 | tf_op jit(solution)/shard_map/all_to_all | solution.py:40
  71.3 1.7 copy-start.3
  73.1 8.1 %copy-start.7 = (f32[2560]{0:T(1024)S(1)}, f32[2560]{0:T(1024)}, u32[]{:S(2)}) copy-start(f32[2560]{0:T(1024)} %param.30) | copy-start | bytes 30724
  73.1 8.1 %copy-start.8 = (f32[2560]{0:T(1024)S(1)}, f32[2560]{0:T(1024)}, u32[]{:S(2)}) copy-start(f32[2560]{0:T(1024)} %param.31) | copy-start | bytes 30724
  73.1 69.8 %copy-start.4 = (bf16[2560,160]{0,1:T(8,128)(2,1)S(1)}, bf16[2560,160]{0,1:T(8,128)(2,1)}, u32[]{:S(2)}) copy-start(bf16[2560,160]{0,1:T(8,128)(2,1)} %param.33) | copy-start | bytes 2457604
  74.0 4.6 %collective-permute-start.2 = (f32[20,128]{1,0:T(8,128)S(1)}, f32[20,128]{1,0:T(8,128)S(1)}, u32[]{:S(2)}, u32[]{:S(2)}) collective-permute-start(f32[20,128]{1,0:T(8,128)S(1)} %shard_map.196.refs_0_), channel_id=1, source_target_pairs={{0,192},{64,0},{128,64},{192,128},{1,193},{65,1},{129,65},{193,129... | collective-permute-start | bytes 30728 | tf_op jit(solution)/shard_map/ppermute | solution.py:330
  76.7 4.3 %collective-permute-start.1 = (f32[20,128]{1,0:T(8,128)S(1)}, f32[20,128]{1,0:T(8,128)S(1)}, u32[]{:S(2)}, u32[]{:S(2)}) collective-permute-start(f32[20,128]{1,0:T(8,128)S(1)} %shard_map.196.refs_0_), channel_id=1, source_target_pairs={{0,128},{64,192},{128,0},{192,64},{1,129},{65,193},{129,1},{193,65... | collective-permute-start | bytes 30728 | tf_op jit(solution)/shard_map/ppermute | solution.py:330
  77.1 4.1 %collective-permute-start = (f32[20,128]{1,0:T(8,128)S(1)}, f32[20,128]{1,0:T(8,128)S(1)}, u32[]{:S(2)}, u32[]{:S(2)}) collective-permute-start(f32[20,128]{1,0:T(8,128)S(1)} %shard_map.196.refs_0_), channel_id=1, source_target_pairs={{0,64},{64,128},{128,192},{192,0},{1,65},{65,129},{129,193},{193,1... | collective-permute-start | bytes 30728 | tf_op jit(solution)/shard_map/ppermute | solution.py:330
  142.8 1.1 copy-start.5
  144.0 1.1 copy-start.6
  145.1 21.9 %copy-start.9 = (f32[2560]{0:T(1024)S(1)}, f32[2560]{0:T(1024)}, u32[]{:S(2)}) copy-start(f32[2560]{0:T(1024)} %param.32) | copy-start | bytes 30724
  168.1 20.8 %all-to-all-start.6 = ((bf16[64,20,128]{2,1,0:T(8,128)(2,1)}), bf16[64,20,128]{2,1,0:T(8,128)(2,1)S(1)}, u32[]{:S(2)}, u32[]{:S(2)}) async-start(bf16[64,20,128]{2,1,0:T(8,128)(2,1)} %shard_map.199), calls=%async_computation.6 | async-start | bytes 786432 | tf_op jit(solution)/shard_map/all_to_all | solution.py:40
  188.9 57.6 %all-to-all-start.7 = ((bf16[64,2,32,256]{3,2,1,0:T(8,128)(2,1)}), bf16[64,2,32,256]{3,2,1,0:T(8,128)(2,1)}, u32[]{:S(2)}, u32[]{:S(2)}) async-start(bf16[64,2,32,256]{3,2,1,0:T(8,128)(2,1)} %bitcast.49), calls=%async_computation.7 | async-start | bytes 4194304 | tf_op jit(solution)/shard_map/all_to_all | solution.py:40

commit v6 on v4

--- a/solution.py
+++ b/solution.py
@@ -198,43 +198,34 @@
         pltpu.make_async_copy(held.at[j], out, out_sem.at[j]).wait()
 
 
-def assemble_body(counts, cap, place_ref, arrive_ref, fresh_ref, *refs):
-    arrays = len(counts)
-    chunks, outs = refs[: sum(counts)], refs[sum(counts) : -3]
+def place_body(cap, tile, place_ref, arrive_ref, fresh_ref, *refs):
+    chunks, out = refs[:-4], refs[-4]
     held, in_sem, out_sem = refs[-3:]
-    page = outs[0].shape[1]
-    requests, tiles = fresh_ref.shape[:2]
-    first = 0
-    for p in range(arrays):
-        inner = chunks[first].shape[0] // cap
-        for j in range(counts[p]):
-            for i in range(inner):
-                at = place_ref[p, j * inner + i] * cap
-                pltpu.make_async_copy(
-                    chunks[first + j].at[i * cap : (i + 1) * cap],
-                    held.at[p, pl.ds(at, cap)],
-                    in_sem.at[p],
-                ).start()
-        first += counts[p]
-    for p, out in enumerate(outs):
-        pltpu.make_async_copy(out, held.at[p], in_sem.at[p]).wait()
-
-        @pl.loop(0, requests)
-        def _(r, p=p):
-            where = arrive_ref[r]
-
-            @pl.when(where >= 0)
-            def _():
-                at = tiles - 2 * arrays + 2 * p
-                new = fresh_ref[r].astype(F32)
-                row = jnp.concatenate([new[at : at + 1], new[at + 1 : at + 2]], axis=1)
-                old = held[p, where // page].astype(F32)
-                here = lax.broadcasted_iota(jnp.int32, old.shape, 0) == where % page
-                held[p, where // page] = jnp.where(here, row, old).astype(BF16)
-
-        pltpu.make_async_copy(held.at[p], out, out_sem.at[p]).start()
-    for p, out in enumerate(outs):
-        pltpu.make_async_copy(held.at[p], out, out_sem.at[p]).wait()
+    page = out.shape[1]
+    inner = chunks[0].shape[0] // cap
+    for j, chunk in enumerate(chunks):
+        for i in range(inner):
+            at = place_ref[j * inner + i] * cap
+            pltpu.make_async_copy(
+                chunk.at[i * cap : (i + 1) * cap], held.at[pl.ds(at, cap)], in_sem
+            ).start()
+    pltpu.make_async_copy(out, held, in_sem).wait()
+
+    @pl.loop(0, fresh_ref.shape[0])
+    def _(r):
+        where = arrive_ref[r]
+
+        @pl.when(where >= 0)
+        def _():
+            new = fresh_ref[r].astype(F32)
+            row = jnp.concatenate([new[tile : tile + 1], new[tile + 1 : tile + 2]], axis=1)
+            old = held[where // page].astype(F32)
+            here = lax.broadcasted_iota(jnp.int32, old.shape, 0) == where % page
+            held[where // page] = jnp.where(here, row, old).astype(BF16)
+
+    copy = pltpu.make_async_copy(held, out, out_sem)
+    copy.start()
+    copy.wait()
 
 
 def local(
@@ -322,7 +313,6 @@
             cost_estimate=pl.CostEstimate(
                 flops=0, bytes_accessed=6 * slots * page * head, transcendentals=0
             ),
-compiler_params=PARAMS,
         )(source_of, pages)
 
     def regroup(chunks, count):
@@ -339,7 +329,6 @@
             cost_estimate=pl.CostEstimate(
                 flops=0, bytes_accessed=8 * slots * page * head, transcendentals=0
             ),
-compiler_params=PARAMS,
         )(*chunks)
 
     dest = lax.dynamic_slice_in_dim(move_dest[:, 0], device * slots, slots)
@@ -389,7 +378,6 @@
     keys_first = permutes(sends[:near], to_near)
     values_first = permutes(sends[near:], to_along)
     every = exchange(every)
-    every = due(every, (values_first, (4, 1)), (keys_first, (4, 2, 6)))
 
     slot_ids = device * slots + jnp.arange(slots, dtype=jnp.int32)
     page_starts = jnp.arange(pages_per_seq, dtype=jnp.int32) * page
@@ -405,8 +393,7 @@
         4 * slots * page * head,
     )(every.reshape(requests, columns), paged_keys, paged_values, limit)
     parts = exchange(parts.reshape(requests, col_tiles, LANES))
-    parts = due(parts, (values_first, (3, 5)), (keys_first, (5, 3, 7, 1)))
-    keys_sends = regroup(keys_first, depth)
+    parts = due(parts, (values_first, (3, 5)), (keys_first, (2, 6, 4)))
     attn_terms = call(
         functools.partial(merge_body, groups),
         jax.ShapeDtypeStruct((kv_size, model_tiles, LANES), F32),
@@ -416,10 +403,7 @@
     )(parts, own, output_proj)
 
     attn_terms = lax.all_to_all(attn_terms, "kv", split_axis=0, concat_axis=0, tiled=True)
-    attn_terms = due(attn_terms, (values_first, (2, 6, 7)))
-    attn_terms, keys_sends = tie(attn_terms, keys_sends)
-    keys_second = permutes(keys_sends, to_along)
-    values_sends = regroup(values_first, near)
+    attn_terms = due(attn_terms, (values_first, (1, 7, 4)), (keys_first, (3, 7)))
     wide = (model_tiles, LANES)
     residual, ffw_in = call(
         residual_body,
@@ -437,9 +421,7 @@
         ffw_gain.reshape(wide),
     )
     ffw_in = exchange(ffw_in).reshape(requests, model)
-    ffw_in = due(ffw_in, (keys_second, (2, 6)))
-    ffw_in, values_sends = tie(ffw_in, values_sends)
-    values_second = permutes(values_sends, to_near)
+    ffw_in = due(ffw_in, (values_first, (2, 6)), (keys_first, (5, 1)))
     units = gate_weight.shape[1]
     ffw_terms = call(
         ffw_body,
@@ -448,8 +430,12 @@
         6 * requests * units * model,
         6 * units * model,
     )(ffw_in, gate_weight.T, up_weight.T, down_weight)
+    ffw_terms, *arrived = tie(ffw_terms, *keys_first, *values_first)
+    keys_sends = regroup(arrived[:near], depth)
+    keys_second = permutes(keys_sends, to_along)
+    _, *arrived = tie(keys_sends[0], *arrived[near:])
+    values_second = permutes(regroup(arrived, near), to_near)
     ffw_terms = exchange(ffw_terms.reshape((requests,) + wide))
-    ffw_terms = due(ffw_terms, (keys_second, (3, 5)), (values_second, (4, 2, 6)))
     out_rows = call(
         output_body,
         jax.ShapeDtypeStruct((requests,) + wide, BF16),
@@ -490,28 +476,35 @@
             across - near_step // cores, along - along_step, core ^ (near_step % cores)
         ).reshape(-1)
 
-    place = jnp.stack(
-        [
-            source_index(back_along[:, None], back_near[None, :]),
-            source_index(back_along[None, :], back_near[:, None]),
-        ]
-    )
-    moved = jax.ShapeDtypeStruct((recv_slots, page, head), BF16)
-    relocated_keys, relocated_values = pl.pallas_call(
-        functools.partial(assemble_body, (depth, near), capacity),
-        out_shape=[moved] * 2,
-        in_specs=[smem, smem, vmem] + [anywhere] * (depth + near),
-        out_specs=[anywhere] * 2,
-        scratch_shapes=[
-            pltpu.VMEM((2, recv_slots, page, head), BF16),
-            pltpu.SemaphoreType.DMA((2,)),
-            pltpu.SemaphoreType.DMA((2,)),
-        ],
-        cost_estimate=pl.CostEstimate(
-            flops=0, bytes_accessed=16 * slots * page * head, transcendentals=0
-        ),
-compiler_params=PARAMS,
-    )(place, arrive, every, *keys_second, *values_second)
+    def place(chunks, places, tile):
+        return pl.pallas_call(
+            functools.partial(place_body, capacity, tile),
+            out_shape=jax.ShapeDtypeStruct((recv_slots, page, head), BF16),
+            in_specs=[smem, smem, vmem] + [anywhere] * len(chunks),
+            out_specs=anywhere,
+            scratch_shapes=[
+                pltpu.VMEM((recv_slots, page, head), BF16),
+                pltpu.SemaphoreType.DMA,
+                pltpu.SemaphoreType.DMA,
+            ],
+            cost_estimate=pl.CostEstimate(
+                flops=0, bytes_accessed=8 * slots * page * head, transcendentals=0
+            ),
+        )(places, arrive, every, *chunks)
+
+    by_along = (0, 3, 5, 4, 2, 6, 1, 7)
+    by_near = (0, 4, 5, 2, 6, 3, 7, 1)
+    relocated_keys = place(
+        [keys_second[k] for k in by_along],
+        source_index(jnp.array(by_along, jnp.int32)[:, None], back_near[None, :]),
+        2 * groups,
+    )
+    relocated_keys, *values_second = tie(relocated_keys, *values_second)
+    relocated_values = place(
+        [values_second[k] for k in by_near],
+        source_index(back_along[None, :], jnp.array(by_near, jnp.int32)[:, None]),
+        2 * groups + 2,
+    )
     return (out_hidden, relocated_keys, relocated_values)
 
 

time: 238 us -> 226 us (0.950)
  local copies, waits for them, and re-layouts: 36.9 us -> 13 us
  starting transfers between devices: 113 us -> 126 us
    unnamed x123 -> x83, local copies, waits for them, and re-layouts: 32.2 us -> 7.21 us
    all_to_all x6, starting transfers between devices: 48.9 us -> 55.8 us  [exchange(): return lax.all_to_all(x, 'blk', split_axis=0, concat_axis=0, tiled=True)]
    ppermute x28, starting transfers between devices: 59.9 us -> 66.3 us  [permutes(): lax.ppermute(sends[k], 'blk', targets[k])]
    ppermute x28, waiting for transfers between devices: 45.4 us -> 39 us  [permutes(): lax.ppermute(sends[k], 'blk', targets[k])]
    all_to_all x6, waiting for transfers between devices: 5.41 us -> 9.25 us  [exchange(): return lax.all_to_all(x, 'blk', split_axis=0, concat_axis=0, tiled=True)]
    pallas_call x1 -> x2, Pallas kernels: 9.58 us -> 7.48 us  [place(): pl.pallas_call(functools.partial(place_body, capacity, tile), out_shape=j...]
  transfers between devices with their start and end apart: 35 -> 35, of which waited for: 8 -> 12; matrix products, arithmetic and copies ran while one was open for 4% -> 5% of each run, Pallas kernels for 9% -> 10%
where the time goes in v6:
time: 226 us; the launch traced here: 224 us
  starting transfers between devices  126 us (56%)
  waiting for transfers between devices  49.3 us (22%)
  Pallas kernels  25.5 us (11%)
  local copies, waits for them, and re-layouts  13 us (6%)
  other arithmetic  6.63 us (3%)
    ppermute x28, starting transfers between devices, permutes(): lax.ppermute(sends[k], 'blk', targets[k])  66.3 us
    all_to_all x6, starting transfers between devices, exchange(): return lax.all_to_all(x, 'blk', split_axis=0, concat_axis=0, tiled=True)  55.8 us
    ppermute x28, waiting for transfers between devices, permutes(): lax.ppermute(sends[k], 'blk', targets[k])  39 us
    all_to_all x6, waiting for transfers between devices, exchange(): return lax.all_to_all(x, 'blk', split_axis=0, concat_axis=0, tiled=True)  9.25 us
    pallas_call x2, Pallas kernels, place(): pl.pallas_call(functools.partial(place_body, capacity, tile), out_shape=j...  7.48 us
    unnamed x83, local copies, waits for them, and re-layouts  7.21 us
    pallas_call x2, Pallas kernels, gather(): pl.pallas_call(gather_body, out_shape=buffers(count), in_specs=[smem, vme...  6.13 us
    pallas_call x2, Pallas kernels, regroup(): pl.pallas_call(functools.partial(regroup_body, len(chunks)), out_shape=bu...  4.76 us
  transfers between devices with their start and end apart: 35, of which 12 were waited for; matrix products, arithmetic and copies ran while one was open for 5% of the time, Pallas kernels for 10%

profile of v6, /device:TPU:1, one launch (start us, length us, event | category | flops | bytes accessed | tf_op | source)
XLA Modules:
  0.0 223.6 jit_solution(12323332284805133822)
XLA Ops:
  4.5 13.0 %all-to-all-start = ((bf16[64,8,128]{2,1,0:T(8,128)(2,1)}), bf16[64,8,128]{2,1,0:T(8,128)(2,1)S(1)}, u32[]{:S(2)}, u32[]{:S(2)}) async-start(bf16[64,8,128]{2,1,0:T(8,128)(2,1)} %bitcast.12), calls=%async_computation | async-start | bytes 262144 | tf_op jit(solution)/shard_map/all_to_all | solution.py:40
  22.5 3.0 %shard_map.211 = (bf16[16,32,256]{2,1,0:T(8,128)(2,1)}, bf16[16,32,256]{2,1,0:T(8,128)(2,1)}, bf16[16,32,256]{2,1,0:T(8,128)(2,1)}, bf16[16,32,256]{2,1,0:T(8,12...) custom-call(s32[128]{0:T(128)} %broadcast_add_fusion.1.source_ref, ...), custom_call_target="tpu_custom_call" | custom-call | bytes 3145728 | tf_op jit(solution)/shard_map/pallas_call | solution.py:308
  25.5 3.1 %shard_map.212 = (bf16[16,32,256]{2,1,0:T(8,128)(2,1)}, bf16[16,32,256]{2,1,0:T(8,128)(2,1)}, bf16[16,32,256]{2,1,0:T(8,128)(2,1)}, bf16[16,32,256]{2,1,0:T(8,12...) custom-call(s32[128]{0:T(128)} %broadcast_add_fusion.source_ref, ...), custom_call_target="tpu_custom_call" | custom-call | bytes 3145728 | tf_op jit(solution)/shard_map/pallas_call | solution.py:308
  29.6 10.3 %all-to-all-start.1 = ((bf16[64,8,128]{2,1,0:T(8,128)(2,1)}), bf16[64,8,128]{2,1,0:T(8,128)(2,1)S(1)}, u32[]{:S(2)}, u32[]{:S(2)}) async-start(bf16[64,8,128]{2,1,0:T(8,128)(2,1)} %get-tuple-element.158), calls=%async_computation.1 | async-start | bytes 262144 | tf_op jit(solution)/shard_map/all_to_all | solution.py:40
  39.9 3.3 %collective-permute-start = (bf16[16,32,256]{2,1,0:T(8,128)(2,1)}, bf16[16,32,256]{2,1,0:T(8,128)(2,1)}, u32[]{:S(2)}, u32[]{:S(2)}) collective-permute-start(bf16[16,32,256]{2,1,0:T(8,128)(2,1)} %get-tuple-element.159), channel_id=1, source_target_pairs={{0,6},{1,7},{2,8},{3,9},{4,10},{5,11},{6,12},{7,13},{8,14},{9,15},... | collective-permute-start | bytes 786440 | tf_op jit(solution)/shard_map/ppermute | solution.py:346
  44.5 1.4 collective-permute-start.2
  45.9 1.4 collective-permute-start.3
  47.3 1.6 collective-permute-start.4
  50.2 1.6 all-to-all-done.1.fresh_ref
  51.9 1.9 shard_map.214
  54.5 8.5 %all-to-all-start.2 = ((bf16[64,8,128]{2,1,0:T(8,128)(2,1)}), bf16[64,8,128]{2,1,0:T(8,128)(2,1)S(1)}, u32[]{:S(2)}, u32[]{:S(2)}) async-start(bf16[64,8,128]{2,1,0:T(8,128)(2,1)} %bitcast.16), calls=%async_computation.2 | async-start | bytes 262144 | tf_op jit(solution)/shard_map/all_to_all | solution.py:40
  63.0 1.5 collective-permute-start.5
  64.5 1.7 collective-permute-start.6
  66.2 4.9 %collective-permute-start.7 = (bf16[16,32,256]{2,1,0:T(8,128)(2,1)}, bf16[16,32,256]{2,1,0:T(8,128)(2,1)S(1)}, u32[]{:S(2)}, u32[]{:S(2)}) collective-permute-start(bf16[16,32,256]{2,1,0:T(8,128)(2,1)} %get-tuple-element.168), channel_id=1, source_target_pairs={{0,8},{1,9},{2,10},{3,11},{4,12},{5,13},{6,14},{7,15},{8,0},{9,1},... | collective-permute-start | bytes 786440 | tf_op jit(solution)/shard_map/ppermute | solution.py:346
  71.1 2.3 %collective-permute-start.8 = (bf16[16,32,256]{2,1,0:T(8,128)(2,1)}, bf16[16,32,256]{2,1,0:T(8,128)(2,1)S(1)}, u32[]{:S(2)}, u32[]{:S(2)}) collective-permute-start(bf16[16,32,256]{2,1,0:T(8,128)(2,1)} %get-tuple-element.169), channel_id=1, source_target_pairs={{0,17},{1,16},{2,19},{3,18},{4,21},{5,20},{6,23},{7,22},{8,25},{9,... | collective-permute-start | bytes 786440 | tf_op jit(solution)/shard_map/ppermute | solution.py:346
  73.4 1.5 collective-permute-start.9
  74.9 1.7 copy-done.3
  76.6 1.5 shard_map.215
  78.2 4.2 %all-to-all-start.3 = ((f32[4,20,128]{2,1,0:T(8,128)}), f32[4,20,128]{2,1,0:T(8,128)S(1)}, u32[]{:S(2)}, u32[]{:S(2)}) async-start(f32[4,20,128]{2,1,0:T(8,128)} %shard_map.215), calls=%async_computation.3 | async-start | bytes 98304 | tf_op jit(solution)/shard_map/all_to_all | solution.py:405
  83.4 2.6 %collective-permute-done.7.refs_4_ = bf16[16,32,256]{2,1,0:T(8,128)(2,1)S(1)} collective-permute-done((bf16[16,32,256]{2,1,0:T(8,128)(2,1)}, bf16[16,32,256]{2,1,0:T(8,128)(2,1)S(1)}, u32[]{:S(2)}, u32[]{:S(2)}) %collective-permute-start.7) | collective-permute-done | bytes 262176 | tf_op jit(solution)/shard_map/ppermute | solution.py:346
  88.0 8.9 %all-to-all-start.4 = ((bf16[64,20,128]{2,1,0:T(8,128)(2,1)}), bf16[64,20,128]{2,1,0:T(8,128)(2,1)S(1)}, u32[]{:S(2)}, u32[]{:S(2)}) async-start(bf16[64,20,128]{2,1,0:T(8,128)(2,1)} %get-tuple-element.172), calls=%async_computation.4 | async-start | bytes 786432 | tf_op jit(solution)/shard_map/all_to_all | solution.py:40
  96.9 2.4 %collective-permute-start.10 = (bf16[16,32,256]{2,1,0:T(8,128)(2,1)}, bf16[16,32,256]{2,1,0:T(8,128)(2,1)S(1)}, u32[]{:S(2)}, u32[]{:S(2)}) collective-permute-start(bf16[16,32,256]{2,1,0:T(8,128)(2,1)} %get-tuple-element.173), channel_id=1, source_target_pairs={{0,4},{1,5},{2,6},{3,7},{4,8},{5,9},{6,10},{7,11},{8,12},{9,13},{1... | collective-permute-start | bytes 786440 | tf_op jit(solution)/shard_map/ppermute | solution.py:346
  100.6 3.8 %collective-permute-start.12 = (bf16[16,32,256]{2,1,0:T(8,128)(2,1)}, bf16[16,32,256]{2,1,0:T(8,128)(2,1)S(1)}, u32[]{:S(2)}, u32[]{:S(2)}) collective-permute-start(bf16[16,32,256]{2,1,0:T(8,128)(2,1)} %get-tuple-element.175), channel_id=1, source_target_pairs={{0,33},{1,32},{2,35},{3,34},{4,37},{5,36},{6,39},{7,38},{8,41},{9,... | collective-permute-start | bytes 786440 | tf_op jit(solution)/shard_map/ppermute | solution.py:346
  104.4 7.7 %all-to-all-done.4 = bf16[64,20,128]{2,1,0:T(8,128)(2,1)S(1)} async-done(((bf16[64,20,128]{2,1,0:T(8,128)(2,1)}), bf16[64,20,128]{2,1,0:T(8,128)(2,1)S(1)}, u32[]{:S(2)}, u32[]{:S(2)}) %all-to-all-start.4) | async-done | bytes 327712 | tf_op jit(solution)/shard_map/all_to_all | solution.py:40
  112.1 5.8 %collective-permute-done.10.refs_2_ = bf16[16,32,256]{2,1,0:T(8,128)(2,1)S(1)} collective-permute-done((bf16[16,32,256]{2,1,0:T(8,128)(2,1)}, bf16[16,32,256]{2,1,0:T(8,128)(2,1)S(1)}, u32[]{:S(2)}, u32[]{:S(2)}) %collective-permute-start.10) | collective-permute-done | bytes 262176 | tf_op jit(solution)/shard_map/ppermute | solution.py:346
  117.9 1.5 collective-permute-done.11.refs_6_
  124.4 8.9 %all-to-all-start.5 = ((bf16[64,20,128]{2,1,0:T(8,128)(2,1)}), bf16[64,20,128]{2,1,0:T(8,128)(2,1)S(1)}, u32[]{:S(2)}, u32[]{:S(2)}) async-start(bf16[64,20,128]{2,1,0:T(8,128)(2,1)} %reshape.496), calls=%async_computation.5 | async-start | bytes 786432 | tf_op jit(solution)/shard_map/all_to_all | solution.py:40
  133.6 2.4 %shard_map.219 = (bf16[16,32,256]{2,1,0:T(8,128)(2,1)}, bf16[16,32,256]{2,1,0:T(8,128)(2,1)}, bf16[16,32,256]{2,1,0:T(8,128)(2,1)}, bf16[16,32,256]{2,1,0:T(8,12...) custom-call(bf16[16,32,256]{2,1,0:T(8,128)(2,1)} %get-tuple-element., ...), custom_call_target="tpu_custom_call" | custom-call | bytes 4194304 | tf_op jit(solution)/shard_map/pallas_call | solution.py:319
  136.0 2.4 %shard_map.221 = (bf16[16,32,256]{2,1,0:T(8,128)(2,1)}, bf16[16,32,256]{2,1,0:T(8,128)(2,1)}, bf16[16,32,256]{2,1,0:T(8,128)(2,1)}, bf16[16,32,256]{2,1,0:T(8,12...) custom-call(bf16[16,32,256]{2,1,0:T(8,128)(2,1)} %get-tuple-element., ...), custom_call_target="tpu_custom_call" | custom-call | bytes 4194304 | tf_op jit(solution)/shard_map/pallas_call | solution.py:319
  140.2 3.0 %collective-permute-start.14 = (bf16[16,32,256]{2,1,0:T(8,128)(2,1)}, bf16[16,32,256]{2,1,0:T(8,128)(2,1)S(1)}, u32[]{:S(2)}, u32[]{:S(2)}) collective-permute-start(bf16[16,32,256]{2,1,0:T(8,128)(2,1)} %get-tuple-element.205), channel_id=1, source_target_pairs={{0,6},{1,7},{2,8},{3,9},{4,10},{5,11},{6,12},{7,13},{8,14},{9,15},... | collective-permute-start | bytes 786440 | tf_op jit(solution)/shard_map/ppermute | solution.py:346
  143.2 1.5 collective-permute-start.15
  144.8 5.2 %collective-permute-start.16 = (bf16[16,32,256]{2,1,0:T(8,128)(2,1)}, bf16[16,32,256]{2,1,0:T(8,128)(2,1)S(1)}, u32[]{:S(2)}, u32[]{:S(2)}) collective-permute-start(bf16[16,32,256]{2,1,0:T(8,128)(2,1)} %get-tuple-element.207), channel_id=1, source_target_pairs={{0,8},{1,9},{2,10},{3,11},{4,12},{5,13},{6,14},{7,15},{8,0},{9,1},... | collective-permute-start | bytes 786440 | tf_op jit(solution)/shard_map/ppermute | solution.py:346
  150.9 6.3 %all-to-all-start.6 = ((bf16[64,20,128]{2,1,0:T(8,128)(2,1)}), bf16[64,20,128]{2,1,0:T(8,128)(2,1)S(1)}, u32[]{:S(2)}, u32[]{:S(2)}) async-start(bf16[64,20,128]{2,1,0:T(8,128)(2,1)} %shard_map.218), calls=%async_computation.6 | async-start | bytes 786432 | tf_op jit(solution)/shard_map/all_to_all | solution.py:40
  157.2 2.4 %collective-permute-start.17 = (bf16[16,32,256]{2,1,0:T(8,128)(2,1)S(1)}, bf16[16,32,256]{2,1,0:T(8,128)(2,1)S(1)}, u32[]{:S(2)}, u32[]{:S(2)}) collective-permute-start(bf16[16,32,256]{2,1,0:T(8,128)(2,1)S(1)} %copy-done.37), channel_id=1, source_target_pairs={{0,4},{1,5},{2,6},{3,7},{4,8},{5,9},{6,10},{7,11},{8,12},{9,13},{1... | collective-permute-start | bytes 786440 | tf_op jit(solution)/shard_map/ppermute | solution.py:346
  159.6 1.3 collective-permute-start.18
  160.9 1.3 collective-permute-done.14.refs_1_
  162.7 10.5 %collective-permute-start.20 = (bf16[16,32,256]{2,1,0:T(8,128)(2,1)}, bf16[16,32,256]{2,1,0:T(8,128)(2,1)S(1)}, u32[]{:S(2)}, u32[]{:S(2)}) collective-permute-start(bf16[16,32,256]{2,1,0:T(8,128)(2,1)} %get-tuple-element.211), channel_id=1, source_target_pairs={{0,14},{1,15},{2,0},{3,1},{4,2},{5,3},{6,4},{7,5},{8,6},{9,7},{10,... | collective-permute-start | bytes 786440 | tf_op jit(solution)/shard_map/ppermute | solution.py:346
  173.3 2.0 collective-permute-start.23
  175.3 15.9 %collective-permute-done.17.refs_4_ = bf16[16,32,256]{2,1,0:T(8,128)(2,1)S(1)} collective-permute-done((bf16[16,32,256]{2,1,0:T(8,128)(2,1)S(1)}, bf16[16,32,256]{2,1,0:T(8,128)(2,1)S(1)}, u32[]{:S(2)}, u32[]{:S(2)}) %collective-permute-start.17) | collective-permute-done | bytes 262176 | tf_op jit(solution)/shard_map/ppermute | solution.py:346
  191.2 3.1 %collective-permute-start.24 = (bf16[16,32,256]{2,1,0:T(8,128)(2,1)}, bf16[16,32,256]{2,1,0:T(8,128)(2,1)S(1)}, u32[]{:S(2)}, u32[]{:S(2)}) collective-permute-start(bf16[16,32,256]{2,1,0:T(8,128)(2,1)} %get-tuple-element.232), channel_id=1, source_target_pairs={{0,32},{1,33},{2,34},{3,35},{4,36},{5,37},{6,38},{7,39},{8,40},{9,... | collective-permute-start | bytes 786440 | tf_op jit(solution)/shard_map/ppermute | solution.py:346
  194.3 1.5 collective-permute-done.18.refs_5_
  195.8 3.1 %collective-permute-start.25 = (bf16[16,32,256]{2,1,0:T(8,128)(2,1)}, bf16[16,32,256]{2,1,0:T(8,128)(2,1)}, u32[]{:S(2)}, u32[]{:S(2)}) collective-permute-start(bf16[16,32,256]{2,1,0:T(8,128)(2,1)} %get-tuple-element.233), channel_id=1, source_target_pairs={{0,33},{1,32},{2,35},{3,34},{4,37},{5,36},{6,39},{7,38},{8,41},{9,... | collective-permute-start | bytes 786440 | tf_op jit(solution)/shard_map/ppermute | solution.py:346
  199.6 2.0 collective-permute-start.26
  201.5 1.8 collective-permute-start.27
  205.6 3.7 %shard_map.220 = bf16[128,32,256]{2,1,0:T(8,128)(2,1)} custom-call(s32[64]{0:T(128)} %add.302.place_ref, s32[64]{0:T(128)} %compare_select_fusion.12.arrive_ref, bf16[64,8,128]{2,1,0:T(8,128)(2,1)} %copy-done.12, bf16[16,32,256]{2,1,0:T(8,128)(2,1)} %get-tuple-element.204.refs_0_, bf16[16,32,256]{2,1,0:T(8,128)(2,1)} %copy-done.16, ...), custom_call_target="tpu_custom_call" | custom-call | bytes 4194304 | tf_op jit(solution)/shard_map/pallas_call | solution.py:480
  209.4 3.1 %collective-permute-done.26.refs_4_ = bf16[16,32,256]{2,1,0:T(8,128)(2,1)} collective-permute-done((bf16[16,32,256]{2,1,0:T(8,128)(2,1)}, bf16[16,32,256]{2,1,0:T(8,128)(2,1)}, u32[]{:S(2)}, u32[]{:S(2)}) %collective-permute-start.26) | collective-permute-done | bytes 262176 | tf_op jit(solution)/shard_map/ppermute | solution.py:346
  212.5 6.5 %collective-permute-done.27.refs_6_ = bf16[16,32,256]{2,1,0:T(8,128)(2,1)} collective-permute-done((bf16[16,32,256]{2,1,0:T(8,128)(2,1)}, bf16[16,32,256]{2,1,0:T(8,128)(2,1)}, u32[]{:S(2)}, u32[]{:S(2)}) %collective-permute-start.27) | collective-permute-done | bytes 262176 | tf_op jit(solution)/shard_map/ppermute | solution.py:346
  219.0 3.7 %shard_map.222 = bf16[128,32,256]{2,1,0:T(8,128)(2,1)} custom-call(s32[64]{0:T(128)} %add.314.place_ref, s32[64]{0:T(128)} %compare_select_fusion.12.arrive_ref, bf16[64,8,128]{2,1,0:T(8,128)(2,1)} %copy-done.12, bf16[16,32,256]{2,1,0:T(8,128)(2,1)} %get-tuple-element.237.refs_0_, bf16[16,32,256]{2,1,0:T(8,128)(2,1)} %copy-done.23, ...), custom_call_target="tpu_custom_call" | custom-call | bytes 4194304 | tf_op jit(solution)/shard_map/pallas_call | solution.py:480
  (152 shorter events, 29.3 us)
Async XLA Ops:
  0.7 51.1 %copy-start.1 = (bf16[64,32,256]{2,1,0:T(8,128)(2,1)S(1)}, bf16[64,32,256]{2,1,0:T(8,128)(2,1)}, u32[]{:S(2)}) copy-start(bf16[64,32,256]{2,1,0:T(8,128)(2,1)} %keys_ref.1) | copy-start | bytes 3145732
  0.7 51.1 %copy-start.2 = (bf16[64,32,256]{2,1,0:T(8,128)(2,1)S(1)}, bf16[64,32,256]{2,1,0:T(8,128)(2,1)}, u32[]{:S(2)}) copy-start(bf16[64,32,256]{2,1,0:T(8,128)(2,1)} %values_ref.1) | copy-start | bytes 3145732
  0.7 48.2 %copy-start.13 = (s32[64,512]{1,0:T(8,128)S(1)}, s32[64,512]{1,0:T(8,128)}, u32[]{:S(2)}) copy-start(s32[64,512]{1,0:T(8,128)} %param.23) | copy-start | bytes 393220
  4.5 24.2 %all-to-all-start = ((bf16[64,8,128]{2,1,0:T(8,128)(2,1)}), bf16[64,8,128]{2,1,0:T(8,128)(2,1)S(1)}, u32[]{:S(2)}, u32[]{:S(2)}) async-start(bf16[64,8,128]{2,1,0:T(8,128)(2,1)} %bitcast.12), calls=%async_computation | async-start | bytes 262144 | tf_op jit(solution)/shard_map/all_to_all | solution.py:40
  29.6 22.2 %all-to-all-start.1 = ((bf16[64,8,128]{2,1,0:T(8,128)(2,1)}), bf16[64,8,128]{2,1,0:T(8,128)(2,1)S(1)}, u32[]{:S(2)}, u32[]{:S(2)}) async-start(bf16[64,8,128]{2,1,0:T(8,128)(2,1)} %get-tuple-element.158), calls=%async_computation.1 | async-start | bytes 262144 | tf_op jit(solution)/shard_map/all_to_all | solution.py:40
  39.9 23.1 %collective-permute-start = (bf16[16,32,256]{2,1,0:T(8,128)(2,1)}, bf16[16,32,256]{2,1,0:T(8,128)(2,1)}, u32[]{:S(2)}, u32[]{:S(2)}) collective-permute-start(bf16[16,32,256]{2,1,0:T(8,128)(2,1)} %get-tuple-element.159), channel_id=1, source_target_pairs={{0,6},{1,7},{2,8},{3,9},{4,10},{5,11},{6,12},{7,13},{8,14},{9,15},... | collective-permute-start | bytes 786440 | tf_op jit(solution)/shard_map/ppermute | solution.py:346
  43.2 21.3 %collective-permute-start.1 = (bf16[16,32,256]{2,1,0:T(8,128)(2,1)}, bf16[16,32,256]{2,1,0:T(8,128)(2,1)}, u32[]{:S(2)}, u32[]{:S(2)}) collective-permute-start(bf16[16,32,256]{2,1,0:T(8,128)(2,1)} %get-tuple-element.160), channel_id=1, source_target_pairs={{0,10},{1,11},{2,12},{3,13},{4,14},{5,15},{6,0},{7,1},{8,2},{9,3},... | collective-permute-start | bytes 786440 | tf_op jit(solution)/shard_map/ppermute | solution.py:346
  44.5 21.7 %collective-permute-start.2 = (bf16[16,32,256]{2,1,0:T(8,128)(2,1)}, bf16[16,32,256]{2,1,0:T(8,128)(2,1)}, u32[]{:S(2)}, u32[]{:S(2)}) collective-permute-start(bf16[16,32,256]{2,1,0:T(8,128)(2,1)} %get-tuple-element.161), channel_id=1, source_target_pairs={{0,16},{1,17},{2,18},{3,19},{4,20},{5,21},{6,22},{7,23},{8,24},{9,... | collective-permute-start | bytes 786440 | tf_op jit(solution)/shard_map/ppermute | solution.py:346
  45.9 25.2 %collective-permute-start.3 = (bf16[16,32,256]{2,1,0:T(8,128)(2,1)}, bf16[16,32,256]{2,1,0:T(8,128)(2,1)}, u32[]{:S(2)}, u32[]{:S(2)}) collective-permute-start(bf16[16,32,256]{2,1,0:T(8,128)(2,1)} %get-tuple-element.162), channel_id=1, source_target_pairs={{0,48},{1,49},{2,50},{3,51},{4,52},{5,53},{6,54},{7,55},{8,56},{9,... | collective-permute-start | bytes 786440 | tf_op jit(solution)/shard_map/ppermute | solution.py:346
  47.3 26.1 %collective-permute-start.4 = (bf16[16,32,256]{2,1,0:T(8,128)(2,1)}, bf16[16,32,256]{2,1,0:T(8,128)(2,1)}, u32[]{:S(2)}, u32[]{:S(2)}) collective-permute-start(bf16[16,32,256]{2,1,0:T(8,128)(2,1)} %get-tuple-element.163), channel_id=1, source_target_pairs={{0,32},{1,33},{2,34},{3,35},{4,36},{5,37},{6,38},{7,39},{8,40},{9,... | collective-permute-start | bytes 786440 | tf_op jit(solution)/shard_map/ppermute | solution.py:346
  51.8 68.4 %copy-start.4 = (bf16[2560,160]{0,1:T(8,128)(2,1)S(1)}, bf16[2560,160]{0,1:T(8,128)(2,1)}, u32[]{:S(2)}) copy-start(bf16[2560,160]{0,1:T(8,128)(2,1)} %param.35) | copy-start | bytes 2457604
  53.8 50.6 %copy-start.38 = (s32[8]{0:T(128)S(1)}, s32[8]{0:T(128)}, u32[]{:S(2)}) copy-start(s32[8]{0:T(128)} %constant.261) | copy-start | bytes 100
  53.8 50.6 %copy-start.36 = (s32[8]{0:T(128)S(1)}, s32[8]{0:T(128)}, u32[]{:S(2)}) copy-start(s32[8]{0:T(128)} %constant.242) | copy-start | bytes 100
  54.5 20.4 %all-to-all-start.2 = ((bf16[64,8,128]{2,1,0:T(8,128)(2,1)}), bf16[64,8,128]{2,1,0:T(8,128)(2,1)S(1)}, u32[]{:S(2)}, u32[]{:S(2)}) async-start(bf16[64,8,128]{2,1,0:T(8,128)(2,1)} %bitcast.16), calls=%async_computation.2 | async-start | bytes 262144 | tf_op jit(solution)/shard_map/all_to_all | solution.py:40
  63.0 20.4 %collective-permute-start.5 = (bf16[16,32,256]{2,1,0:T(8,128)(2,1)}, bf16[16,32,256]{2,1,0:T(8,128)(2,1)S(1)}, u32[]{:S(2)}, u32[]{:S(2)}) collective-permute-start(bf16[16,32,256]{2,1,0:T(8,128)(2,1)} %get-tuple-element.166), channel_id=1, source_target_pairs={{0,2},{1,3},{2,4},{3,5},{4,6},{5,7},{6,8},{7,9},{8,10},{9,11},{10,... | collective-permute-start | bytes 786440 | tf_op jit(solution)/shard_map/ppermute | solution.py:346
  64.5 18.9 %collective-permute-start.6 = (bf16[16,32,256]{2,1,0:T(8,128)(2,1)}, bf16[16,32,256]{2,1,0:T(8,128)(2,1)S(1)}, u32[]{:S(2)}, u32[]{:S(2)}) collective-permute-start(bf16[16,32,256]{2,1,0:T(8,128)(2,1)} %get-tuple-element.167), channel_id=1, source_target_pairs={{0,14},{1,15},{2,0},{3,1},{4,2},{5,3},{6,4},{7,5},{8,6},{9,7},{10,... | collective-permute-start | bytes 786440 | tf_op jit(solution)/shard_map/ppermute | solution.py:346
  66.2 19.8 %collective-permute-start.7 = (bf16[16,32,256]{2,1,0:T(8,128)(2,1)}, bf16[16,32,256]{2,1,0:T(8,128)(2,1)S(1)}, u32[]{:S(2)}, u32[]{:S(2)}) collective-permute-start(bf16[16,32,256]{2,1,0:T(8,128)(2,1)} %get-tuple-element.168), channel_id=1, source_target_pairs={{0,8},{1,9},{2,10},{3,11},{4,12},{5,13},{6,14},{7,15},{8,0},{9,1},... | collective-permute-start | bytes 786440 | tf_op jit(solution)/shard_map/ppermute | solution.py:346
  71.1 14.9 %collective-permute-start.8 = (bf16[16,32,256]{2,1,0:T(8,128)(2,1)}, bf16[16,32,256]{2,1,0:T(8,128)(2,1)S(1)}, u32[]{:S(2)}, u32[]{:S(2)}) collective-permute-start(bf16[16,32,256]{2,1,0:T(8,128)(2,1)} %get-tuple-element.169), channel_id=1, source_target_pairs={{0,17},{1,16},{2,19},{3,18},{4,21},{5,20},{6,23},{7,22},{8,25},{9,... | collective-permute-start | bytes 786440 | tf_op jit(solution)/shard_map/ppermute | solution.py:346
  73.4 12.6 %collective-permute-start.9 = (bf16[16,32,256]{2,1,0:T(8,128)(2,1)}, bf16[16,32,256]{2,1,0:T(8,128)(2,1)S(1)}, u32[]{:S(2)}, u32[]{:S(2)}) collective-permute-start(bf16[16,32,256]{2,1,0:T(8,128)(2,1)} %get-tuple-element.170), channel_id=1, source_target_pairs={{0,49},{1,48},{2,51},{3,50},{4,53},{5,52},{6,55},{7,54},{8,57},{9,... | collective-permute-start | bytes 786440 | tf_op jit(solution)/shard_map/ppermute | solution.py:346
  78.2 8.9 %all-to-all-start.3 = ((f32[4,20,128]{2,1,0:T(8,128)}), f32[4,20,128]{2,1,0:T(8,128)S(1)}, u32[]{:S(2)}, u32[]{:S(2)}) async-start(f32[4,20,128]{2,1,0:T(8,128)} %shard_map.215), calls=%async_computation.3 | async-start | bytes 98304 | tf_op jit(solution)/shard_map/all_to_all | solution.py:405
  83.4 41.0 %copy-start.25 = (bf16[16,32,256]{2,1,0:T(8,128)(2,1)}, bf16[16,32,256]{2,1,0:T(8,128)(2,1)S(1)}, u32[]{:S(2)}) copy-start(bf16[16,32,256]{2,1,0:T(8,128)(2,1)S(1)} %collective-permute-done.5.refs_1_) | copy-start | bytes 786436
  83.4 41.0 %copy-start.26 = (bf16[16,32,256]{2,1,0:T(8,128)(2,1)}, bf16[16,32,256]{2,1,0:T(8,128)(2,1)S(1)}, u32[]{:S(2)}) copy-start(bf16[16,32,256]{2,1,0:T(8,128)(2,1)S(1)} %collective-permute-done.6.refs_7_) | copy-start | bytes 786436
  86.0 38.4 %copy-start.27 = (bf16[16,32,256]{2,1,0:T(8,128)(2,1)}, bf16[16,32,256]{2,1,0:T(8,128)(2,1)S(1)}, u32[]{:S(2)}) copy-start(bf16[16,32,256]{2,1,0:T(8,128)(2,1)S(1)} %collective-permute-done.7.refs_4_) | copy-start | bytes 786436
  88.0 24.0 %all-to-all-start.4 = ((bf16[64,20,128]{2,1,0:T(8,128)(2,1)}), bf16[64,20,128]{2,1,0:T(8,128)(2,1)S(1)}, u32[]{:S(2)}, u32[]{:S(2)}) async-start(bf16[64,20,128]{2,1,0:T(8,128)(2,1)} %get-tuple-element.172), calls=%async_computation.4 | async-start | bytes 786432 | tf_op jit(solution)/shard_map/all_to_all | solution.py:40
  96.9 21.0 %collective-permute-start.10 = (bf16[16,32,256]{2,1,0:T(8,128)(2,1)}, bf16[16,32,256]{2,1,0:T(8,128)(2,1)S(1)}, u32[]{:S(2)}, u32[]{:S(2)}) collective-permute-start(bf16[16,32,256]{2,1,0:T(8,128)(2,1)} %get-tuple-element.173), channel_id=1, source_target_pairs={{0,4},{1,5},{2,6},{3,7},{4,8},{5,9},{6,10},{7,11},{8,12},{9,13},{1... | collective-permute-start | bytes 786440 | tf_op jit(solution)/shard_map/ppermute | solution.py:346
  99.3 20.2 %collective-permute-start.11 = (bf16[16,32,256]{2,1,0:T(8,128)(2,1)}, bf16[16,32,256]{2,1,0:T(8,128)(2,1)S(1)}, u32[]{:S(2)}, u32[]{:S(2)}) collective-permute-start(bf16[16,32,256]{2,1,0:T(8,128)(2,1)} %get-tuple-element.174), channel_id=1, source_target_pairs={{0,12},{1,13},{2,14},{3,15},{4,0},{5,1},{6,2},{7,3},{8,4},{9,5},{1... | collective-permute-start | bytes 786440 | tf_op jit(solution)/shard_map/ppermute | solution.py:346
  100.6 18.9 %collective-permute-start.12 = (bf16[16,32,256]{2,1,0:T(8,128)(2,1)}, bf16[16,32,256]{2,1,0:T(8,128)(2,1)S(1)}, u32[]{:S(2)}, u32[]{:S(2)}) collective-permute-start(bf16[16,32,256]{2,1,0:T(8,128)(2,1)} %get-tuple-element.175), channel_id=1, source_target_pairs={{0,33},{1,32},{2,35},{3,34},{4,37},{5,36},{6,39},{7,38},{8,41},{9,... | collective-permute-start | bytes 786440 | tf_op jit(solution)/shard_map/ppermute | solution.py:346
  104.4 15.1 %collective-permute-start.13 = (bf16[16,32,256]{2,1,0:T(8,128)(2,1)}, bf16[16,32,256]{2,1,0:T(8,128)(2,1)}, u32[]{:S(2)}, u32[]{:S(2)}) collective-permute-start(bf16[16,32,256]{2,1,0:T(8,128)(2,1)} %get-tuple-element.176), channel_id=1, source_target_pairs={{0,1},{1,0},{2,3},{3,2},{4,5},{5,4},{6,7},{7,6},{8,9},{9,8},{10,11... | collective-permute-start | bytes 786440 | tf_op jit(solution)/shard_map/ppermute | solution.py:346
  124.4 25.6 %all-to-all-start.5 = ((bf16[64,20,128]{2,1,0:T(8,128)(2,1)}), bf16[64,20,128]{2,1,0:T(8,128)(2,1)S(1)}, u32[]{:S(2)}, u32[]{:S(2)}) async-start(bf16[64,20,128]{2,1,0:T(8,128)(2,1)} %reshape.496), calls=%async_computation.5 | async-start | bytes 786432 | tf_op jit(solution)/shard_map/all_to_all | solution.py:40
  138.4 18.8 %collective-permute-start.21 = (bf16[16,32,256]{2,1,0:T(8,128)(2,1)}, bf16[16,32,256]{2,1,0:T(8,128)(2,1)S(1)}, u32[]{:S(2)}, u32[]{:S(2)}) collective-permute-start(bf16[16,32,256]{2,1,0:T(8,128)(2,1)} %get-tuple-element.229), channel_id=1, source_target_pairs={{0,1},{1,0},{2,3},{3,2},{4,5},{5,4},{6,7},{7,6},{8,9},{9,8},{10,11... | collective-permute-start | bytes 786440 | tf_op jit(solution)/shard_map/ppermute | solution.py:346
  138.9 20.7 %collective-permute-start.22 = (bf16[16,32,256]{2,1,0:T(8,128)(2,1)}, bf16[16,32,256]{2,1,0:T(8,128)(2,1)S(1)}, u32[]{:S(2)}, u32[]{:S(2)}) collective-permute-start(bf16[16,32,256]{2,1,0:T(8,128)(2,1)} %get-tuple-element.230), channel_id=1, source_target_pairs={{0,16},{1,17},{2,18},{3,19},{4,20},{5,21},{6,22},{7,23},{8,24},{9,... | collective-permute-start | bytes 786440 | tf_op jit(solution)/shard_map/ppermute | solution.py:346
  140.2 22.0 %collective-permute-start.14 = (bf16[16,32,256]{2,1,0:T(8,128)(2,1)}, bf16[16,32,256]{2,1,0:T(8,128)(2,1)S(1)}, u32[]{:S(2)}, u32[]{:S(2)}) collective-permute-start(bf16[16,32,256]{2,1,0:T(8,128)(2,1)} %get-tuple-element.205), channel_id=1, source_target_pairs={{0,6},{1,7},{2,8},{3,9},{4,10},{5,11},{6,12},{7,13},{8,14},{9,15},... | collective-permute-start | bytes 786440 | tf_op jit(solution)/shard_map/ppermute | solution.py:346
  143.2 19.5 %collective-permute-start.15 = (bf16[16,32,256]{2,1,0:T(8,128)(2,1)}, bf16[16,32,256]{2,1,0:T(8,128)(2,1)S(1)}, u32[]{:S(2)}, u32[]{:S(2)}) collective-permute-start(bf16[16,32,256]{2,1,0:T(8,128)(2,1)} %get-tuple-element.206), channel_id=1, source_target_pairs={{0,10},{1,11},{2,12},{3,13},{4,14},{5,15},{6,0},{7,1},{8,2},{9,3},... | collective-permute-start | bytes 786440 | tf_op jit(solution)/shard_map/ppermute | solution.py:346
  144.8 28.5 %collective-permute-start.16 = (bf16[16,32,256]{2,1,0:T(8,128)(2,1)}, bf16[16,32,256]{2,1,0:T(8,128)(2,1)S(1)}, u32[]{:S(2)}, u32[]{:S(2)}) collective-permute-start(bf16[16,32,256]{2,1,0:T(8,128)(2,1)} %get-tuple-element.207), channel_id=1, source_target_pairs={{0,8},{1,9},{2,10},{3,11},{4,12},{5,13},{6,14},{7,15},{8,0},{9,1},... | collective-permute-start | bytes 786440 | tf_op jit(solution)/shard_map/ppermute | solution.py:346
  150.9 71.8 %all-to-all-start.6 = ((bf16[64,20,128]{2,1,0:T(8,128)(2,1)}), bf16[64,20,128]{2,1,0:T(8,128)(2,1)S(1)}, u32[]{:S(2)}, u32[]{:S(2)}) async-start(bf16[64,20,128]{2,1,0:T(8,128)(2,1)} %shard_map.218), calls=%async_computation.6 | async-start | bytes 786432 | tf_op jit(solution)/shard_map/all_to_all | solution.py:40
  157.2 61.8 %copy-start.14 = (bf16[16,32,256]{2,1,0:T(8,128)(2,1)}, bf16[16,32,256]{2,1,0:T(8,128)(2,1)S(1)}, u32[]{:S(2)}) copy-start(bf16[16,32,256]{2,1,0:T(8,128)(2,1)S(1)} %collective-permute-done.21.refs_7_) | copy-start | bytes 786436
  157.2 34.0 %collective-permute-start.17 = (bf16[16,32,256]{2,1,0:T(8,128)(2,1)S(1)}, bf16[16,32,256]{2,1,0:T(8,128)(2,1)S(1)}, u32[]{:S(2)}, u32[]{:S(2)}) collective-permute-start(bf16[16,32,256]{2,1,0:T(8,128)(2,1)S(1)} %copy-done.37), channel_id=1, source_target_pairs={{0,4},{1,5},{2,6},{3,7},{4,8},{5,9},{6,10},{7,11},{8,12},{9,13},{1... | collective-permute-start | bytes 786440 | tf_op jit(solution)/shard_map/ppermute | solution.py:346
  159.6 59.4 %copy-start.15 = (bf16[16,32,256]{2,1,0:T(8,128)(2,1)}, bf16[16,32,256]{2,1,0:T(8,128)(2,1)S(1)}, u32[]{:S(2)}) copy-start(bf16[16,32,256]{2,1,0:T(8,128)(2,1)S(1)} %collective-permute-done.22.refs_3_) | copy-start | bytes 786436
  159.6 36.2 %collective-permute-start.18 = (bf16[16,32,256]{2,1,0:T(8,128)(2,1)}, bf16[16,32,256]{2,1,0:T(8,128)(2,1)S(1)}, u32[]{:S(2)}, u32[]{:S(2)}) collective-permute-start(bf16[16,32,256]{2,1,0:T(8,128)(2,1)} %get-tuple-element.209), channel_id=1, source_target_pairs={{0,12},{1,13},{2,14},{3,15},{4,0},{5,1},{6,2},{7,3},{8,4},{9,5},{1... | collective-permute-start | bytes 786440 | tf_op jit(solution)/shard_map/ppermute | solution.py:346
  162.3 43.3 %copy-start.16 = (bf16[16,32,256]{2,1,0:T(8,128)(2,1)}, bf16[16,32,256]{2,1,0:T(8,128)(2,1)S(1)}, u32[]{:S(2)}) copy-start(bf16[16,32,256]{2,1,0:T(8,128)(2,1)S(1)} %collective-permute-done.14.refs_1_) | copy-start | bytes 786436
  162.3 37.3 %collective-permute-start.19 = (bf16[16,32,256]{2,1,0:T(8,128)(2,1)}, bf16[16,32,256]{2,1,0:T(8,128)(2,1)S(1)}, u32[]{:S(2)}, u32[]{:S(2)}) collective-permute-start(bf16[16,32,256]{2,1,0:T(8,128)(2,1)} %get-tuple-element.210), channel_id=1, source_target_pairs={{0,2},{1,3},{2,4},{3,5},{4,6},{5,7},{6,8},{7,9},{8,10},{9,11},{10,... | collective-permute-start | bytes 786440 | tf_op jit(solution)/shard_map/ppermute | solution.py:346
  162.7 42.8 %copy-start.17 = (bf16[16,32,256]{2,1,0:T(8,128)(2,1)}, bf16[16,32,256]{2,1,0:T(8,128)(2,1)S(1)}, u32[]{:S(2)}) copy-start(bf16[16,32,256]{2,1,0:T(8,128)(2,1)S(1)} %collective-permute-done.15.refs_2_) | copy-start | bytes 786436
  162.7 38.8 %collective-permute-start.20 = (bf16[16,32,256]{2,1,0:T(8,128)(2,1)}, bf16[16,32,256]{2,1,0:T(8,128)(2,1)S(1)}, u32[]{:S(2)}, u32[]{:S(2)}) collective-permute-start(bf16[16,32,256]{2,1,0:T(8,128)(2,1)} %get-tuple-element.211), channel_id=1, source_target_pairs={{0,14},{1,15},{2,0},{3,1},{4,2},{5,3},{6,4},{7,5},{8,6},{9,7},{10,... | collective-permute-start | bytes 786440 | tf_op jit(solution)/shard_map/ppermute | solution.py:346
  173.3 36.1 %collective-permute-start.23 = (bf16[16,32,256]{2,1,0:T(8,128)(2,1)}, bf16[16,32,256]{2,1,0:T(8,128)(2,1)S(1)}, u32[]{:S(2)}, u32[]{:S(2)}) collective-permute-start(bf16[16,32,256]{2,1,0:T(8,128)(2,1)} %get-tuple-element.231), channel_id=1, source_target_pairs={{0,17},{1,16},{2,19},{3,18},{4,21},{5,20},{6,23},{7,22},{8,25},{9,... | collective-permute-start | bytes 786440 | tf_op jit(solution)/shard_map/ppermute | solution.py:346
  191.2 18.2 %collective-permute-start.24 = (bf16[16,32,256]{2,1,0:T(8,128)(2,1)}, bf16[16,32,256]{2,1,0:T(8,128)(2,1)S(1)}, u32[]{:S(2)}, u32[]{:S(2)}) collective-permute-start(bf16[16,32,256]{2,1,0:T(8,128)(2,1)} %get-tuple-element.232), channel_id=1, source_target_pairs={{0,32},{1,33},{2,34},{3,35},{4,36},{5,37},{6,38},{7,39},{8,40},{9,... | collective-permute-start | bytes 786440 | tf_op jit(solution)/shard_map/ppermute | solution.py:346
  195.8 13.6 %collective-permute-start.25 = (bf16[16,32,256]{2,1,0:T(8,128)(2,1)}, bf16[16,32,256]{2,1,0:T(8,128)(2,1)}, u32[]{:S(2)}, u32[]{:S(2)}) collective-permute-start(bf16[16,32,256]{2,1,0:T(8,128)(2,1)} %get-tuple-element.233), channel_id=1, source_target_pairs={{0,33},{1,32},{2,35},{3,34},{4,37},{5,36},{6,39},{7,38},{8,41},{9,... | collective-permute-start | bytes 786440 | tf_op jit(solution)/shard_map/ppermute | solution.py:346
  199.6 12.9 %collective-permute-start.26 = (bf16[16,32,256]{2,1,0:T(8,128)(2,1)}, bf16[16,32,256]{2,1,0:T(8,128)(2,1)}, u32[]{:S(2)}, u32[]{:S(2)}) collective-permute-start(bf16[16,32,256]{2,1,0:T(8,128)(2,1)} %get-tuple-element.234), channel_id=1, source_target_pairs={{0,48},{1,49},{2,50},{3,51},{4,52},{5,53},{6,54},{7,55},{8,56},{9,... | collective-permute-start | bytes 786440 | tf_op jit(solution)/shard_map/ppermute | solution.py:346
  201.5 17.4 %collective-permute-start.27 = (bf16[16,32,256]{2,1,0:T(8,128)(2,1)}, bf16[16,32,256]{2,1,0:T(8,128)(2,1)}, u32[]{:S(2)}, u32[]{:S(2)}) collective-permute-start(bf16[16,32,256]{2,1,0:T(8,128)(2,1)} %get-tuple-element.235), channel_id=1, source_target_pairs={{0,49},{1,48},{2,51},{3,50},{4,53},{5,52},{6,55},{7,54},{8,57},{9,... | collective-permute-start | bytes 786440 | tf_op jit(solution)/shard_map/ppermute | solution.py:346
  (26 other events, 433.1 us)
